TPU v7x, 256 devices: a whole 4x4x8 slice. The times are simulated.
256 devices in a mesh: tm: 16 (over x, y), space: 16 (over z, core).
Axes of the slice: x: 4, y: 4, z: 8, core: 2. Of those that a mesh axis runs over, the one named last changes fastest.
Arguments:
- initial: float32 [3, 64, 16, 128], P(None, 'space'), may hold values from -4 to 4
- guesses: float32 [64, 3, 64, 16, 128], P('tm', None, 'space'), may hold values from -4 to 4
- viscosity: float32 [64, 16, 128], P('space'), may hold values from 0.5 to 1
- forcing: float32 [3, 64, 16, 128], P(None, 'space'), may hold values from -6 to 6, as said below
Outputs:
- solution: float32 [256, 3, 64, 16, 128], P('tm', None, 'space')
Inputs may be any that keep to these rules, and one draw needn't show every extreme that they name: `forcing`: a body force for each cell and component.
All inputs are finite; a program needn't handle non-finite values.
Results may differ from a plain program's by a relative error of at most 0.00002.
Values sent between devices are 32-bit elements; how exact they have to be, the bound alone decides.
No kernel may reach another device: no remote copies, remote signals or barrier semaphores. Data moves between devices by JAX's collectives and lax.ppermute only.
A program may use at most 64 MiB of HBM per device.

v0:
```python
import functools

import jax
import jax.numpy as jnp
from jax import lax
from jax.experimental import pallas as pl
from jax.experimental.pallas import tpu as pltpu
from jax.sharding import PartitionSpec as P


time_step = 0.019
FINE, MIDDLE, COARSE = time_step, 2.0 * time_step, 8.0 * time_step
DEPTH = 4
AXES = ("tm", "space")


INITIAL, FORCING = 9, 12


def slab(low, own, high, base=0):
    def get(c, z):
        if z < 0:
            return low[base + c, z + DEPTH]
        if z >= DEPTH:
            return high[base + c, z - DEPTH]
        return own[base + c, z]

    return get


def reader(ref, shift=DEPTH):
    return lambda c, z: ref[c, z + shift]


def writer(ref, shift=DEPTH):
    def put(c, z, value):
        ref[c, z + shift] = value

    return put


def advance(get, put, first, last, table, step_size):
    for z in range(first, last):
        alpha = table[0, z + DEPTH]
        keep = table[1, z + DEPTH]
        center = [get(c, z) for c in range(3)]
        half = [value * (0.5 * step_size) for value in center]
        east, west = alpha - half[0], alpha + half[0]
        north, south = alpha - half[1], alpha + half[1]
        up, down = alpha - half[2], alpha + half[2]
        for c in range(3):
            value = center[c]
            along_x = east * pltpu.roll(value, 127, 1) + west * pltpu.roll(value, 1, 1)
            along_y = north * pltpu.roll(value, 15, 0) + south * pltpu.roll(value, 1, 0)
            along_z = up * get(c, z + 1) + down * get(c, z - 1)
            put(c, z, (keep * value + table[2 + c, z + DEPTH]) + along_x + (along_y + along_z))


def tables_kernel(low, own, high, fine, middle, coarse, first_low, first, first_high, kept):
    for source, target in ((low, first_low), (own, first), (high, first_high), (own, kept)):
        for c in range(3):
            for z in range(DEPTH):
                target[c, z] = source[INITIAL + c, z]
    get = slab(low, own, high, FORCING)
    for table, step_size in ((fine, FINE), (middle, MIDDLE), (coarse, COARSE)):
        for z in range(-DEPTH, 2 * DEPTH):
            alpha = get(3, z) * step_size
            table[0, z + DEPTH] = alpha
            table[1, z + DEPTH] = 1.0 - 6.0 * alpha
            for c in range(3):
                table[2 + c, z + DEPTH] = get(c, z) * step_size


def defects_kernel(low, own, high, fine, middle, out, one, two):
    def body(i, carry):
        start = slab(low, own, high, 3 * i)
        advance(start, writer(one), -3, 7, fine, FINE)
        advance(reader(one), writer(two), -2, 6, fine, FINE)
        advance(reader(two), writer(one), -1, 5, fine, FINE)

        def store(c, z, value):
            out[i, c, z] = value

        def subtract(c, z, value):
            out[i, c, z] = out[i, c, z] - value

        advance(reader(one), store, 0, 4, fine, FINE)
        advance(start, writer(two), -1, 5, middle, MIDDLE)
        advance(reader(two), subtract, 0, 4, middle, MIDDLE)
        return carry

    lax.fori_loop(0, 3, body, 0)


def opening_kernel(low, own, high, fine, defects, to_up, to_down, one, two):
    advance(slab(low, own, high), writer(one), -3, 7, fine, FINE)
    advance(reader(one), writer(two), -2, 6, fine, FINE)
    advance(reader(two), writer(one), -1, 5, fine, FINE)

    def store(c, z, value):
        to_up[c, z] = value
        to_down[c, z] = value

    advance(reader(one), store, 0, 4, fine, FINE)
    for c in range(3):
        for z in range(2):
            to_up[c, 4 + z] = defects[0, c, 2 + z]
            to_down[c, 4 + z] = defects[0, c, z]


def remainder_kernel(low, own, high, middle, coarse, defects, first, defect, rest, one):
    start = slab(low, own, high)
    advance(start, writer(one), -1, 5, middle, MIDDLE)

    def subtract(c, z, value):
        defect[c, z] = first[c, z] - value

    advance(reader(one), subtract, 0, 4, middle, MIDDLE)
    advance(start, writer(one), -1, 5, coarse, COARSE)

    def subtract_rest(c, z, value):
        rest[c, z] = defects[2, c, z] - value

    advance(reader(one), subtract_rest, 0, 4, coarse, COARSE)


def second_kernel(low, own, high, middle, defects, defect, rest, to_up, to_down, one, two):
    def added(c, z, value):
        if z < 0:
            term = low[c, 4 + 2 + z]
        elif z >= DEPTH:
            term = high[c, 4 + z - DEPTH]
        else:
            term = defects[0, c, z]
        two[c, z + DEPTH] = value + term

    def third(c, z, value):
        value = value + defects[1, c, z]
        to_up[c, z] = value
        to_down[c, z] = value

    advance(slab(low, own, high), writer(one), -3, 7, middle, MIDDLE)
    advance(reader(one), added, -2, 6, middle, MIDDLE)
    advance(reader(two), writer(one), -1, 5, middle, MIDDLE)
    advance(reader(one), third, 0, 4, middle, MIDDLE)
    for c in range(3):
        for z in range(2):
            to_up[c, 4 + z] = rest[c, 2 + z]
            to_down[c, 4 + z] = rest[c, z]
            to_up[c, 6 + z] = defect[c, 2 + z]
            to_down[c, 6 + z] = defect[c, z]


def coarse_defect_kernel(low, own, high, middle, rest, out, middle_out, one):
    def added(c, z, value):
        if z < 0:
            term = low[c, 4 + 2 + z]
        elif z >= DEPTH:
            term = high[c, 4 + z - DEPTH]
        else:
            term = rest[c, z]
        out[c, z + 2] = value + term
        if 0 <= z < DEPTH:
            middle_out[c, z] = value + term

    advance(slab(low, own, high), writer(one), -3, 7, middle, MIDDLE)
    advance(reader(one), added, -2, 6, middle, MIDDLE)


def take(kept, arrived, shift):
    for c in range(3):
        for z in range(DEPTH):
            kept[c, z] = arrived[c, z + shift]


def march_kernel(
    done, low, own, high, coarse, term_one, term_two, term, kept_in,
    state, message_one, message_two, kept, one, two,
):
    def first(c, z, value):
        value = value + term_one[c, z + 2]
        two[c, z + DEPTH] = value
        message_one[c, z + 2] = value

    def second(c, z, value):
        value = value + term_two[c, z]
        state[c, z] = value
        message_two[c, z] = value

    column = lax.axis_index("tm")
    marching = column == lax.axis_size("tm") - 1

    @pl.when(marching)
    def _():
        advance(slab(low, own, high), writer(one), -3, 7, coarse, COARSE)
        advance(reader(one), first, -2, 6, coarse, COARSE)
        advance(reader(two), writer(one), -1, 5, coarse, COARSE)
        advance(reader(one), second, 0, 4, coarse, COARSE)

    @pl.when(jnp.logical_not(marching))
    def _():
        for c in range(3):
            for z in range(2 * DEPTH):
                message_one[c, z] = term[c, z]
            for z in range(DEPTH):
                message_two[c, z] = term[c, z + 2]
                state[c, z] = own[c, z]

    if done[0] is not None:
        pl.when(column == done[0])(functools.partial(take, kept, term_one, 2))
    if done[1] is not None:
        pl.when(column == done[1])(functools.partial(take, kept, term_two, 0))


def last_march_kernel(done, low, own, high, coarse, term_one, kept, *rest):
    arrivals, (start, one) = rest[:-2], rest[-2:]
    column = lax.axis_index("tm")
    marching = column == lax.axis_size("tm") - 1

    def first(c, z, value):
        start[c, z] = value + term_one[c, z + 2]

    @pl.when(marching)
    def _():
        advance(slab(low, own, high), writer(one), -1, 5, coarse, COARSE)
        advance(reader(one), first, 0, 4, coarse, COARSE)

    pl.when(jnp.logical_not(marching))(functools.partial(take, start, kept, 0))
    for t, arrived in zip(done, (term_one,) + arrivals):
        if t is not None:
            pl.when(column == t)(functools.partial(take, start, arrived, 2 if t % 2 else 0))


def stations_kernel(low, own, high, middle, defect_low, defect, defect_high, defects, out, one, two):
    def first(c, z, value):
        if z < 0:
            term = defect_low[c, 6 + 2 + z]
        elif z >= DEPTH:
            term = defect_high[c, 6 + z - DEPTH]
        else:
            term = defect[c, z]
        value = value + term
        two[c, z + DEPTH] = value
        if 0 <= z < DEPTH:
            out[c, z] = value

    def second(c, z, value):
        out[3 + c, z] = value + defects[0, c, z]

    advance(slab(low, own, high), writer(one), -3, 7, middle, MIDDLE)
    advance(reader(one), first, -2, 6, middle, MIDDLE)
    advance(reader(two), writer(one), -1, 5, middle, MIDDLE)
    advance(reader(one), second, 0, 4, middle, MIDDLE)


def third_kernel(low, own, high, middle, defects, out, one):
    def third(c, z, value):
        out[c, z] = value + defects[1, c, z]

    advance(slab(low, own, high, 3), writer(one), -1, 5, middle, MIDDLE)
    advance(reader(one), third, 0, 4, middle, MIDDLE)


def fine_rows(start, fine, rows, at, one, two):
    def first(c, z, value):
        one[c, z + DEPTH] = value
        if 0 <= z < DEPTH:
            rows[at, c, z] = value

    def second(c, z, value):
        two[c, z + DEPTH] = value
        if 0 <= z < DEPTH:
            rows[at + 1, c, z] = value

    def third(c, z, value):
        rows[at + 2, c, z] = value

    advance(start, first, -2, 6, fine, FINE)
    advance(reader(one), second, -1, 5, fine, FINE)
    advance(reader(two), third, 0, 4, fine, FINE)


def send_rows(rows, result, sem, places):
    copies = [
        pltpu.make_async_copy(rows.at[at], result.at[place], sem.at[at])
        for at, place in enumerate(places)
    ]
    for copy in copies:
        copy.start()
    for copy in copies:
        copy.wait()


def first_rows_kernel(low, own, high, fine, coarse, term, stations, result, rows, one, two, sem):
    start = slab(low, own, high)
    fine_rows(start, fine, rows, 0, one, two)
    for c in range(3):
        for z in range(DEPTH):
            rows[3, c, z] = stations[c, z]
            rows[4, c, z] = stations[3 + c, z]

    def end(c, z, value):
        rows[5, c, z] = value + term[c, z + 2]

    advance(start, writer(one), -1, 5, coarse, COARSE)
    advance(reader(one), end, 0, 4, coarse, COARSE)
    send_rows(rows, result, sem, (0, 1, 2, 3, 7, 15))


def middle_rows_kernel(low, own, high, fine, station, before, result, rows, one, two, sem):
    for i in range(2):
        fine_rows(slab(low, own, high, 3 * i), fine, rows, 3 * i, one, two)
    for c in range(3):
        for z in range(DEPTH):
            rows[6, c, z] = station[c, z]
    send_rows(rows, result, sem, (4, 5, 6, 8, 9, 10, 11))


def last_rows_kernel(low, own, high, fine, before, result, rows, one, two, sem):
    fine_rows(slab(low, own, high), fine, rows, 0, one, two)
    send_rows(rows, result, sem, (12, 13, 14))


def permute(x, moves):
    spaces = lax.axis_size("space")
    times = lax.axis_size("tm")
    pairs = []
    for t in range(times):
        if t in moves:
            target, by = moves[t]
            pairs += [(t * spaces + s, target * spaces + (s + by) % spaces) for s in range(spaces)]
        else:
            pairs += [(t * spaces + s, t * spaces + (s ^ 1)) for s in range(spaces)]
    return lax.ppermute(x, AXES, pairs)


def halos(to_up, to_down, columns):
    return (
        permute(to_up, {t: (t, 1) for t in columns}),
        permute(to_down, {t: (t, -1) for t in columns}),
    )


def cycle(x, *columns):
    return permute(x, {t: (after, 0) for t, after in zip(columns, columns[1:] + columns[:1])})


PLANE = (16, 128)
WORK = pltpu.VMEM((3, 3 * DEPTH) + PLANE, jnp.float32)
VMEM_SPEC = pl.BlockSpec(memory_space=pltpu.VMEM)


def call(kernel, shapes, inputs, works, units, aliases=None):
    outs = [jax.ShapeDtypeStruct(tuple(shape) + PLANE, jnp.float32) for shape in shapes]
    result = pl.pallas_call(
        kernel,
        out_shape=outs,
        in_specs=[VMEM_SPEC] * len(inputs),
        out_specs=[VMEM_SPEC] * len(outs),
        scratch_shapes=[WORK] * works,
        input_output_aliases=aliases or {},
        compiler_params=pltpu.CompilerParams(vmem_limit_bytes=8 << 20),
        cost_estimate=pl.CostEstimate(flops=units * 120000, bytes_accessed=units * 60000, transcendentals=0),
    )(*inputs)
    return result[0] if len(outs) == 1 else result


def emit(kernel, inputs, count, before, units):
    specs = [VMEM_SPEC] * len(inputs)
    if before is not None:
        inputs = list(inputs) + [before]
        specs.append(pl.BlockSpec(memory_space=pl.ANY))
    return pl.pallas_call(
        kernel,
        out_shape=jax.ShapeDtypeStruct((16, 3, DEPTH) + PLANE, jnp.float32),
        in_specs=specs,
        out_specs=pl.BlockSpec(memory_space=pl.ANY),
        scratch_shapes=[pltpu.VMEM((count, 3, DEPTH) + PLANE, jnp.float32), WORK, WORK, pltpu.SemaphoreType.DMA((count,))],
        input_output_aliases={} if before is None else {len(inputs) - 1: 0},
        compiler_params=pltpu.CompilerParams(vmem_limit_bytes=8 << 20),
        cost_estimate=pl.CostEstimate(flops=units * 120000, bytes_accessed=units * 60000, transcendentals=0),
    )(*inputs)


def pack(initial, guesses, viscosity, forcing):
    last, guesses = lax.optimization_barrier((guesses[3], guesses))
    members = guesses[:3].reshape((9,) + guesses.shape[2:])
    return last, jnp.concatenate([members, initial, forcing, viscosity[None]], axis=0)


def on_device(initial, guesses, viscosity, forcing):
    times = lax.axis_size("tm")
    column = lax.axis_index("tm")
    every = range(times)
    marcher = times - 1
    alone = (marcher,)

    last, bulk = pack(initial, guesses, viscosity, forcing)
    incoming = permute(last, {t: ((t + 1) % times, 0) for t in every})
    bulk_low, bulk_high = halos(bulk, bulk, every)
    opening = jnp.where(column == 0, bulk[INITIAL : INITIAL + 3], incoming)
    open_low, open_high = halos(opening, opening, every)

    table = (5, 3 * DEPTH)
    fine, middle, coarse, first_low, first, first_high, kept = call(
        tables_kernel, [table] * 3 + [(3, DEPTH)] * 4, [bulk_low, bulk, bulk_high], 0, 10
    )
    defects = call(defects_kernel, [(3, 3, DEPTH)], [bulk_low, bulk, bulk_high, fine, middle], 2, 114)
    to_up, to_down = call(opening_kernel, [(3, 6)] * 2, [open_low, opening, open_high, fine, defects], 2, 28)
    low, high = halos(to_up, to_down, every)
    defect, rest = call(
        remainder_kernel, [(3, DEPTH)] * 2, [open_low, opening, open_high, middle, coarse, defects, to_up], 1, 20
    )
    second_up, second_down = call(second_kernel, [(3, 8)] * 2, [low, to_up, high, middle, defects, defect, rest], 2, 28)
    defect_low, defect_high = halos(second_up, second_down, every)
    term, term_middle = call(
        coarse_defect_kernel, [(3, 8), (3, DEPTH)], [defect_low, second_up, defect_high, middle, rest], 1, 18
    )

    terms = {marcher: term}
    ahead = (term, term_middle)
    for t in range(min(6, marcher)):
        terms[t] = cycle(ahead[t % 2], t, marcher)
        if t % 2:
            ahead = lax.optimization_barrier((term, term_middle, terms[t - 1], terms[t]))
            ahead, (terms[t - 1], terms[t]) = ahead[:2], ahead[2:]
    state, low, high = first, first_low, first_high
    brought, extra = {}, {}
    messages = None
    for period in range(times // 2):
        if period:
            low, high = halos(state, state, alone)
            for i in range(2):
                t = 2 * period + 4 + i
                done = 2 * period - 1 + i
                if t < marcher:
                    terms[t] = cycle(messages[i], t, marcher, done)
                    brought[t] = done
                else:
                    extra[done] = cycle(messages[i], marcher, done)
        if 2 * period + 2 < times:
            pair = (2 * period, 2 * period + 1)
            state, *messages, kept = call(
                functools.partial(march_kernel, [brought.get(t) for t in pair]),
                [(3, DEPTH), (3, 8), (3, DEPTH), (3, DEPTH)],
                [low, state, high, coarse, terms[pair[0]], terms[pair[1]], term, kept],
                2,
                28,
                {7: 3},
            )
        else:
            start = call(
                functools.partial(last_march_kernel, [brought.get(2 * period)] + list(extra)),
                [(3, DEPTH)],
                [low, state, high, coarse, terms[2 * period], kept] + list(extra.values()),
                1,
                10,
            )

    low, high = halos(start, start, every)
    stations = call(
        stations_kernel, [(6, DEPTH)], [low, start, high, middle, defect_low, defect, defect_high, defects], 2, 28
    )
    station_low, station_high = halos(stations, stations, every)
    result = emit(first_rows_kernel, [low, start, high, fine, coarse, term, stations], 6, None, 28)
    third = call(third_kernel, [(3, DEPTH)], [station_low, stations, station_high, middle, defects], 1, 10)
    third_low, third_high = halos(third, third, every)
    result = emit(middle_rows_kernel, [station_low, stations, station_high, fine, third], 7, result, 36)
    return emit(last_rows_kernel, [third_low, third, third_high, fine], 3, result, 18)


def solution(mesh):
    return jax.shard_map(
        on_device,
        mesh=mesh,
        in_specs=(
            P(None, "space", None, None),
            P("tm", None, "space", None, None),
            P("space", None, None),
            P(None, "space", None, None),
        ),
        out_specs=P("tm", None, "space", None, None),
        check_vma=False,
    )
```

profile of v0, /device:TPU:31, one launch (start us, length us, event | category | flops | bytes accessed | tf_op | source)
XLA Modules:
  0.0 122.1 jit_solution(7549278836445543793)
XLA Ops:
  2.9 2.2 %collective-permute-start = (f32[16,4,16,128]{3,2,1,0:T(8,128)S(1)}, f32[16,4,16,128]{3,2,1,0:T(8,128)S(1)}, u32[]{:S(2)}, u32[]{:S(2)}) collective-permute-start(f32[16,4,16,128]{3,2,1,0:T(8,128)S(1)} %pad_maximum_fusion.own), channel_id=1, source_target_pairs={{0,1},{1,2},{2,3},{3,4},{4,5},{5,6},{6,7},{7,8},{8,9},{9,10},{10,1... | collective-permute-start | bytes 1572872 | tf_op jit(solution)/shard_map/ppermute | solution.py:334
  5.2 3.4 %collective-permute-done.2 = f32[3,4,16,128]{3,2,1,0:T(8,128)S(1)} collective-permute-done((f32[3,4,16,128]{3,2,1,0:T(8,128)S(1)}, f32[3,4,16,128]{3,2,1,0:T(8,128)S(1)}, u32[]{:S(2)}, u32[]{:S(2)}) %collective-permute-start.2) | collective-permute-done | bytes 98336 | tf_op jit(solution)/shard_map/ppermute | solution.py:334
  8.6 3.3 %collective-permute-start.3 = (f32[3,4,16,128]{3,2,1,0:T(8,128)S(1)}, f32[3,4,16,128]{3,2,1,0:T(8,128)S(1)}, u32[]{:S(2)}, u32[]{:S(2)}) collective-permute-start(f32[3,4,16,128]{3,2,1,0:T(8,128)S(1)} %broadcast_select_fusion.own), channel_id=1, source_target_pairs={{0,1},{1,2},{2,3},{3,4},{4,5},{5,6},{6,7},{7,8},{8,9},{9,10},{10,1... | collective-permute-start | bytes 294920 | tf_op jit(solution)/shard_map/ppermute | solution.py:334
  14.2 2.1 %shard_map.47.defects = f32[3,3,4,16,128]{4,3,2,1,0:T(8,128)S(1)} custom-call(f32[16,4,16,128]{3,2,1,0:T(8,128)S(1)} %collective-permute-done.low, f32[16,4,16,128]{3,2,1,0:T(8,128)S(1)} %pad_maximum_fusion.own, f32[16,4,16,128]{3,2,1,0:T(8,128)S(1)} %collective-permute-done.1.high, f32[5,12,16,128]{3,2,1,0:T(8,128)S(1)} %get-tuple-element.66.fine, ...), custom_call_target="tpu_custom_call" | custom-call | flops 13680000 | bytes 6840000 | tf_op jit(solution)/shard_map/pallas_call | solution.py:355
  16.8 2.6 %collective-permute-start.6 = (f32[3,6,16,128]{3,2,1,0:T(8,128)S(1)}, f32[3,6,16,128]{3,2,1,0:T(8,128)S(1)}, u32[]{:S(2)}, u32[]{:S(2)}) collective-permute-start(f32[3,6,16,128]{3,2,1,0:T(8,128)S(1)} %get-tuple-element.69), channel_id=1, source_target_pairs={{0,15},{1,0},{2,1},{3,2},{4,3},{5,4},{6,5},{7,6},{8,7},{9,8},{10,9... | collective-permute-start | bytes 442376 | tf_op jit(solution)/shard_map/ppermute | solution.py:334
  22.2 3.5 %collective-permute-start.8 = (f32[3,8,16,128]{3,2,1,0:T(8,128)S(1)}, f32[3,8,16,128]{3,2,1,0:T(8,128)S(1)}, u32[]{:S(2)}, u32[]{:S(2)}) collective-permute-start(f32[3,8,16,128]{3,2,1,0:T(8,128)S(1)} %get-tuple-element.73), channel_id=1, source_target_pairs={{0,15},{1,0},{2,1},{3,2},{4,3},{5,4},{6,5},{7,6},{8,7},{9,8},{10,9... | collective-permute-start | bytes 589832 | tf_op jit(solution)/shard_map/ppermute | solution.py:334
  27.9 2.9 %collective-permute-start.9 = (f32[3,8,16,128]{3,2,1,0:T(8,128)S(1)}, f32[3,8,16,128]{3,2,1,0:T(8,128)S(1)}, u32[]{:S(2)}, u32[]{:S(2)}) collective-permute-start(f32[3,8,16,128]{3,2,1,0:T(8,128)S(1)} %get-tuple-element.86.term), channel_id=1, source_target_pairs={{0,240},{1,241},{2,242},{3,243},{4,244},{5,245},{6,246},{7,247},{8... | collective-permute-start | bytes 589832 | tf_op jit(solution)/shard_map/ppermute | solution.py:334
  30.9 2.5 %collective-permute-start.10 = (f32[3,4,16,128]{3,2,1,0:T(8,128)S(1)}, f32[3,4,16,128]{3,2,1,0:T(8,128)S(1)}, u32[]{:S(2)}, u32[]{:S(2)}) collective-permute-start(f32[3,4,16,128]{3,2,1,0:T(8,128)S(1)} %get-tuple-element.87), channel_id=1, source_target_pairs={{0,1},{1,0},{2,3},{3,2},{4,5},{5,4},{6,7},{7,6},{8,9},{9,8},{10,11... | collective-permute-start | bytes 294920 | tf_op jit(solution)/shard_map/ppermute | solution.py:334
  33.3 4.6 %collective-permute-done.10.term_two = f32[3,4,16,128]{3,2,1,0:T(8,128)S(1)} collective-permute-done((f32[3,4,16,128]{3,2,1,0:T(8,128)S(1)}, f32[3,4,16,128]{3,2,1,0:T(8,128)S(1)}, u32[]{:S(2)}, u32[]{:S(2)}) %collective-permute-start.10) | collective-permute-done | bytes 98336 | tf_op jit(solution)/shard_map/ppermute | solution.py:334
  39.9 5.0 %collective-permute-start.12 = (f32[3,4,16,128]{3,2,1,0:T(8,128)S(1)}, f32[3,4,16,128]{3,2,1,0:T(8,128)S(1)}, u32[]{:S(2)}, u32[]{:S(2)}) collective-permute-start(f32[3,4,16,128]{3,2,1,0:T(8,128)S(1)} %get-tuple-element.79.own), channel_id=1, source_target_pairs={{0,1},{1,0},{2,3},{3,2},{4,5},{5,4},{6,7},{7,6},{8,9},{9,8},{10,11... | collective-permute-start | bytes 294920 | tf_op jit(solution)/shard_map/ppermute | solution.py:334
  47.7 5.0 %collective-permute-start.16 = (f32[3,4,16,128]{3,2,1,0:T(8,128)S(1)}, f32[3,4,16,128]{3,2,1,0:T(8,128)S(1)}, u32[]{:S(2)}, u32[]{:S(2)}) collective-permute-start(f32[3,4,16,128]{3,2,1,0:T(8,128)S(1)} %get-tuple-element.85.own), channel_id=1, source_target_pairs={{0,1},{1,0},{2,3},{3,2},{4,5},{5,4},{6,7},{7,6},{8,9},{9,8},{10,11... | collective-permute-start | bytes 294920 | tf_op jit(solution)/shard_map/ppermute | solution.py:334
  54.6 3.4 %collective-permute-start.19 = (f32[3,4,16,128]{3,2,1,0:T(8,128)S(1)}, f32[3,4,16,128]{3,2,1,0:T(8,128)S(1)}, u32[]{:S(2)}, u32[]{:S(2)}) collective-permute-start(f32[3,4,16,128]{3,2,1,0:T(8,128)S(1)} %get-tuple-element.91.own), channel_id=1, source_target_pairs={{0,1},{1,0},{2,3},{3,2},{4,5},{5,4},{6,7},{7,6},{8,9},{9,8},{10,11... | collective-permute-start | bytes 294920 | tf_op jit(solution)/shard_map/ppermute | solution.py:334
  58.0 5.0 %collective-permute-start.20 = (f32[3,4,16,128]{3,2,1,0:T(8,128)S(1)}, f32[3,4,16,128]{3,2,1,0:T(8,128)S(1)}, u32[]{:S(2)}, u32[]{:S(2)}) collective-permute-start(f32[3,4,16,128]{3,2,1,0:T(8,128)S(1)} %get-tuple-element.91.own), channel_id=1, source_target_pairs={{0,1},{1,0},{2,3},{3,2},{4,5},{5,4},{6,7},{7,6},{8,9},{9,8},{10,11... | collective-permute-start | bytes 294920 | tf_op jit(solution)/shard_map/ppermute | solution.py:334
  64.5 5.3 %collective-permute-start.23 = (f32[3,4,16,128]{3,2,1,0:T(8,128)S(1)}, f32[3,4,16,128]{3,2,1,0:T(8,128)S(1)}, u32[]{:S(2)}, u32[]{:S(2)}) collective-permute-start(f32[3,4,16,128]{3,2,1,0:T(8,128)S(1)} %get-tuple-element.95.own), channel_id=1, source_target_pairs={{0,1},{1,0},{2,3},{3,2},{4,5},{5,4},{6,7},{7,6},{8,9},{9,8},{10,11... | collective-permute-start | bytes 294920 | tf_op jit(solution)/shard_map/ppermute | solution.py:334
  71.4 3.9 %collective-permute-done.24.high = f32[3,4,16,128]{3,2,1,0:T(8,128)S(1)} collective-permute-done((f32[3,4,16,128]{3,2,1,0:T(8,128)S(1)}, f32[3,4,16,128]{3,2,1,0:T(8,128)S(1)}, u32[]{:S(2)}, u32[]{:S(2)}) %collective-permute-start.24) | collective-permute-done | bytes 98336 | tf_op jit(solution)/shard_map/ppermute | solution.py:334
  77.6 3.5 %collective-permute-done.28.high = f32[3,4,16,128]{3,2,1,0:T(8,128)S(1)} collective-permute-done((f32[3,4,16,128]{3,2,1,0:T(8,128)S(1)}, f32[3,4,16,128]{3,2,1,0:T(8,128)S(1)}, u32[]{:S(2)}, u32[]{:S(2)}) %collective-permute-start.28) | collective-permute-done | bytes 98336 | tf_op jit(solution)/shard_map/ppermute | solution.py:334
  81.7 2.4 %collective-permute-start.31 = (f32[3,4,16,128]{3,2,1,0:T(8,128)S(1)}, f32[3,4,16,128]{3,2,1,0:T(8,128)S(1)}, u32[]{:S(2)}, u32[]{:S(2)}) collective-permute-start(f32[3,4,16,128]{3,2,1,0:T(8,128)S(1)} %get-tuple-element.103.own), channel_id=1, source_target_pairs={{0,1},{1,0},{2,3},{3,2},{4,5},{5,4},{6,7},{7,6},{8,9},{9,8},{10,11... | collective-permute-start | bytes 294920 | tf_op jit(solution)/shard_map/ppermute | solution.py:334
  86.4 3.7 %collective-permute-done.32.high = f32[3,4,16,128]{3,2,1,0:T(8,128)S(1)} collective-permute-done((f32[3,4,16,128]{3,2,1,0:T(8,128)S(1)}, f32[3,4,16,128]{3,2,1,0:T(8,128)S(1)}, u32[]{:S(2)}, u32[]{:S(2)}) %collective-permute-start.32) | collective-permute-done | bytes 98336 | tf_op jit(solution)/shard_map/ppermute | solution.py:334
  90.8 4.2 %collective-permute-start.35 = (f32[3,4,16,128]{3,2,1,0:T(8,128)S(1)}, f32[3,4,16,128]{3,2,1,0:T(8,128)S(1)}, u32[]{:S(2)}, u32[]{:S(2)}) collective-permute-start(f32[3,4,16,128]{3,2,1,0:T(8,128)S(1)} %get-tuple-element.107.own), channel_id=1, source_target_pairs={{0,1},{1,0},{2,3},{3,2},{4,5},{5,4},{6,7},{7,6},{8,9},{9,8},{10,11... | collective-permute-start | bytes 294920 | tf_op jit(solution)/shard_map/ppermute | solution.py:334
  96.6 2.7 %collective-permute-done.36.high = f32[3,4,16,128]{3,2,1,0:T(8,128)S(1)} collective-permute-done((f32[3,4,16,128]{3,2,1,0:T(8,128)S(1)}, f32[3,4,16,128]{3,2,1,0:T(8,128)S(1)}, u32[]{:S(2)}, u32[]{:S(2)}) %collective-permute-start.36) | collective-permute-done | bytes 98336 | tf_op jit(solution)/shard_map/ppermute | solution.py:334
  99.6 2.9 %collective-permute-start.43 = (f32[3,4,16,128]{3,2,1,0:T(8,128)S(1)}, f32[3,4,16,128]{3,2,1,0:T(8,128)S(1)}, u32[]{:S(2)}, u32[]{:S(2)}) collective-permute-start(f32[3,4,16,128]{3,2,1,0:T(8,128)S(1)} %shard_map.59.own), channel_id=1, source_target_pairs={{0,1},{1,2},{2,3},{3,4},{4,5},{5,6},{6,7},{7,8},{8,9},{9,10},{10,1... | collective-permute-start | bytes 294920 | tf_op jit(solution)/shard_map/ppermute | solution.py:334
  104.1 4.2 %collective-permute-done.44.high = f32[3,4,16,128]{3,2,1,0:T(8,128)S(1)} collective-permute-done((f32[3,4,16,128]{3,2,1,0:T(8,128)S(1)}, f32[3,4,16,128]{3,2,1,0:T(8,128)S(1)}, u32[]{:S(2)}, u32[]{:S(2)}) %collective-permute-start.44) | collective-permute-done | bytes 98336 | tf_op jit(solution)/shard_map/ppermute | solution.py:334
  110.0 2.6 %collective-permute-done.45.low = f32[6,4,16,128]{3,2,1,0:T(8,128)S(1)} collective-permute-done((f32[6,4,16,128]{3,2,1,0:T(8,128)S(1)}, f32[6,4,16,128]{3,2,1,0:T(8,128)S(1)}, u32[]{:S(2)}, u32[]{:S(2)}) %collective-permute-start.45) | collective-permute-done | bytes 196640 | tf_op jit(solution)/shard_map/ppermute | solution.py:334
  112.6 4.0 %collective-permute-done.46.high = f32[6,4,16,128]{3,2,1,0:T(8,128)S(1)} collective-permute-done((f32[6,4,16,128]{3,2,1,0:T(8,128)S(1)}, f32[6,4,16,128]{3,2,1,0:T(8,128)S(1)}, u32[]{:S(2)}, u32[]{:S(2)}) %collective-permute-start.46) | collective-permute-done | bytes 196640 | tf_op jit(solution)/shard_map/ppermute | solution.py:334
  (99 shorter events, 36.9 us)
Async XLA Ops:
  2.9 10.7 %collective-permute-start = (f32[16,4,16,128]{3,2,1,0:T(8,128)S(1)}, f32[16,4,16,128]{3,2,1,0:T(8,128)S(1)}, u32[]{:S(2)}, u32[]{:S(2)}) collective-permute-start(f32[16,4,16,128]{3,2,1,0:T(8,128)S(1)} %pad_maximum_fusion.own), channel_id=1, source_target_pairs={{0,1},{1,2},{2,3},{3,4},{4,5},{5,6},{6,7},{7,8},{8,9},{9,10},{10,1... | collective-permute-start | bytes 1572872 | tf_op jit(solution)/shard_map/ppermute | solution.py:334
  5.1 8.9 %collective-permute-start.1 = (f32[16,4,16,128]{3,2,1,0:T(8,128)S(1)}, f32[16,4,16,128]{3,2,1,0:T(8,128)S(1)}, u32[]{:S(2)}, u32[]{:S(2)}) collective-permute-start(f32[16,4,16,128]{3,2,1,0:T(8,128)S(1)} %pad_maximum_fusion.own), channel_id=1, source_target_pairs={{0,15},{1,0},{2,1},{3,2},{4,3},{5,4},{6,5},{7,6},{8,7},{9,8},{10,9... | collective-permute-start | bytes 1572872 | tf_op jit(solution)/shard_map/ppermute | solution.py:334
  8.6 7.6 %collective-permute-start.3 = (f32[3,4,16,128]{3,2,1,0:T(8,128)S(1)}, f32[3,4,16,128]{3,2,1,0:T(8,128)S(1)}, u32[]{:S(2)}, u32[]{:S(2)}) collective-permute-start(f32[3,4,16,128]{3,2,1,0:T(8,128)S(1)} %broadcast_select_fusion.own), channel_id=1, source_target_pairs={{0,1},{1,2},{2,3},{3,4},{4,5},{5,6},{6,7},{7,8},{8,9},{9,10},{10,1... | collective-permute-start | bytes 294920 | tf_op jit(solution)/shard_map/ppermute | solution.py:334
  27.9 10.0 %collective-permute-start.9 = (f32[3,8,16,128]{3,2,1,0:T(8,128)S(1)}, f32[3,8,16,128]{3,2,1,0:T(8,128)S(1)}, u32[]{:S(2)}, u32[]{:S(2)}) collective-permute-start(f32[3,8,16,128]{3,2,1,0:T(8,128)S(1)} %get-tuple-element.86.term), channel_id=1, source_target_pairs={{0,240},{1,241},{2,242},{3,243},{4,244},{5,245},{6,246},{7,247},{8... | collective-permute-start | bytes 589832 | tf_op jit(solution)/shard_map/ppermute | solution.py:334
  30.9 7.1 %collective-permute-start.10 = (f32[3,4,16,128]{3,2,1,0:T(8,128)S(1)}, f32[3,4,16,128]{3,2,1,0:T(8,128)S(1)}, u32[]{:S(2)}, u32[]{:S(2)}) collective-permute-start(f32[3,4,16,128]{3,2,1,0:T(8,128)S(1)} %get-tuple-element.87), channel_id=1, source_target_pairs={{0,1},{1,0},{2,3},{3,2},{4,5},{5,4},{6,7},{7,6},{8,9},{9,8},{10,11... | collective-permute-start | bytes 294920 | tf_op jit(solution)/shard_map/ppermute | solution.py:334
  37.9 7.0 %collective-permute-start.13 = (f32[3,8,16,128]{3,2,1,0:T(8,128)S(1)}, f32[3,8,16,128]{3,2,1,0:T(8,128)S(1)}, u32[]{:S(2)}, u32[]{:S(2)}) collective-permute-start(f32[3,8,16,128]{3,2,1,0:T(8,128)S(1)} %get-tuple-element.86.term), channel_id=1, source_target_pairs={{0,1},{1,0},{2,3},{3,2},{4,5},{5,4},{6,7},{7,6},{8,9},{9,8},{10,11... | collective-permute-start | bytes 589832 | tf_op jit(solution)/shard_map/ppermute | solution.py:334
  37.9 6.9 %collective-permute-start.14 = (f32[3,4,16,128]{3,2,1,0:T(8,128)S(1)}, f32[3,4,16,128]{3,2,1,0:T(8,128)S(1)}, u32[]{:S(2)}, u32[]{:S(2)}) collective-permute-start(f32[3,4,16,128]{3,2,1,0:T(8,128)S(1)} %get-tuple-element.87), channel_id=1, source_target_pairs={{0,1},{1,0},{2,3},{3,2},{4,5},{5,4},{6,7},{7,6},{8,9},{9,8},{10,11... | collective-permute-start | bytes 294920 | tf_op jit(solution)/shard_map/ppermute | solution.py:334
  38.5 7.1 %collective-permute-start.11 = (f32[3,4,16,128]{3,2,1,0:T(8,128)S(1)}, f32[3,4,16,128]{3,2,1,0:T(8,128)S(1)}, u32[]{:S(2)}, u32[]{:S(2)}) collective-permute-start(f32[3,4,16,128]{3,2,1,0:T(8,128)S(1)} %get-tuple-element.79.own), channel_id=1, source_target_pairs={{0,1},{1,0},{2,3},{3,2},{4,5},{5,4},{6,7},{7,6},{8,9},{9,8},{10,11... | collective-permute-start | bytes 294920 | tf_op jit(solution)/shard_map/ppermute | solution.py:334
  44.9 9.2 %collective-permute-start.17 = (f32[3,8,16,128]{3,2,1,0:T(8,128)S(1)}, f32[3,8,16,128]{3,2,1,0:T(8,128)S(1)}, u32[]{:S(2)}, u32[]{:S(2)}) collective-permute-start(f32[3,8,16,128]{3,2,1,0:T(8,128)S(1)} %get-tuple-element.86.term), channel_id=1, source_target_pairs={{0,1},{1,0},{2,3},{3,2},{4,5},{5,4},{6,7},{7,6},{8,9},{9,8},{10,11... | collective-permute-start | bytes 589832 | tf_op jit(solution)/shard_map/ppermute | solution.py:334
  44.9 8.5 %collective-permute-start.18 = (f32[3,4,16,128]{3,2,1,0:T(8,128)S(1)}, f32[3,4,16,128]{3,2,1,0:T(8,128)S(1)}, u32[]{:S(2)}, u32[]{:S(2)}) collective-permute-start(f32[3,4,16,128]{3,2,1,0:T(8,128)S(1)} %get-tuple-element.87), channel_id=1, source_target_pairs={{0,1},{1,0},{2,3},{3,2},{4,5},{5,4},{6,7},{7,6},{8,9},{9,8},{10,11... | collective-permute-start | bytes 294920 | tf_op jit(solution)/shard_map/ppermute | solution.py:334
  47.0 7.1 %collective-permute-start.15 = (f32[3,4,16,128]{3,2,1,0:T(8,128)S(1)}, f32[3,4,16,128]{3,2,1,0:T(8,128)S(1)}, u32[]{:S(2)}, u32[]{:S(2)}) collective-permute-start(f32[3,4,16,128]{3,2,1,0:T(8,128)S(1)} %get-tuple-element.85.own), channel_id=1, source_target_pairs={{0,1},{1,0},{2,3},{3,2},{4,5},{5,4},{6,7},{7,6},{8,9},{9,8},{10,11... | collective-permute-start | bytes 294920 | tf_op jit(solution)/shard_map/ppermute | solution.py:334
  52.7 10.3 %collective-permute-start.21 = (f32[3,8,16,128]{3,2,1,0:T(8,128)S(1)}, f32[3,8,16,128]{3,2,1,0:T(8,128)S(1)}, u32[]{:S(2)}, u32[]{:S(2)}) collective-permute-start(f32[3,8,16,128]{3,2,1,0:T(8,128)S(1)} %get-tuple-element.92), channel_id=1, source_target_pairs={{0,1},{1,0},{2,3},{3,2},{4,5},{5,4},{6,7},{7,6},{8,9},{9,8},{10,11... | collective-permute-start | bytes 589832 | tf_op jit(solution)/shard_map/ppermute | solution.py:334
  53.4 9.6 %collective-permute-start.22 = (f32[3,4,16,128]{3,2,1,0:T(8,128)S(1)}, f32[3,4,16,128]{3,2,1,0:T(8,128)S(1)}, u32[]{:S(2)}, u32[]{:S(2)}) collective-permute-start(f32[3,4,16,128]{3,2,1,0:T(8,128)S(1)} %get-tuple-element.93), channel_id=1, source_target_pairs={{0,1},{1,0},{2,3},{3,2},{4,5},{5,4},{6,7},{7,6},{8,9},{9,8},{10,11... | collective-permute-start | bytes 294920 | tf_op jit(solution)/shard_map/ppermute | solution.py:334
  54.6 9.1 %collective-permute-start.19 = (f32[3,4,16,128]{3,2,1,0:T(8,128)S(1)}, f32[3,4,16,128]{3,2,1,0:T(8,128)S(1)}, u32[]{:S(2)}, u32[]{:S(2)}) collective-permute-start(f32[3,4,16,128]{3,2,1,0:T(8,128)S(1)} %get-tuple-element.91.own), channel_id=1, source_target_pairs={{0,1},{1,0},{2,3},{3,2},{4,5},{5,4},{6,7},{7,6},{8,9},{9,8},{10,11... | collective-permute-start | bytes 294920 | tf_op jit(solution)/shard_map/ppermute | solution.py:334
  63.0 7.7 %collective-permute-start.25 = (f32[3,8,16,128]{3,2,1,0:T(8,128)S(1)}, f32[3,8,16,128]{3,2,1,0:T(8,128)S(1)}, u32[]{:S(2)}, u32[]{:S(2)}) collective-permute-start(f32[3,8,16,128]{3,2,1,0:T(8,128)S(1)} %get-tuple-element.96), channel_id=1, source_target_pairs={{0,1},{1,0},{2,3},{3,2},{4,5},{5,4},{6,7},{7,6},{8,9},{9,8},{10,11... | collective-permute-start | bytes 589832 | tf_op jit(solution)/shard_map/ppermute | solution.py:334
  63.0 6.9 %collective-permute-start.26 = (f32[3,4,16,128]{3,2,1,0:T(8,128)S(1)}, f32[3,4,16,128]{3,2,1,0:T(8,128)S(1)}, u32[]{:S(2)}, u32[]{:S(2)}) collective-permute-start(f32[3,4,16,128]{3,2,1,0:T(8,128)S(1)} %get-tuple-element.97), channel_id=1, source_target_pairs={{0,1},{1,0},{2,3},{3,2},{4,5},{5,4},{6,7},{7,6},{8,9},{9,8},{10,11... | collective-permute-start | bytes 294920 | tf_op jit(solution)/shard_map/ppermute | solution.py:334
  64.5 7.0 %collective-permute-start.23 = (f32[3,4,16,128]{3,2,1,0:T(8,128)S(1)}, f32[3,4,16,128]{3,2,1,0:T(8,128)S(1)}, u32[]{:S(2)}, u32[]{:S(2)}) collective-permute-start(f32[3,4,16,128]{3,2,1,0:T(8,128)S(1)} %get-tuple-element.95.own), channel_id=1, source_target_pairs={{0,1},{1,0},{2,3},{3,2},{4,5},{5,4},{6,7},{7,6},{8,9},{9,8},{10,11... | collective-permute-start | bytes 294920 | tf_op jit(solution)/shard_map/ppermute | solution.py:334
  76.5 7.7 %collective-permute-start.33 = (f32[3,8,16,128]{3,2,1,0:T(8,128)S(1)}, f32[3,8,16,128]{3,2,1,0:T(8,128)S(1)}, u32[]{:S(2)}, u32[]{:S(2)}) collective-permute-start(f32[3,8,16,128]{3,2,1,0:T(8,128)S(1)} %get-tuple-element.104), channel_id=1, source_target_pairs={{0,1},{1,0},{2,3},{3,2},{4,5},{5,4},{6,7},{7,6},{8,9},{9,8},{10,11... | collective-permute-start | bytes 589832 | tf_op jit(solution)/shard_map/ppermute | solution.py:334
  76.5 7.5 %collective-permute-start.34 = (f32[3,4,16,128]{3,2,1,0:T(8,128)S(1)}, f32[3,4,16,128]{3,2,1,0:T(8,128)S(1)}, u32[]{:S(2)}, u32[]{:S(2)}) collective-permute-start(f32[3,4,16,128]{3,2,1,0:T(8,128)S(1)} %get-tuple-element.105), channel_id=1, source_target_pairs={{0,1},{1,0},{2,3},{3,2},{4,5},{5,4},{6,7},{7,6},{8,9},{9,8},{10,11... | collective-permute-start | bytes 294920 | tf_op jit(solution)/shard_map/ppermute | solution.py:334
  84.0 11.1 %collective-permute-start.37 = (f32[3,8,16,128]{3,2,1,0:T(8,128)S(1)}, f32[3,8,16,128]{3,2,1,0:T(8,128)S(1)}, u32[]{:S(2)}, u32[]{:S(2)}) collective-permute-start(f32[3,8,16,128]{3,2,1,0:T(8,128)S(1)} %get-tuple-element.108), channel_id=1, source_target_pairs={{0,1},{1,0},{2,3},{3,2},{4,5},{5,4},{6,7},{7,6},{8,9},{9,8},{10,11... | collective-permute-start | bytes 589832 | tf_op jit(solution)/shard_map/ppermute | solution.py:334
  84.0 6.8 %collective-permute-start.38 = (f32[3,4,16,128]{3,2,1,0:T(8,128)S(1)}, f32[3,4,16,128]{3,2,1,0:T(8,128)S(1)}, u32[]{:S(2)}, u32[]{:S(2)}) collective-permute-start(f32[3,4,16,128]{3,2,1,0:T(8,128)S(1)} %get-tuple-element.110), channel_id=1, source_target_pairs={{0,1},{1,0},{2,3},{3,2},{4,5},{5,4},{6,7},{7,6},{8,9},{9,8},{10,11... | collective-permute-start | bytes 294920 | tf_op jit(solution)/shard_map/ppermute | solution.py:334
  84.1 15.2 %collective-permute-start.39 = (f32[3,8,16,128]{3,2,1,0:T(8,128)S(1)}, f32[3,8,16,128]{3,2,1,0:T(8,128)S(1)}, u32[]{:S(2)}, u32[]{:S(2)}) collective-permute-start(f32[3,8,16,128]{3,2,1,0:T(8,128)S(1)} %get-tuple-element.111), channel_id=1, source_target_pairs={{0,1},{1,0},{2,3},{3,2},{4,5},{5,4},{6,7},{7,6},{8,9},{9,8},{10,11... | collective-permute-start | bytes 589832 | tf_op jit(solution)/shard_map/ppermute | solution.py:334
  85.7 9.3 %collective-permute-start.40 = (f32[3,4,16,128]{3,2,1,0:T(8,128)S(1)}, f32[3,4,16,128]{3,2,1,0:T(8,128)S(1)}, u32[]{:S(2)}, u32[]{:S(2)}) collective-permute-start(f32[3,4,16,128]{3,2,1,0:T(8,128)S(1)} %get-tuple-element.112), channel_id=1, source_target_pairs={{0,1},{1,0},{2,3},{3,2},{4,5},{5,4},{6,7},{7,6},{8,9},{9,8},{10,11... | collective-permute-start | bytes 294920 | tf_op jit(solution)/shard_map/ppermute | solution.py:334
  90.7 8.6 %collective-permute-start.41 = (f32[3,8,16,128]{3,2,1,0:T(8,128)S(1)}, f32[3,8,16,128]{3,2,1,0:T(8,128)S(1)}, u32[]{:S(2)}, u32[]{:S(2)}) collective-permute-start(f32[3,8,16,128]{3,2,1,0:T(8,128)S(1)} %get-tuple-element.113), channel_id=1, source_target_pairs={{0,1},{1,0},{2,3},{3,2},{4,5},{5,4},{6,7},{7,6},{8,9},{9,8},{10,11... | collective-permute-start | bytes 589832 | tf_op jit(solution)/shard_map/ppermute | solution.py:334
  (26 other events, 131.8 us)
where the time goes:
time: 122 us
  starting transfers between devices  57.7 us (47%)
  waiting for transfers between devices  48.4 us (40%)
  Pallas kernels  12.6 us (10%)
  local copies, waits for them, and re-layouts  1.92 us (2%)
    ppermute x49, starting transfers between devices, permute(): return lax.ppermute(x, AXES, pairs)  57.7 us
    ppermute x49, waiting for transfers between devices, permute(): return lax.ppermute(x, AXES, pairs)  48.4 us
    pallas_call x16, Pallas kernels, call(): pl.pallas_call(kernel, out_shape=outs, in_specs=[VMEM_SPEC] * len(inputs)...  8.62 us
    pallas_call x3, Pallas kernels, emit(): pl.pallas_call(kernel, out_shape=jax.ShapeDtypeStruct((16, 3, DEPTH) + PL...  4 us
  transfers between devices with their start and end apart: 49, of which 28 were waited for; matrix products, arithmetic and copies ran while one was open for 0% of the time, Pallas kernels for 8%

commit v1 on v0

--- a/solution.py
+++ b/solution.py
@@ -12,9 +12,6 @@
 FINE, MIDDLE, COARSE = time_step, 2.0 * time_step, 8.0 * time_step
 DEPTH = 4
 AXES = ("tm", "space")
-
-
-INITIAL, FORCING = 9, 12
 
 
 def slab(low, own, high, base=0):
@@ -56,12 +53,8 @@
             put(c, z, (keep * value + table[2 + c, z + DEPTH]) + along_x + (along_y + along_z))
 
 
-def tables_kernel(low, own, high, fine, middle, coarse, first_low, first, first_high, kept):
-    for source, target in ((low, first_low), (own, first), (high, first_high), (own, kept)):
-        for c in range(3):
-            for z in range(DEPTH):
-                target[c, z] = source[INITIAL + c, z]
-    get = slab(low, own, high, FORCING)
+def tables_kernel(low, own, high, fine, middle, coarse):
+    get = slab(low, own, high)
     for table, step_size in ((fine, FINE), (middle, MIDDLE), (coarse, COARSE)):
         for z in range(-DEPTH, 2 * DEPTH):
             alpha = get(3, z) * step_size
@@ -108,7 +101,9 @@
             to_down[c, 4 + z] = defects[0, c, z]
 
 
-def remainder_kernel(low, own, high, middle, coarse, defects, first, defect, rest, one):
+def remainder_kernel(
+    low, own, high, middle, coarse, defects, first, initial, defect, rest, late_up, late_down, kept, one
+):
     start = slab(low, own, high)
     advance(start, writer(one), -1, 5, middle, MIDDLE)
 
@@ -122,9 +117,17 @@
         rest[c, z] = defects[2, c, z] - value
 
     advance(reader(one), subtract_rest, 0, 4, coarse, COARSE)
-
-
-def second_kernel(low, own, high, middle, defects, defect, rest, to_up, to_down, one, two):
+    for c in range(3):
+        for z in range(DEPTH):
+            late_up[c, z] = initial[c, z]
+            late_down[c, z] = initial[c, z]
+            kept[c, z] = initial[c, z]
+        for z in range(2):
+            late_up[c, 4 + z] = defect[c, 2 + z]
+            late_down[c, 4 + z] = defect[c, z]
+
+
+def second_kernel(low, own, high, middle, defects, rest, to_up, to_down, one, two):
     def added(c, z, value):
         if z < 0:
             term = low[c, 4 + 2 + z]
@@ -147,8 +150,6 @@
         for z in range(2):
             to_up[c, 4 + z] = rest[c, 2 + z]
             to_down[c, 4 + z] = rest[c, z]
-            to_up[c, 6 + z] = defect[c, 2 + z]
-            to_down[c, 6 + z] = defect[c, z]
 
 
 def coarse_defect_kernel(low, own, high, middle, rest, out, middle_out, one):
@@ -167,7 +168,8 @@
     advance(reader(one), added, -2, 6, middle, MIDDLE)
 
 
-def take(kept, arrived, shift):
+def take(kept, arrived):
+    shift = (arrived.shape[1] - DEPTH) // 2
     for c in range(3):
         for z in range(DEPTH):
             kept[c, z] = arrived[c, z + shift]
@@ -180,13 +182,15 @@
     def first(c, z, value):
         value = value + term_one[c, z + 2]
         two[c, z + DEPTH] = value
-        message_one[c, z + 2] = value
+        if 0 <= z + edge < message_one.shape[1]:
+            message_one[c, z + edge] = value
 
     def second(c, z, value):
         value = value + term_two[c, z]
         state[c, z] = value
         message_two[c, z] = value
 
+    edge = (message_one.shape[1] - DEPTH) // 2
     column = lax.axis_index("tm")
     marching = column == lax.axis_size("tm") - 1
 
@@ -200,16 +204,16 @@
     @pl.when(jnp.logical_not(marching))
     def _():
         for c in range(3):
-            for z in range(2 * DEPTH):
-                message_one[c, z] = term[c, z]
+            for z in range(message_one.shape[1]):
+                message_one[c, z] = term[c, z + 2 - edge]
             for z in range(DEPTH):
                 message_two[c, z] = term[c, z + 2]
                 state[c, z] = own[c, z]
 
     if done[0] is not None:
-        pl.when(column == done[0])(functools.partial(take, kept, term_one, 2))
+        pl.when(column == done[0])(functools.partial(take, kept, term_one))
     if done[1] is not None:
-        pl.when(column == done[1])(functools.partial(take, kept, term_two, 0))
+        pl.when(column == done[1])(functools.partial(take, kept, term_two))
 
 
 def last_march_kernel(done, low, own, high, coarse, term_one, kept, *rest):
@@ -225,18 +229,18 @@
         advance(slab(low, own, high), writer(one), -1, 5, coarse, COARSE)
         advance(reader(one), first, 0, 4, coarse, COARSE)
 
-    pl.when(jnp.logical_not(marching))(functools.partial(take, start, kept, 0))
+    pl.when(jnp.logical_not(marching))(functools.partial(take, start, kept))
     for t, arrived in zip(done, (term_one,) + arrivals):
         if t is not None:
-            pl.when(column == t)(functools.partial(take, start, arrived, 2 if t % 2 else 0))
+            pl.when(column == t)(functools.partial(take, start, arrived))
 
 
 def stations_kernel(low, own, high, middle, defect_low, defect, defect_high, defects, out, one, two):
     def first(c, z, value):
         if z < 0:
-            term = defect_low[c, 6 + 2 + z]
+            term = defect_low[c, 4 + 2 + z]
         elif z >= DEPTH:
-            term = defect_high[c, 6 + z - DEPTH]
+            term = defect_high[c, 4 + z - DEPTH]
         else:
             term = defect[c, z]
         value = value + term
@@ -382,12 +386,6 @@
     )(*inputs)
 
 
-def pack(initial, guesses, viscosity, forcing):
-    last, guesses = lax.optimization_barrier((guesses[3], guesses))
-    members = guesses[:3].reshape((9,) + guesses.shape[2:])
-    return last, jnp.concatenate([members, initial, forcing, viscosity[None]], axis=0)
-
-
 def on_device(initial, guesses, viscosity, forcing):
     times = lax.axis_size("tm")
     column = lax.axis_index("tm")
@@ -395,44 +393,52 @@
     marcher = times - 1
     alone = (marcher,)
 
-    last, bulk = pack(initial, guesses, viscosity, forcing)
+    last, guesses = lax.optimization_barrier((guesses[3], guesses))
+    members = guesses[:3].reshape((9,) + guesses.shape[2:])
     incoming = permute(last, {t: ((t + 1) % times, 0) for t in every})
-    bulk_low, bulk_high = halos(bulk, bulk, every)
-    opening = jnp.where(column == 0, bulk[INITIAL : INITIAL + 3], incoming)
+    member_low, member_high = halos(members, members, every)
+    fields = jnp.concatenate([forcing, viscosity[None]], axis=0)
+    field_low, field_high = halos(fields, fields, every)
+    opening = jnp.where(column == 0, initial, incoming)
     open_low, open_high = halos(opening, opening, every)
 
     table = (5, 3 * DEPTH)
-    fine, middle, coarse, first_low, first, first_high, kept = call(
-        tables_kernel, [table] * 3 + [(3, DEPTH)] * 4, [bulk_low, bulk, bulk_high], 0, 10
-    )
-    defects = call(defects_kernel, [(3, 3, DEPTH)], [bulk_low, bulk, bulk_high, fine, middle], 2, 114)
+    fine, middle, coarse = call(tables_kernel, [table] * 3, [field_low, fields, field_high], 0, 10)
+    defects = call(defects_kernel, [(3, 3, DEPTH)], [member_low, members, member_high, fine, middle], 2, 114)
     to_up, to_down = call(opening_kernel, [(3, 6)] * 2, [open_low, opening, open_high, fine, defects], 2, 28)
     low, high = halos(to_up, to_down, every)
-    defect, rest = call(
-        remainder_kernel, [(3, DEPTH)] * 2, [open_low, opening, open_high, middle, coarse, defects, to_up], 1, 20
+    defect, rest, late_up, late_down, kept = call(
+        remainder_kernel,
+        [(3, DEPTH)] * 2 + [(3, 6)] * 2 + [(3, DEPTH)],
+        [open_low, opening, open_high, middle, coarse, defects, to_up, initial],
+        1,
+        20,
     )
-    second_up, second_down = call(second_kernel, [(3, 8)] * 2, [low, to_up, high, middle, defects, defect, rest], 2, 28)
-    defect_low, defect_high = halos(second_up, second_down, every)
+    second_up, second_down = call(second_kernel, [(3, 6)] * 2, [low, to_up, high, middle, defects, rest], 2, 28)
+    rest_low, rest_high = halos(second_up, second_down, every)
     term, term_middle = call(
-        coarse_defect_kernel, [(3, 8), (3, DEPTH)], [defect_low, second_up, defect_high, middle, rest], 1, 18
+        coarse_defect_kernel, [(3, 8), (3, DEPTH)], [rest_low, second_up, rest_high, middle, rest], 1, 18
     )
 
     terms = {marcher: term}
     ahead = (term, term_middle)
     for t in range(min(6, marcher)):
+        if t == 4:
+            ahead = lax.optimization_barrier((term, term_middle, terms[0], terms[1]))
+            ahead, (terms[0], terms[1]) = ahead[:2], ahead[2:]
         terms[t] = cycle(ahead[t % 2], t, marcher)
-        if t % 2:
-            ahead = lax.optimization_barrier((term, term_middle, terms[t - 1], terms[t]))
-            ahead, (terms[t - 1], terms[t]) = ahead[:2], ahead[2:]
-    state, low, high = first, first_low, first_high
+    late_low, late_high = halos(late_up, late_down, every)
+    state, low, high = late_up, late_low, late_high
     brought, extra = {}, {}
     messages = None
     for period in range(times // 2):
         if period:
             low, high = halos(state, state, alone)
             for i in range(2):
-                t = 2 * period + 4 + i
+                t = 2 * period + 6 + i
                 done = 2 * period - 1 + i
+                if period == 1 and t - 2 < marcher:
+                    terms[t - 2] = cycle(messages[i], t - 2, marcher)
                 if t < marcher:
                     terms[t] = cycle(messages[i], t, marcher, done)
                     brought[t] = done
@@ -442,7 +448,7 @@
             pair = (2 * period, 2 * period + 1)
             state, *messages, kept = call(
                 functools.partial(march_kernel, [brought.get(t) for t in pair]),
-                [(3, DEPTH), (3, 8), (3, DEPTH), (3, DEPTH)],
+                [(3, DEPTH), (3, 8 if 2 * period + 8 < marcher else DEPTH), (3, DEPTH), (3, DEPTH)],
                 [low, state, high, coarse, terms[pair[0]], terms[pair[1]], term, kept],
                 2,
                 28,
@@ -459,7 +465,7 @@
 
     low, high = halos(start, start, every)
     stations = call(
-        stations_kernel, [(6, DEPTH)], [low, start, high, middle, defect_low, defect, defect_high, defects], 2, 28
+        stations_kernel, [(6, DEPTH)], [low, start, high, middle, late_low, defect, late_high, defects], 2, 28
     )
     station_low, station_high = halos(stations, stations, every)
     result = emit(first_rows_kernel, [low, start, high, fine, coarse, term, stations], 6, None, 28)

time: 122 us -> 119 us (0.975)
  the two profiles are of different devices: /device:TPU:31 before, /device:TPU:30 now
where the time goes in v1:
time: 119 us
  starting transfers between devices  51.7 us (43%)
  waiting for transfers between devices  50.6 us (43%)
  Pallas kernels  12.8 us (11%)
  local copies, waits for them, and re-layouts  1.88 us (2%)
    ppermute x55, starting transfers between devices, permute(): return lax.ppermute(x, AXES, pairs)  51.7 us
    ppermute x55, waiting for transfers between devices, permute(): return lax.ppermute(x, AXES, pairs)  50.6 us
    pallas_call x16, Pallas kernels, call(): pl.pallas_call(kernel, out_shape=outs, in_specs=[VMEM_SPEC] * len(inputs)...  8.84 us
    pallas_call x3, Pallas kernels, emit(): pl.pallas_call(kernel, out_shape=jax.ShapeDtypeStruct((16, 3, DEPTH) + PL...  4 us
  transfers between devices with their start and end apart: 55, of which 20 were waited for; matrix products, arithmetic and copies ran while one was open for 2% of the time, Pallas kernels for 8%

profile of v1, /device:TPU:30, one launch (start us, length us, event | category | flops | bytes accessed | tf_op | source)
XLA Modules:
  0.0 118.5 jit_solution(3988571053427626134)
XLA Ops:
  3.7 3.5 %collective-permute-start.4 = (f32[4,4,16,128]{3,2,1,0:T(8,128)S(1)}, f32[4,4,16,128]{3,2,1,0:T(8,128)S(1)}, u32[]{:S(2)}, u32[]{:S(2)}) collective-permute-start(f32[4,4,16,128]{3,2,1,0:T(8,128)S(1)} %pad_maximum_fusion.own), channel_id=1, source_target_pairs={{0,15},{1,0},{2,1},{3,2},{4,3},{5,4},{6,5},{7,6},{8,7},{9,8},{10,9... | collective-permute-start | bytes 393224 | tf_op jit(solution)/shard_map/ppermute | solution.py:338
  8.2 2.9 %collective-permute-start.6 = (f32[9,4,16,128]{3,2,1,0:T(8,128)S(1)}, f32[9,4,16,128]{3,2,1,0:T(8,128)S(1)}, u32[]{:S(2)}, u32[]{:S(2)}) collective-permute-start(f32[9,4,16,128]{3,2,1,0:T(8,128)S(1)} %bitcast.5), channel_id=1, source_target_pairs={{0,15},{1,0},{2,1},{3,2},{4,3},{5,4},{6,5},{7,6},{8,7},{9,8},{10,9... | collective-permute-start | bytes 884744 | tf_op jit(solution)/shard_map/ppermute | solution.py:338
  11.2 2.9 %collective-permute-start.2 = (f32[3,4,16,128]{3,2,1,0:T(8,128)S(1)}, f32[3,4,16,128]{3,2,1,0:T(8,128)S(1)}, u32[]{:S(2)}, u32[]{:S(2)}) collective-permute-start(f32[3,4,16,128]{3,2,1,0:T(8,128)S(1)} %broadcast_select_fusion.own), channel_id=1, source_target_pairs={{0,15},{1,0},{2,1},{3,2},{4,3},{5,4},{6,5},{7,6},{8,7},{9,8},{10,9... | collective-permute-start | bytes 294920 | tf_op jit(solution)/shard_map/ppermute | solution.py:338
  18.2 3.0 %collective-permute-start.10 = (f32[3,6,16,128]{3,2,1,0:T(8,128)S(1)}, f32[3,6,16,128]{3,2,1,0:T(8,128)S(1)}, u32[]{:S(2)}, u32[]{:S(2)}) collective-permute-start(f32[3,6,16,128]{3,2,1,0:T(8,128)S(1)} %get-tuple-element.61), channel_id=1, source_target_pairs={{0,15},{1,0},{2,1},{3,2},{4,3},{5,4},{6,5},{7,6},{8,7},{9,8},{10,9... | collective-permute-start | bytes 442376 | tf_op jit(solution)/shard_map/ppermute | solution.py:338
  24.5 3.0 %collective-permute-start.12 = (f32[3,6,16,128]{3,2,1,0:T(8,128)S(1)}, f32[3,6,16,128]{3,2,1,0:T(8,128)S(1)}, u32[]{:S(2)}, u32[]{:S(2)}) collective-permute-start(f32[3,6,16,128]{3,2,1,0:T(8,128)S(1)} %get-tuple-element.64), channel_id=1, source_target_pairs={{0,15},{1,0},{2,1},{3,2},{4,3},{5,4},{6,5},{7,6},{8,7},{9,8},{10,9... | collective-permute-start | bytes 442376 | tf_op jit(solution)/shard_map/ppermute | solution.py:338
  27.5 2.8 %collective-permute-done.11.low = f32[3,6,16,128]{3,2,1,0:T(8,128)S(1)} collective-permute-done((f32[3,6,16,128]{3,2,1,0:T(8,128)S(1)}, f32[3,6,16,128]{3,2,1,0:T(8,128)S(1)}, u32[]{:S(2)}, u32[]{:S(2)}) %collective-permute-start.11) | collective-permute-done | bytes 147488 | tf_op jit(solution)/shard_map/ppermute | solution.py:338
  32.1 3.0 %collective-permute-start.8 = (f32[3,6,16,128]{3,2,1,0:T(8,128)S(1)}, f32[3,6,16,128]{3,2,1,0:T(8,128)S(1)}, u32[]{:S(2)}, u32[]{:S(2)}) collective-permute-start(f32[3,6,16,128]{3,2,1,0:T(8,128)S(1)} %get-tuple-element.60), channel_id=1, source_target_pairs={{0,15},{1,0},{2,1},{3,2},{4,3},{5,4},{6,5},{7,6},{8,7},{9,8},{10,9... | collective-permute-start | bytes 442376 | tf_op jit(solution)/shard_map/ppermute | solution.py:338
  36.2 7.1 %collective-permute-done.14.term_two = f32[3,4,16,128]{3,2,1,0:T(8,128)S(1)} collective-permute-done((f32[3,4,16,128]{3,2,1,0:T(8,128)S(1)}, f32[3,4,16,128]{3,2,1,0:T(8,128)S(1)}, u32[]{:S(2)}, u32[]{:S(2)}) %collective-permute-start.14) | collective-permute-done | bytes 98336 | tf_op jit(solution)/shard_map/ppermute | solution.py:338
  44.0 2.9 %collective-permute-start.16 = (f32[3,4,16,128]{3,2,1,0:T(8,128)S(1)}, f32[3,4,16,128]{3,2,1,0:T(8,128)S(1)}, u32[]{:S(2)}, u32[]{:S(2)}) collective-permute-start(f32[3,4,16,128]{3,2,1,0:T(8,128)S(1)} %get-tuple-element.70.own), channel_id=1, source_target_pairs={{0,1},{1,0},{2,3},{3,2},{4,5},{5,4},{6,7},{7,6},{8,9},{9,8},{10,11... | collective-permute-start | bytes 294920 | tf_op jit(solution)/shard_map/ppermute | solution.py:338
  49.9 3.0 %collective-permute-start.20 = (f32[3,4,16,128]{3,2,1,0:T(8,128)S(1)}, f32[3,4,16,128]{3,2,1,0:T(8,128)S(1)}, u32[]{:S(2)}, u32[]{:S(2)}) collective-permute-start(f32[3,4,16,128]{3,2,1,0:T(8,128)S(1)} %get-tuple-element.72.own), channel_id=1, source_target_pairs={{0,1},{1,0},{2,3},{3,2},{4,5},{5,4},{6,7},{7,6},{8,9},{9,8},{10,11... | collective-permute-start | bytes 294920 | tf_op jit(solution)/shard_map/ppermute | solution.py:338
  52.9 4.8 %collective-permute-done.22.term_two = f32[3,4,16,128]{3,2,1,0:T(8,128)S(1)} collective-permute-done((f32[3,4,16,128]{3,2,1,0:T(8,128)S(1)}, f32[3,4,16,128]{3,2,1,0:T(8,128)S(1)}, u32[]{:S(2)}, u32[]{:S(2)}) %collective-permute-start.22) | collective-permute-done | bytes 98336 | tf_op jit(solution)/shard_map/ppermute | solution.py:338
  58.5 2.9 %collective-permute-start.24 = (f32[3,4,16,128]{3,2,1,0:T(8,128)S(1)}, f32[3,4,16,128]{3,2,1,0:T(8,128)S(1)}, u32[]{:S(2)}, u32[]{:S(2)}) collective-permute-start(f32[3,4,16,128]{3,2,1,0:T(8,128)S(1)} %get-tuple-element.76.own), channel_id=1, source_target_pairs={{0,1},{1,0},{2,3},{3,2},{4,5},{5,4},{6,7},{7,6},{8,9},{9,8},{10,11... | collective-permute-start | bytes 294920 | tf_op jit(solution)/shard_map/ppermute | solution.py:338
  64.5 3.0 %collective-permute-start.28 = (f32[3,4,16,128]{3,2,1,0:T(8,128)S(1)}, f32[3,4,16,128]{3,2,1,0:T(8,128)S(1)}, u32[]{:S(2)}, u32[]{:S(2)}) collective-permute-start(f32[3,4,16,128]{3,2,1,0:T(8,128)S(1)} %get-tuple-element.80.own), channel_id=1, source_target_pairs={{0,1},{1,0},{2,3},{3,2},{4,5},{5,4},{6,7},{7,6},{8,9},{9,8},{10,11... | collective-permute-start | bytes 294920 | tf_op jit(solution)/shard_map/ppermute | solution.py:338
  67.4 3.4 %collective-permute-done.30.term_two = f32[3,4,16,128]{3,2,1,0:T(8,128)S(1)} collective-permute-done((f32[3,4,16,128]{3,2,1,0:T(8,128)S(1)}, f32[3,4,16,128]{3,2,1,0:T(8,128)S(1)}, u32[]{:S(2)}, u32[]{:S(2)}) %collective-permute-start.30) | collective-permute-done | bytes 98336 | tf_op jit(solution)/shard_map/ppermute | solution.py:338
  71.5 2.9 %collective-permute-start.32 = (f32[3,4,16,128]{3,2,1,0:T(8,128)S(1)}, f32[3,4,16,128]{3,2,1,0:T(8,128)S(1)}, u32[]{:S(2)}, u32[]{:S(2)}) collective-permute-start(f32[3,4,16,128]{3,2,1,0:T(8,128)S(1)} %get-tuple-element.82.own), channel_id=1, source_target_pairs={{0,1},{1,0},{2,3},{3,2},{4,5},{5,4},{6,7},{7,6},{8,9},{9,8},{10,11... | collective-permute-start | bytes 294920 | tf_op jit(solution)/shard_map/ppermute | solution.py:338
  78.0 2.7 %collective-permute-start.36 = (f32[3,4,16,128]{3,2,1,0:T(8,128)S(1)}, f32[3,4,16,128]{3,2,1,0:T(8,128)S(1)}, u32[]{:S(2)}, u32[]{:S(2)}) collective-permute-start(f32[3,4,16,128]{3,2,1,0:T(8,128)S(1)} %get-tuple-element.86.own), channel_id=1, source_target_pairs={{0,1},{1,0},{2,3},{3,2},{4,5},{5,4},{6,7},{7,6},{8,9},{9,8},{10,11... | collective-permute-start | bytes 294920 | tf_op jit(solution)/shard_map/ppermute | solution.py:338
  81.8 2.7 %collective-permute-done.37.term_one = f32[3,8,16,128]{3,2,1,0:T(8,128)S(1)} collective-permute-done((f32[3,8,16,128]{3,2,1,0:T(8,128)S(1)}, f32[3,8,16,128]{3,2,1,0:T(8,128)S(1)}, u32[]{:S(2)}, u32[]{:S(2)}) %collective-permute-start.37) | collective-permute-done | bytes 196640 | tf_op jit(solution)/shard_map/ppermute | solution.py:338
  85.2 4.4 %collective-permute-done.42.rest_0_ = f32[3,4,16,128]{3,2,1,0:T(8,128)S(1)} collective-permute-done((f32[3,4,16,128]{3,2,1,0:T(8,128)S(1)}, f32[3,4,16,128]{3,2,1,0:T(8,128)S(1)}, u32[]{:S(2)}, u32[]{:S(2)}) %collective-permute-start.42) | collective-permute-done | bytes 98336 | tf_op jit(solution)/shard_map/ppermute | solution.py:338
  92.7 2.7 %collective-permute-done.46.rest_4_ = f32[3,4,16,128]{3,2,1,0:T(8,128)S(1)} collective-permute-done((f32[3,4,16,128]{3,2,1,0:T(8,128)S(1)}, f32[3,4,16,128]{3,2,1,0:T(8,128)S(1)}, u32[]{:S(2)}, u32[]{:S(2)}) %collective-permute-start.46) | collective-permute-done | bytes 98336 | tf_op jit(solution)/shard_map/ppermute | solution.py:338
  95.4 3.3 %collective-permute-done.47.rest_5_ = f32[3,4,16,128]{3,2,1,0:T(8,128)S(1)} collective-permute-done((f32[3,4,16,128]{3,2,1,0:T(8,128)S(1)}, f32[3,4,16,128]{3,2,1,0:T(8,128)S(1)}, u32[]{:S(2)}, u32[]{:S(2)}) %collective-permute-start.47) | collective-permute-done | bytes 98336 | tf_op jit(solution)/shard_map/ppermute | solution.py:338
  99.0 2.9 %collective-permute-start.50 = (f32[3,4,16,128]{3,2,1,0:T(8,128)S(1)}, f32[3,4,16,128]{3,2,1,0:T(8,128)S(1)}, u32[]{:S(2)}, u32[]{:S(2)}) collective-permute-start(f32[3,4,16,128]{3,2,1,0:T(8,128)S(1)} %shard_map.59.own), channel_id=1, source_target_pairs={{0,15},{1,0},{2,1},{3,2},{4,3},{5,4},{6,5},{7,6},{8,7},{9,8},{10,9... | collective-permute-start | bytes 294920 | tf_op jit(solution)/shard_map/ppermute | solution.py:338
  104.9 2.8 %collective-permute-start.52 = (f32[6,4,16,128]{3,2,1,0:T(8,128)S(1)}, f32[6,4,16,128]{3,2,1,0:T(8,128)S(1)}, u32[]{:S(2)}, u32[]{:S(2)}) collective-permute-start(f32[6,4,16,128]{3,2,1,0:T(8,128)S(1)} %shard_map.60.own.stations), channel_id=1, source_target_pairs={{0,15},{1,0},{2,1},{3,2},{4,3},{5,4},{6,5},{7,6},{8,7},{9,8},{10,9... | collective-permute-start | bytes 589832 | tf_op jit(solution)/shard_map/ppermute | solution.py:338
  107.7 3.3 %collective-permute-done.51.low = f32[6,4,16,128]{3,2,1,0:T(8,128)S(1)} collective-permute-done((f32[6,4,16,128]{3,2,1,0:T(8,128)S(1)}, f32[6,4,16,128]{3,2,1,0:T(8,128)S(1)}, u32[]{:S(2)}, u32[]{:S(2)}) %collective-permute-start.51) | collective-permute-done | bytes 196640 | tf_op jit(solution)/shard_map/ppermute | solution.py:338
  111.3 3.0 %collective-permute-start.54 = (f32[3,4,16,128]{3,2,1,0:T(8,128)S(1)}, f32[3,4,16,128]{3,2,1,0:T(8,128)S(1)}, u32[]{:S(2)}, u32[]{:S(2)}) collective-permute-start(f32[3,4,16,128]{3,2,1,0:T(8,128)S(1)} %shard_map.61.station.own), channel_id=1, source_target_pairs={{0,15},{1,0},{2,1},{3,2},{4,3},{5,4},{6,5},{7,6},{8,7},{9,8},{10,9... | collective-permute-start | bytes 294920 | tf_op jit(solution)/shard_map/ppermute | solution.py:338
  (111 shorter events, 39.0 us)
Async XLA Ops:
  0.9 10.2 %collective-permute-start = (f32[3,4,16,128]{3,2,1,0:T(8,128)S(1)}, f32[3,4,16,128]{3,2,1,0:T(8,128)S(1)}, u32[]{:S(2)}, u32[]{:S(2)}) collective-permute-start(f32[3,4,16,128]{3,2,1,0:T(8,128)S(1)} %slice_bitcast_fusion), channel_id=1, source_target_pairs={{0,16},{1,17},{2,18},{3,19},{4,20},{5,21},{6,22},{7,23},{8,24},{9,... | collective-permute-start | bytes 294920 | tf_op jit(solution)/shard_map/ppermute | solution.py:338
  3.7 7.5 %collective-permute-start.3 = (f32[4,4,16,128]{3,2,1,0:T(8,128)S(1)}, f32[4,4,16,128]{3,2,1,0:T(8,128)S(1)}, u32[]{:S(2)}, u32[]{:S(2)}) collective-permute-start(f32[4,4,16,128]{3,2,1,0:T(8,128)S(1)} %pad_maximum_fusion.own), channel_id=1, source_target_pairs={{0,1},{1,2},{2,3},{3,4},{4,5},{5,6},{6,7},{7,8},{8,9},{9,10},{10,1... | collective-permute-start | bytes 393224 | tf_op jit(solution)/shard_map/ppermute | solution.py:338
  3.7 10.4 %collective-permute-start.4 = (f32[4,4,16,128]{3,2,1,0:T(8,128)S(1)}, f32[4,4,16,128]{3,2,1,0:T(8,128)S(1)}, u32[]{:S(2)}, u32[]{:S(2)}) collective-permute-start(f32[4,4,16,128]{3,2,1,0:T(8,128)S(1)} %pad_maximum_fusion.own), channel_id=1, source_target_pairs={{0,15},{1,0},{2,1},{3,2},{4,3},{5,4},{6,5},{7,6},{8,7},{9,8},{10,9... | collective-permute-start | bytes 393224 | tf_op jit(solution)/shard_map/ppermute | solution.py:338
  8.2 7.4 %collective-permute-start.5 = (f32[9,4,16,128]{3,2,1,0:T(8,128)S(1)}, f32[9,4,16,128]{3,2,1,0:T(8,128)S(1)}, u32[]{:S(2)}, u32[]{:S(2)}) collective-permute-start(f32[9,4,16,128]{3,2,1,0:T(8,128)S(1)} %bitcast.4), channel_id=1, source_target_pairs={{0,1},{1,2},{2,3},{3,4},{4,5},{5,6},{6,7},{7,8},{8,9},{9,10},{10,1... | collective-permute-start | bytes 884744 | tf_op jit(solution)/shard_map/ppermute | solution.py:338
  8.2 7.3 %collective-permute-start.6 = (f32[9,4,16,128]{3,2,1,0:T(8,128)S(1)}, f32[9,4,16,128]{3,2,1,0:T(8,128)S(1)}, u32[]{:S(2)}, u32[]{:S(2)}) collective-permute-start(f32[9,4,16,128]{3,2,1,0:T(8,128)S(1)} %bitcast.5), channel_id=1, source_target_pairs={{0,15},{1,0},{2,1},{3,2},{4,3},{5,4},{6,5},{7,6},{8,7},{9,8},{10,9... | collective-permute-start | bytes 884744 | tf_op jit(solution)/shard_map/ppermute | solution.py:338
  30.6 12.7 %collective-permute-start.13 = (f32[3,8,16,128]{3,2,1,0:T(8,128)S(1)}, f32[3,8,16,128]{3,2,1,0:T(8,128)S(1)}, u32[]{:S(2)}, u32[]{:S(2)}) collective-permute-start(f32[3,8,16,128]{3,2,1,0:T(8,128)S(1)} %get-tuple-element.73.term), channel_id=1, source_target_pairs={{0,240},{1,241},{2,242},{3,243},{4,244},{5,245},{6,246},{7,247},{8... | collective-permute-start | bytes 589832 | tf_op jit(solution)/shard_map/ppermute | solution.py:338
  32.1 11.2 %collective-permute-start.7 = (f32[3,6,16,128]{3,2,1,0:T(8,128)S(1)}, f32[3,6,16,128]{3,2,1,0:T(8,128)S(1)}, u32[]{:S(2)}, u32[]{:S(2)}) collective-permute-start(f32[3,6,16,128]{3,2,1,0:T(8,128)S(1)} %get-tuple-element.59.own), channel_id=1, source_target_pairs={{0,1},{1,2},{2,3},{3,4},{4,5},{5,6},{6,7},{7,8},{8,9},{9,10},{10,1... | collective-permute-start | bytes 442376 | tf_op jit(solution)/shard_map/ppermute | solution.py:338
  32.1 11.2 %collective-permute-start.8 = (f32[3,6,16,128]{3,2,1,0:T(8,128)S(1)}, f32[3,6,16,128]{3,2,1,0:T(8,128)S(1)}, u32[]{:S(2)}, u32[]{:S(2)}) collective-permute-start(f32[3,6,16,128]{3,2,1,0:T(8,128)S(1)} %get-tuple-element.60), channel_id=1, source_target_pairs={{0,15},{1,0},{2,1},{3,2},{4,3},{5,4},{6,5},{7,6},{8,7},{9,8},{10,9... | collective-permute-start | bytes 442376 | tf_op jit(solution)/shard_map/ppermute | solution.py:338
  35.1 8.2 %collective-permute-start.14 = (f32[3,4,16,128]{3,2,1,0:T(8,128)S(1)}, f32[3,4,16,128]{3,2,1,0:T(8,128)S(1)}, u32[]{:S(2)}, u32[]{:S(2)}) collective-permute-start(f32[3,4,16,128]{3,2,1,0:T(8,128)S(1)} %get-tuple-element.74), channel_id=1, source_target_pairs={{0,1},{1,0},{2,3},{3,2},{4,5},{5,4},{6,7},{7,6},{8,9},{9,8},{10,11... | collective-permute-start | bytes 294920 | tf_op jit(solution)/shard_map/ppermute | solution.py:338
  36.2 13.0 %collective-permute-start.17 = (f32[3,8,16,128]{3,2,1,0:T(8,128)S(1)}, f32[3,8,16,128]{3,2,1,0:T(8,128)S(1)}, u32[]{:S(2)}, u32[]{:S(2)}) collective-permute-start(f32[3,8,16,128]{3,2,1,0:T(8,128)S(1)} %get-tuple-element.73.term), channel_id=1, source_target_pairs={{0,1},{1,0},{2,3},{3,2},{4,5},{5,4},{6,7},{7,6},{8,9},{9,8},{10,11... | collective-permute-start | bytes 589832 | tf_op jit(solution)/shard_map/ppermute | solution.py:338
  46.9 10.8 %collective-permute-start.21 = (f32[3,8,16,128]{3,2,1,0:T(8,128)S(1)}, f32[3,8,16,128]{3,2,1,0:T(8,128)S(1)}, u32[]{:S(2)}, u32[]{:S(2)}) collective-permute-start(f32[3,8,16,128]{3,2,1,0:T(8,128)S(1)} %get-tuple-element.73.term), channel_id=1, source_target_pairs={{0,1},{1,0},{2,3},{3,2},{4,5},{5,4},{6,7},{7,6},{8,9},{9,8},{10,11... | collective-permute-start | bytes 589832 | tf_op jit(solution)/shard_map/ppermute | solution.py:338
  49.2 8.5 %collective-permute-start.22 = (f32[3,4,16,128]{3,2,1,0:T(8,128)S(1)}, f32[3,4,16,128]{3,2,1,0:T(8,128)S(1)}, u32[]{:S(2)}, u32[]{:S(2)}) collective-permute-start(f32[3,4,16,128]{3,2,1,0:T(8,128)S(1)} %get-tuple-element.74), channel_id=1, source_target_pairs={{0,1},{1,0},{2,3},{3,2},{4,5},{5,4},{6,7},{7,6},{8,9},{9,8},{10,11... | collective-permute-start | bytes 294920 | tf_op jit(solution)/shard_map/ppermute | solution.py:338
  49.8 7.9 %collective-permute-start.19 = (f32[3,4,16,128]{3,2,1,0:T(8,128)S(1)}, f32[3,4,16,128]{3,2,1,0:T(8,128)S(1)}, u32[]{:S(2)}, u32[]{:S(2)}) collective-permute-start(f32[3,4,16,128]{3,2,1,0:T(8,128)S(1)} %get-tuple-element.72.own), channel_id=1, source_target_pairs={{0,1},{1,0},{2,3},{3,2},{4,5},{5,4},{6,7},{7,6},{8,9},{9,8},{10,11... | collective-permute-start | bytes 294920 | tf_op jit(solution)/shard_map/ppermute | solution.py:338
  49.9 7.8 %collective-permute-start.20 = (f32[3,4,16,128]{3,2,1,0:T(8,128)S(1)}, f32[3,4,16,128]{3,2,1,0:T(8,128)S(1)}, u32[]{:S(2)}, u32[]{:S(2)}) collective-permute-start(f32[3,4,16,128]{3,2,1,0:T(8,128)S(1)} %get-tuple-element.72.own), channel_id=1, source_target_pairs={{0,1},{1,0},{2,3},{3,2},{4,5},{5,4},{6,7},{7,6},{8,9},{9,8},{10,11... | collective-permute-start | bytes 294920 | tf_op jit(solution)/shard_map/ppermute | solution.py:338
  52.9 10.9 %collective-permute-start.25 = (f32[3,8,16,128]{3,2,1,0:T(8,128)S(1)}, f32[3,8,16,128]{3,2,1,0:T(8,128)S(1)}, u32[]{:S(2)}, u32[]{:S(2)}) collective-permute-start(f32[3,8,16,128]{3,2,1,0:T(8,128)S(1)} %get-tuple-element.77), channel_id=1, source_target_pairs={{0,1},{1,0},{2,3},{3,2},{4,5},{5,4},{6,7},{7,6},{8,9},{9,8},{10,11... | collective-permute-start | bytes 589832 | tf_op jit(solution)/shard_map/ppermute | solution.py:338
  61.5 9.4 %collective-permute-start.29 = (f32[3,8,16,128]{3,2,1,0:T(8,128)S(1)}, f32[3,8,16,128]{3,2,1,0:T(8,128)S(1)}, u32[]{:S(2)}, u32[]{:S(2)}) collective-permute-start(f32[3,8,16,128]{3,2,1,0:T(8,128)S(1)} %get-tuple-element.77), channel_id=1, source_target_pairs={{0,1},{1,0},{2,3},{3,2},{4,5},{5,4},{6,7},{7,6},{8,9},{9,8},{10,11... | collective-permute-start | bytes 589832 | tf_op jit(solution)/shard_map/ppermute | solution.py:338
  67.4 8.0 %collective-permute-start.33 = (f32[3,8,16,128]{3,2,1,0:T(8,128)S(1)}, f32[3,8,16,128]{3,2,1,0:T(8,128)S(1)}, u32[]{:S(2)}, u32[]{:S(2)}) collective-permute-start(f32[3,8,16,128]{3,2,1,0:T(8,128)S(1)} %get-tuple-element.83), channel_id=1, source_target_pairs={{0,1},{1,0},{2,3},{3,2},{4,5},{5,4},{6,7},{7,6},{8,9},{9,8},{10,11... | collective-permute-start | bytes 589832 | tf_op jit(solution)/shard_map/ppermute | solution.py:338
  74.4 10.1 %collective-permute-start.37 = (f32[3,8,16,128]{3,2,1,0:T(8,128)S(1)}, f32[3,8,16,128]{3,2,1,0:T(8,128)S(1)}, u32[]{:S(2)}, u32[]{:S(2)}) collective-permute-start(f32[3,8,16,128]{3,2,1,0:T(8,128)S(1)} %get-tuple-element.87), channel_id=1, source_target_pairs={{0,1},{1,0},{2,3},{3,2},{4,5},{5,4},{6,7},{7,6},{8,9},{9,8},{10,11... | collective-permute-start | bytes 589832 | tf_op jit(solution)/shard_map/ppermute | solution.py:338
  75.4 14.2 %collective-permute-start.41 = (f32[3,8,16,128]{3,2,1,0:T(8,128)S(1)}, f32[3,8,16,128]{3,2,1,0:T(8,128)S(1)}, u32[]{:S(2)}, u32[]{:S(2)}) collective-permute-start(f32[3,8,16,128]{3,2,1,0:T(8,128)S(1)} %get-tuple-element.91), channel_id=1, source_target_pairs={{0,1},{1,0},{2,3},{3,2},{4,5},{5,4},{6,7},{7,6},{8,9},{9,8},{10,11... | collective-permute-start | bytes 589832 | tf_op jit(solution)/shard_map/ppermute | solution.py:338
  77.3 7.3 %collective-permute-start.35 = (f32[3,4,16,128]{3,2,1,0:T(8,128)S(1)}, f32[3,4,16,128]{3,2,1,0:T(8,128)S(1)}, u32[]{:S(2)}, u32[]{:S(2)}) collective-permute-start(f32[3,4,16,128]{3,2,1,0:T(8,128)S(1)} %get-tuple-element.86.own), channel_id=1, source_target_pairs={{0,1},{1,0},{2,3},{3,2},{4,5},{5,4},{6,7},{7,6},{8,9},{9,8},{10,11... | collective-permute-start | bytes 294920 | tf_op jit(solution)/shard_map/ppermute | solution.py:338
  81.8 7.8 %collective-permute-start.42 = (f32[3,4,16,128]{3,2,1,0:T(8,128)S(1)}, f32[3,4,16,128]{3,2,1,0:T(8,128)S(1)}, u32[]{:S(2)}, u32[]{:S(2)}) collective-permute-start(f32[3,4,16,128]{3,2,1,0:T(8,128)S(1)} %get-tuple-element.93), channel_id=1, source_target_pairs={{0,1},{1,0},{2,3},{3,2},{4,5},{5,4},{6,7},{7,6},{8,9},{9,8},{10,11... | collective-permute-start | bytes 294920 | tf_op jit(solution)/shard_map/ppermute | solution.py:338
  84.6 7.0 %collective-permute-start.43 = (f32[3,4,16,128]{3,2,1,0:T(8,128)S(1)}, f32[3,4,16,128]{3,2,1,0:T(8,128)S(1)}, u32[]{:S(2)}, u32[]{:S(2)}) collective-permute-start(f32[3,4,16,128]{3,2,1,0:T(8,128)S(1)} %get-tuple-element.94), channel_id=1, source_target_pairs={{0,1},{1,0},{2,3},{3,2},{4,5},{5,4},{6,7},{7,6},{8,9},{9,8},{10,11... | collective-permute-start | bytes 294920 | tf_op jit(solution)/shard_map/ppermute | solution.py:338
  84.6 8.0 %collective-permute-start.44 = (f32[3,4,16,128]{3,2,1,0:T(8,128)S(1)}, f32[3,4,16,128]{3,2,1,0:T(8,128)S(1)}, u32[]{:S(2)}, u32[]{:S(2)}) collective-permute-start(f32[3,4,16,128]{3,2,1,0:T(8,128)S(1)} %get-tuple-element.95), channel_id=1, source_target_pairs={{0,1},{1,0},{2,3},{3,2},{4,5},{5,4},{6,7},{7,6},{8,9},{9,8},{10,11... | collective-permute-start | bytes 294920 | tf_op jit(solution)/shard_map/ppermute | solution.py:338
  84.6 8.2 %collective-permute-start.45 = (f32[3,4,16,128]{3,2,1,0:T(8,128)S(1)}, f32[3,4,16,128]{3,2,1,0:T(8,128)S(1)}, u32[]{:S(2)}, u32[]{:S(2)}) collective-permute-start(f32[3,4,16,128]{3,2,1,0:T(8,128)S(1)} %get-tuple-element.96), channel_id=1, source_target_pairs={{0,1},{1,0},{2,3},{3,2},{4,5},{5,4},{6,7},{7,6},{8,9},{9,8},{10,11... | collective-permute-start | bytes 294920 | tf_op jit(solution)/shard_map/ppermute | solution.py:338
  (32 other events, 185.4 us)

commit v2 on v1

--- a/solution.py
+++ b/solution.py
@@ -386,7 +386,7 @@
     )(*inputs)
 
 
-def on_device(initial, guesses, viscosity, forcing):
+def cycle_pass(initial, guesses, viscosity, forcing):
     times = lax.axis_size("tm")
     column = lax.axis_index("tm")
     every = range(times)
@@ -446,9 +446,10 @@
                     extra[done] = cycle(messages[i], marcher, done)
         if 2 * period + 2 < times:
             pair = (2 * period, 2 * period + 1)
+            wide = 8 if 2 * period + 8 < marcher else DEPTH
             state, *messages, kept = call(
                 functools.partial(march_kernel, [brought.get(t) for t in pair]),
-                [(3, DEPTH), (3, 8 if 2 * period + 8 < marcher else DEPTH), (3, DEPTH), (3, DEPTH)],
+                [(3, DEPTH), (3, wide), (3, DEPTH), (3, DEPTH)],
                 [low, state, high, coarse, terms[pair[0]], terms[pair[1]], term, kept],
                 2,
                 28,
@@ -477,7 +478,7 @@
 
 def solution(mesh):
     return jax.shard_map(
-        on_device,
+        cycle_pass,
         mesh=mesh,
         in_specs=(
             P(None, "space", None, None),

time: 119 us -> 119 us (level)
  no operation moved by 1% of the time
where the time goes in v2:
time: 119 us
  starting transfers between devices  51.7 us (43%)
  waiting for transfers between devices  50.6 us (43%)
  Pallas kernels  12.8 us (11%)
  local copies, waits for them, and re-layouts  1.88 us (2%)
    ppermute x55, starting transfers between devices, permute(): return lax.ppermute(x, AXES, pairs)  51.7 us
    ppermute x55, waiting for transfers between devices, permute(): return lax.ppermute(x, AXES, pairs)  50.6 us
    pallas_call x16, Pallas kernels, call(): pl.pallas_call(kernel, out_shape=outs, in_specs=[VMEM_SPEC] * len(inputs)...  8.84 us
    pallas_call x3, Pallas kernels, emit(): pl.pallas_call(kernel, out_shape=jax.ShapeDtypeStruct((16, 3, DEPTH) + PL...  4 us
  transfers between devices with their start and end apart: 55, of which 20 were waited for; matrix products, arithmetic and copies ran while one was open for 2% of the time, Pallas kernels for 8%

profile of v2, /device:TPU:30, one launch (start us, length us, event | category | flops | bytes accessed | tf_op | source)
XLA Modules:
  0.0 118.5 jit_solution(3988571053427626134)
XLA Ops:
  3.7 3.5 %collective-permute-start.4 = (f32[4,4,16,128]{3,2,1,0:T(8,128)S(1)}, f32[4,4,16,128]{3,2,1,0:T(8,128)S(1)}, u32[]{:S(2)}, u32[]{:S(2)}) collective-permute-start(f32[4,4,16,128]{3,2,1,0:T(8,128)S(1)} %pad_maximum_fusion.own), channel_id=1, source_target_pairs={{0,15},{1,0},{2,1},{3,2},{4,3},{5,4},{6,5},{7,6},{8,7},{9,8},{10,9... | collective-permute-start | bytes 393224 | tf_op jit(solution)/shard_map/ppermute | solution.py:338
  8.2 2.9 %collective-permute-start.6 = (f32[9,4,16,128]{3,2,1,0:T(8,128)S(1)}, f32[9,4,16,128]{3,2,1,0:T(8,128)S(1)}, u32[]{:S(2)}, u32[]{:S(2)}) collective-permute-start(f32[9,4,16,128]{3,2,1,0:T(8,128)S(1)} %bitcast.5), channel_id=1, source_target_pairs={{0,15},{1,0},{2,1},{3,2},{4,3},{5,4},{6,5},{7,6},{8,7},{9,8},{10,9... | collective-permute-start | bytes 884744 | tf_op jit(solution)/shard_map/ppermute | solution.py:338
  11.2 2.9 %collective-permute-start.2 = (f32[3,4,16,128]{3,2,1,0:T(8,128)S(1)}, f32[3,4,16,128]{3,2,1,0:T(8,128)S(1)}, u32[]{:S(2)}, u32[]{:S(2)}) collective-permute-start(f32[3,4,16,128]{3,2,1,0:T(8,128)S(1)} %broadcast_select_fusion.own), channel_id=1, source_target_pairs={{0,15},{1,0},{2,1},{3,2},{4,3},{5,4},{6,5},{7,6},{8,7},{9,8},{10,9... | collective-permute-start | bytes 294920 | tf_op jit(solution)/shard_map/ppermute | solution.py:338
  18.2 3.0 %collective-permute-start.10 = (f32[3,6,16,128]{3,2,1,0:T(8,128)S(1)}, f32[3,6,16,128]{3,2,1,0:T(8,128)S(1)}, u32[]{:S(2)}, u32[]{:S(2)}) collective-permute-start(f32[3,6,16,128]{3,2,1,0:T(8,128)S(1)} %get-tuple-element.61), channel_id=1, source_target_pairs={{0,15},{1,0},{2,1},{3,2},{4,3},{5,4},{6,5},{7,6},{8,7},{9,8},{10,9... | collective-permute-start | bytes 442376 | tf_op jit(solution)/shard_map/ppermute | solution.py:338
  24.5 3.0 %collective-permute-start.12 = (f32[3,6,16,128]{3,2,1,0:T(8,128)S(1)}, f32[3,6,16,128]{3,2,1,0:T(8,128)S(1)}, u32[]{:S(2)}, u32[]{:S(2)}) collective-permute-start(f32[3,6,16,128]{3,2,1,0:T(8,128)S(1)} %get-tuple-element.64), channel_id=1, source_target_pairs={{0,15},{1,0},{2,1},{3,2},{4,3},{5,4},{6,5},{7,6},{8,7},{9,8},{10,9... | collective-permute-start | bytes 442376 | tf_op jit(solution)/shard_map/ppermute | solution.py:338
  27.5 2.8 %collective-permute-done.11.low = f32[3,6,16,128]{3,2,1,0:T(8,128)S(1)} collective-permute-done((f32[3,6,16,128]{3,2,1,0:T(8,128)S(1)}, f32[3,6,16,128]{3,2,1,0:T(8,128)S(1)}, u32[]{:S(2)}, u32[]{:S(2)}) %collective-permute-start.11) | collective-permute-done | bytes 147488 | tf_op jit(solution)/shard_map/ppermute | solution.py:338
  32.1 3.0 %collective-permute-start.8 = (f32[3,6,16,128]{3,2,1,0:T(8,128)S(1)}, f32[3,6,16,128]{3,2,1,0:T(8,128)S(1)}, u32[]{:S(2)}, u32[]{:S(2)}) collective-permute-start(f32[3,6,16,128]{3,2,1,0:T(8,128)S(1)} %get-tuple-element.60), channel_id=1, source_target_pairs={{0,15},{1,0},{2,1},{3,2},{4,3},{5,4},{6,5},{7,6},{8,7},{9,8},{10,9... | collective-permute-start | bytes 442376 | tf_op jit(solution)/shard_map/ppermute | solution.py:338
  36.2 7.1 %collective-permute-done.14.term_two = f32[3,4,16,128]{3,2,1,0:T(8,128)S(1)} collective-permute-done((f32[3,4,16,128]{3,2,1,0:T(8,128)S(1)}, f32[3,4,16,128]{3,2,1,0:T(8,128)S(1)}, u32[]{:S(2)}, u32[]{:S(2)}) %collective-permute-start.14) | collective-permute-done | bytes 98336 | tf_op jit(solution)/shard_map/ppermute | solution.py:338
  44.0 2.9 %collective-permute-start.16 = (f32[3,4,16,128]{3,2,1,0:T(8,128)S(1)}, f32[3,4,16,128]{3,2,1,0:T(8,128)S(1)}, u32[]{:S(2)}, u32[]{:S(2)}) collective-permute-start(f32[3,4,16,128]{3,2,1,0:T(8,128)S(1)} %get-tuple-element.70.own), channel_id=1, source_target_pairs={{0,1},{1,0},{2,3},{3,2},{4,5},{5,4},{6,7},{7,6},{8,9},{9,8},{10,11... | collective-permute-start | bytes 294920 | tf_op jit(solution)/shard_map/ppermute | solution.py:338
  49.9 3.0 %collective-permute-start.20 = (f32[3,4,16,128]{3,2,1,0:T(8,128)S(1)}, f32[3,4,16,128]{3,2,1,0:T(8,128)S(1)}, u32[]{:S(2)}, u32[]{:S(2)}) collective-permute-start(f32[3,4,16,128]{3,2,1,0:T(8,128)S(1)} %get-tuple-element.72.own), channel_id=1, source_target_pairs={{0,1},{1,0},{2,3},{3,2},{4,5},{5,4},{6,7},{7,6},{8,9},{9,8},{10,11... | collective-permute-start | bytes 294920 | tf_op jit(solution)/shard_map/ppermute | solution.py:338
  52.9 4.8 %collective-permute-done.22.term_two = f32[3,4,16,128]{3,2,1,0:T(8,128)S(1)} collective-permute-done((f32[3,4,16,128]{3,2,1,0:T(8,128)S(1)}, f32[3,4,16,128]{3,2,1,0:T(8,128)S(1)}, u32[]{:S(2)}, u32[]{:S(2)}) %collective-permute-start.22) | collective-permute-done | bytes 98336 | tf_op jit(solution)/shard_map/ppermute | solution.py:338
  58.5 2.9 %collective-permute-start.24 = (f32[3,4,16,128]{3,2,1,0:T(8,128)S(1)}, f32[3,4,16,128]{3,2,1,0:T(8,128)S(1)}, u32[]{:S(2)}, u32[]{:S(2)}) collective-permute-start(f32[3,4,16,128]{3,2,1,0:T(8,128)S(1)} %get-tuple-element.76.own), channel_id=1, source_target_pairs={{0,1},{1,0},{2,3},{3,2},{4,5},{5,4},{6,7},{7,6},{8,9},{9,8},{10,11... | collective-permute-start | bytes 294920 | tf_op jit(solution)/shard_map/ppermute | solution.py:338
  64.5 3.0 %collective-permute-start.28 = (f32[3,4,16,128]{3,2,1,0:T(8,128)S(1)}, f32[3,4,16,128]{3,2,1,0:T(8,128)S(1)}, u32[]{:S(2)}, u32[]{:S(2)}) collective-permute-start(f32[3,4,16,128]{3,2,1,0:T(8,128)S(1)} %get-tuple-element.80.own), channel_id=1, source_target_pairs={{0,1},{1,0},{2,3},{3,2},{4,5},{5,4},{6,7},{7,6},{8,9},{9,8},{10,11... | collective-permute-start | bytes 294920 | tf_op jit(solution)/shard_map/ppermute | solution.py:338
  67.4 3.4 %collective-permute-done.30.term_two = f32[3,4,16,128]{3,2,1,0:T(8,128)S(1)} collective-permute-done((f32[3,4,16,128]{3,2,1,0:T(8,128)S(1)}, f32[3,4,16,128]{3,2,1,0:T(8,128)S(1)}, u32[]{:S(2)}, u32[]{:S(2)}) %collective-permute-start.30) | collective-permute-done | bytes 98336 | tf_op jit(solution)/shard_map/ppermute | solution.py:338
  71.5 2.9 %collective-permute-start.32 = (f32[3,4,16,128]{3,2,1,0:T(8,128)S(1)}, f32[3,4,16,128]{3,2,1,0:T(8,128)S(1)}, u32[]{:S(2)}, u32[]{:S(2)}) collective-permute-start(f32[3,4,16,128]{3,2,1,0:T(8,128)S(1)} %get-tuple-element.82.own), channel_id=1, source_target_pairs={{0,1},{1,0},{2,3},{3,2},{4,5},{5,4},{6,7},{7,6},{8,9},{9,8},{10,11... | collective-permute-start | bytes 294920 | tf_op jit(solution)/shard_map/ppermute | solution.py:338
  78.0 2.7 %collective-permute-start.36 = (f32[3,4,16,128]{3,2,1,0:T(8,128)S(1)}, f32[3,4,16,128]{3,2,1,0:T(8,128)S(1)}, u32[]{:S(2)}, u32[]{:S(2)}) collective-permute-start(f32[3,4,16,128]{3,2,1,0:T(8,128)S(1)} %get-tuple-element.86.own), channel_id=1, source_target_pairs={{0,1},{1,0},{2,3},{3,2},{4,5},{5,4},{6,7},{7,6},{8,9},{9,8},{10,11... | collective-permute-start | bytes 294920 | tf_op jit(solution)/shard_map/ppermute | solution.py:338
  81.8 2.7 %collective-permute-done.37.term_one = f32[3,8,16,128]{3,2,1,0:T(8,128)S(1)} collective-permute-done((f32[3,8,16,128]{3,2,1,0:T(8,128)S(1)}, f32[3,8,16,128]{3,2,1,0:T(8,128)S(1)}, u32[]{:S(2)}, u32[]{:S(2)}) %collective-permute-start.37) | collective-permute-done | bytes 196640 | tf_op jit(solution)/shard_map/ppermute | solution.py:338
  85.2 4.4 %collective-permute-done.42.rest_0_ = f32[3,4,16,128]{3,2,1,0:T(8,128)S(1)} collective-permute-done((f32[3,4,16,128]{3,2,1,0:T(8,128)S(1)}, f32[3,4,16,128]{3,2,1,0:T(8,128)S(1)}, u32[]{:S(2)}, u32[]{:S(2)}) %collective-permute-start.42) | collective-permute-done | bytes 98336 | tf_op jit(solution)/shard_map/ppermute | solution.py:338
  92.7 2.7 %collective-permute-done.46.rest_4_ = f32[3,4,16,128]{3,2,1,0:T(8,128)S(1)} collective-permute-done((f32[3,4,16,128]{3,2,1,0:T(8,128)S(1)}, f32[3,4,16,128]{3,2,1,0:T(8,128)S(1)}, u32[]{:S(2)}, u32[]{:S(2)}) %collective-permute-start.46) | collective-permute-done | bytes 98336 | tf_op jit(solution)/shard_map/ppermute | solution.py:338
  95.4 3.3 %collective-permute-done.47.rest_5_ = f32[3,4,16,128]{3,2,1,0:T(8,128)S(1)} collective-permute-done((f32[3,4,16,128]{3,2,1,0:T(8,128)S(1)}, f32[3,4,16,128]{3,2,1,0:T(8,128)S(1)}, u32[]{:S(2)}, u32[]{:S(2)}) %collective-permute-start.47) | collective-permute-done | bytes 98336 | tf_op jit(solution)/shard_map/ppermute | solution.py:338
  99.0 2.9 %collective-permute-start.50 = (f32[3,4,16,128]{3,2,1,0:T(8,128)S(1)}, f32[3,4,16,128]{3,2,1,0:T(8,128)S(1)}, u32[]{:S(2)}, u32[]{:S(2)}) collective-permute-start(f32[3,4,16,128]{3,2,1,0:T(8,128)S(1)} %shard_map.59.own), channel_id=1, source_target_pairs={{0,15},{1,0},{2,1},{3,2},{4,3},{5,4},{6,5},{7,6},{8,7},{9,8},{10,9... | collective-permute-start | bytes 294920 | tf_op jit(solution)/shard_map/ppermute | solution.py:338
  104.9 2.8 %collective-permute-start.52 = (f32[6,4,16,128]{3,2,1,0:T(8,128)S(1)}, f32[6,4,16,128]{3,2,1,0:T(8,128)S(1)}, u32[]{:S(2)}, u32[]{:S(2)}) collective-permute-start(f32[6,4,16,128]{3,2,1,0:T(8,128)S(1)} %shard_map.60.own.stations), channel_id=1, source_target_pairs={{0,15},{1,0},{2,1},{3,2},{4,3},{5,4},{6,5},{7,6},{8,7},{9,8},{10,9... | collective-permute-start | bytes 589832 | tf_op jit(solution)/shard_map/ppermute | solution.py:338
  107.7 3.3 %collective-permute-done.51.low = f32[6,4,16,128]{3,2,1,0:T(8,128)S(1)} collective-permute-done((f32[6,4,16,128]{3,2,1,0:T(8,128)S(1)}, f32[6,4,16,128]{3,2,1,0:T(8,128)S(1)}, u32[]{:S(2)}, u32[]{:S(2)}) %collective-permute-start.51) | collective-permute-done | bytes 196640 | tf_op jit(solution)/shard_map/ppermute | solution.py:338
  111.3 3.0 %collective-permute-start.54 = (f32[3,4,16,128]{3,2,1,0:T(8,128)S(1)}, f32[3,4,16,128]{3,2,1,0:T(8,128)S(1)}, u32[]{:S(2)}, u32[]{:S(2)}) collective-permute-start(f32[3,4,16,128]{3,2,1,0:T(8,128)S(1)} %shard_map.61.station.own), channel_id=1, source_target_pairs={{0,15},{1,0},{2,1},{3,2},{4,3},{5,4},{6,5},{7,6},{8,7},{9,8},{10,9... | collective-permute-start | bytes 294920 | tf_op jit(solution)/shard_map/ppermute | solution.py:338
  (111 shorter events, 39.0 us)
Async XLA Ops:
  0.9 10.2 %collective-permute-start = (f32[3,4,16,128]{3,2,1,0:T(8,128)S(1)}, f32[3,4,16,128]{3,2,1,0:T(8,128)S(1)}, u32[]{:S(2)}, u32[]{:S(2)}) collective-permute-start(f32[3,4,16,128]{3,2,1,0:T(8,128)S(1)} %slice_bitcast_fusion), channel_id=1, source_target_pairs={{0,16},{1,17},{2,18},{3,19},{4,20},{5,21},{6,22},{7,23},{8,24},{9,... | collective-permute-start | bytes 294920 | tf_op jit(solution)/shard_map/ppermute | solution.py:338
  3.7 7.5 %collective-permute-start.3 = (f32[4,4,16,128]{3,2,1,0:T(8,128)S(1)}, f32[4,4,16,128]{3,2,1,0:T(8,128)S(1)}, u32[]{:S(2)}, u32[]{:S(2)}) collective-permute-start(f32[4,4,16,128]{3,2,1,0:T(8,128)S(1)} %pad_maximum_fusion.own), channel_id=1, source_target_pairs={{0,1},{1,2},{2,3},{3,4},{4,5},{5,6},{6,7},{7,8},{8,9},{9,10},{10,1... | collective-permute-start | bytes 393224 | tf_op jit(solution)/shard_map/ppermute | solution.py:338
  3.7 10.4 %collective-permute-start.4 = (f32[4,4,16,128]{3,2,1,0:T(8,128)S(1)}, f32[4,4,16,128]{3,2,1,0:T(8,128)S(1)}, u32[]{:S(2)}, u32[]{:S(2)}) collective-permute-start(f32[4,4,16,128]{3,2,1,0:T(8,128)S(1)} %pad_maximum_fusion.own), channel_id=1, source_target_pairs={{0,15},{1,0},{2,1},{3,2},{4,3},{5,4},{6,5},{7,6},{8,7},{9,8},{10,9... | collective-permute-start | bytes 393224 | tf_op jit(solution)/shard_map/ppermute | solution.py:338
  8.2 7.4 %collective-permute-start.5 = (f32[9,4,16,128]{3,2,1,0:T(8,128)S(1)}, f32[9,4,16,128]{3,2,1,0:T(8,128)S(1)}, u32[]{:S(2)}, u32[]{:S(2)}) collective-permute-start(f32[9,4,16,128]{3,2,1,0:T(8,128)S(1)} %bitcast.4), channel_id=1, source_target_pairs={{0,1},{1,2},{2,3},{3,4},{4,5},{5,6},{6,7},{7,8},{8,9},{9,10},{10,1... | collective-permute-start | bytes 884744 | tf_op jit(solution)/shard_map/ppermute | solution.py:338
  8.2 7.3 %collective-permute-start.6 = (f32[9,4,16,128]{3,2,1,0:T(8,128)S(1)}, f32[9,4,16,128]{3,2,1,0:T(8,128)S(1)}, u32[]{:S(2)}, u32[]{:S(2)}) collective-permute-start(f32[9,4,16,128]{3,2,1,0:T(8,128)S(1)} %bitcast.5), channel_id=1, source_target_pairs={{0,15},{1,0},{2,1},{3,2},{4,3},{5,4},{6,5},{7,6},{8,7},{9,8},{10,9... | collective-permute-start | bytes 884744 | tf_op jit(solution)/shard_map/ppermute | solution.py:338
  30.6 12.7 %collective-permute-start.13 = (f32[3,8,16,128]{3,2,1,0:T(8,128)S(1)}, f32[3,8,16,128]{3,2,1,0:T(8,128)S(1)}, u32[]{:S(2)}, u32[]{:S(2)}) collective-permute-start(f32[3,8,16,128]{3,2,1,0:T(8,128)S(1)} %get-tuple-element.73.term), channel_id=1, source_target_pairs={{0,240},{1,241},{2,242},{3,243},{4,244},{5,245},{6,246},{7,247},{8... | collective-permute-start | bytes 589832 | tf_op jit(solution)/shard_map/ppermute | solution.py:338
  32.1 11.2 %collective-permute-start.7 = (f32[3,6,16,128]{3,2,1,0:T(8,128)S(1)}, f32[3,6,16,128]{3,2,1,0:T(8,128)S(1)}, u32[]{:S(2)}, u32[]{:S(2)}) collective-permute-start(f32[3,6,16,128]{3,2,1,0:T(8,128)S(1)} %get-tuple-element.59.own), channel_id=1, source_target_pairs={{0,1},{1,2},{2,3},{3,4},{4,5},{5,6},{6,7},{7,8},{8,9},{9,10},{10,1... | collective-permute-start | bytes 442376 | tf_op jit(solution)/shard_map/ppermute | solution.py:338
  32.1 11.2 %collective-permute-start.8 = (f32[3,6,16,128]{3,2,1,0:T(8,128)S(1)}, f32[3,6,16,128]{3,2,1,0:T(8,128)S(1)}, u32[]{:S(2)}, u32[]{:S(2)}) collective-permute-start(f32[3,6,16,128]{3,2,1,0:T(8,128)S(1)} %get-tuple-element.60), channel_id=1, source_target_pairs={{0,15},{1,0},{2,1},{3,2},{4,3},{5,4},{6,5},{7,6},{8,7},{9,8},{10,9... | collective-permute-start | bytes 442376 | tf_op jit(solution)/shard_map/ppermute | solution.py:338
  35.1 8.2 %collective-permute-start.14 = (f32[3,4,16,128]{3,2,1,0:T(8,128)S(1)}, f32[3,4,16,128]{3,2,1,0:T(8,128)S(1)}, u32[]{:S(2)}, u32[]{:S(2)}) collective-permute-start(f32[3,4,16,128]{3,2,1,0:T(8,128)S(1)} %get-tuple-element.74), channel_id=1, source_target_pairs={{0,1},{1,0},{2,3},{3,2},{4,5},{5,4},{6,7},{7,6},{8,9},{9,8},{10,11... | collective-permute-start | bytes 294920 | tf_op jit(solution)/shard_map/ppermute | solution.py:338
  36.2 13.0 %collective-permute-start.17 = (f32[3,8,16,128]{3,2,1,0:T(8,128)S(1)}, f32[3,8,16,128]{3,2,1,0:T(8,128)S(1)}, u32[]{:S(2)}, u32[]{:S(2)}) collective-permute-start(f32[3,8,16,128]{3,2,1,0:T(8,128)S(1)} %get-tuple-element.73.term), channel_id=1, source_target_pairs={{0,1},{1,0},{2,3},{3,2},{4,5},{5,4},{6,7},{7,6},{8,9},{9,8},{10,11... | collective-permute-start | bytes 589832 | tf_op jit(solution)/shard_map/ppermute | solution.py:338
  46.9 10.8 %collective-permute-start.21 = (f32[3,8,16,128]{3,2,1,0:T(8,128)S(1)}, f32[3,8,16,128]{3,2,1,0:T(8,128)S(1)}, u32[]{:S(2)}, u32[]{:S(2)}) collective-permute-start(f32[3,8,16,128]{3,2,1,0:T(8,128)S(1)} %get-tuple-element.73.term), channel_id=1, source_target_pairs={{0,1},{1,0},{2,3},{3,2},{4,5},{5,4},{6,7},{7,6},{8,9},{9,8},{10,11... | collective-permute-start | bytes 589832 | tf_op jit(solution)/shard_map/ppermute | solution.py:338
  49.2 8.5 %collective-permute-start.22 = (f32[3,4,16,128]{3,2,1,0:T(8,128)S(1)}, f32[3,4,16,128]{3,2,1,0:T(8,128)S(1)}, u32[]{:S(2)}, u32[]{:S(2)}) collective-permute-start(f32[3,4,16,128]{3,2,1,0:T(8,128)S(1)} %get-tuple-element.74), channel_id=1, source_target_pairs={{0,1},{1,0},{2,3},{3,2},{4,5},{5,4},{6,7},{7,6},{8,9},{9,8},{10,11... | collective-permute-start | bytes 294920 | tf_op jit(solution)/shard_map/ppermute | solution.py:338
  49.8 7.9 %collective-permute-start.19 = (f32[3,4,16,128]{3,2,1,0:T(8,128)S(1)}, f32[3,4,16,128]{3,2,1,0:T(8,128)S(1)}, u32[]{:S(2)}, u32[]{:S(2)}) collective-permute-start(f32[3,4,16,128]{3,2,1,0:T(8,128)S(1)} %get-tuple-element.72.own), channel_id=1, source_target_pairs={{0,1},{1,0},{2,3},{3,2},{4,5},{5,4},{6,7},{7,6},{8,9},{9,8},{10,11... | collective-permute-start | bytes 294920 | tf_op jit(solution)/shard_map/ppermute | solution.py:338
  49.9 7.8 %collective-permute-start.20 = (f32[3,4,16,128]{3,2,1,0:T(8,128)S(1)}, f32[3,4,16,128]{3,2,1,0:T(8,128)S(1)}, u32[]{:S(2)}, u32[]{:S(2)}) collective-permute-start(f32[3,4,16,128]{3,2,1,0:T(8,128)S(1)} %get-tuple-element.72.own), channel_id=1, source_target_pairs={{0,1},{1,0},{2,3},{3,2},{4,5},{5,4},{6,7},{7,6},{8,9},{9,8},{10,11... | collective-permute-start | bytes 294920 | tf_op jit(solution)/shard_map/ppermute | solution.py:338
  52.9 10.9 %collective-permute-start.25 = (f32[3,8,16,128]{3,2,1,0:T(8,128)S(1)}, f32[3,8,16,128]{3,2,1,0:T(8,128)S(1)}, u32[]{:S(2)}, u32[]{:S(2)}) collective-permute-start(f32[3,8,16,128]{3,2,1,0:T(8,128)S(1)} %get-tuple-element.77), channel_id=1, source_target_pairs={{0,1},{1,0},{2,3},{3,2},{4,5},{5,4},{6,7},{7,6},{8,9},{9,8},{10,11... | collective-permute-start | bytes 589832 | tf_op jit(solution)/shard_map/ppermute | solution.py:338
  61.5 9.4 %collective-permute-start.29 = (f32[3,8,16,128]{3,2,1,0:T(8,128)S(1)}, f32[3,8,16,128]{3,2,1,0:T(8,128)S(1)}, u32[]{:S(2)}, u32[]{:S(2)}) collective-permute-start(f32[3,8,16,128]{3,2,1,0:T(8,128)S(1)} %get-tuple-element.77), channel_id=1, source_target_pairs={{0,1},{1,0},{2,3},{3,2},{4,5},{5,4},{6,7},{7,6},{8,9},{9,8},{10,11... | collective-permute-start | bytes 589832 | tf_op jit(solution)/shard_map/ppermute | solution.py:338
  67.4 8.0 %collective-permute-start.33 = (f32[3,8,16,128]{3,2,1,0:T(8,128)S(1)}, f32[3,8,16,128]{3,2,1,0:T(8,128)S(1)}, u32[]{:S(2)}, u32[]{:S(2)}) collective-permute-start(f32[3,8,16,128]{3,2,1,0:T(8,128)S(1)} %get-tuple-element.83), channel_id=1, source_target_pairs={{0,1},{1,0},{2,3},{3,2},{4,5},{5,4},{6,7},{7,6},{8,9},{9,8},{10,11... | collective-permute-start | bytes 589832 | tf_op jit(solution)/shard_map/ppermute | solution.py:338
  74.4 10.1 %collective-permute-start.37 = (f32[3,8,16,128]{3,2,1,0:T(8,128)S(1)}, f32[3,8,16,128]{3,2,1,0:T(8,128)S(1)}, u32[]{:S(2)}, u32[]{:S(2)}) collective-permute-start(f32[3,8,16,128]{3,2,1,0:T(8,128)S(1)} %get-tuple-element.87), channel_id=1, source_target_pairs={{0,1},{1,0},{2,3},{3,2},{4,5},{5,4},{6,7},{7,6},{8,9},{9,8},{10,11... | collective-permute-start | bytes 589832 | tf_op jit(solution)/shard_map/ppermute | solution.py:338
  75.4 14.2 %collective-permute-start.41 = (f32[3,8,16,128]{3,2,1,0:T(8,128)S(1)}, f32[3,8,16,128]{3,2,1,0:T(8,128)S(1)}, u32[]{:S(2)}, u32[]{:S(2)}) collective-permute-start(f32[3,8,16,128]{3,2,1,0:T(8,128)S(1)} %get-tuple-element.91), channel_id=1, source_target_pairs={{0,1},{1,0},{2,3},{3,2},{4,5},{5,4},{6,7},{7,6},{8,9},{9,8},{10,11... | collective-permute-start | bytes 589832 | tf_op jit(solution)/shard_map/ppermute | solution.py:338
  77.3 7.3 %collective-permute-start.35 = (f32[3,4,16,128]{3,2,1,0:T(8,128)S(1)}, f32[3,4,16,128]{3,2,1,0:T(8,128)S(1)}, u32[]{:S(2)}, u32[]{:S(2)}) collective-permute-start(f32[3,4,16,128]{3,2,1,0:T(8,128)S(1)} %get-tuple-element.86.own), channel_id=1, source_target_pairs={{0,1},{1,0},{2,3},{3,2},{4,5},{5,4},{6,7},{7,6},{8,9},{9,8},{10,11... | collective-permute-start | bytes 294920 | tf_op jit(solution)/shard_map/ppermute | solution.py:338
  81.8 7.8 %collective-permute-start.42 = (f32[3,4,16,128]{3,2,1,0:T(8,128)S(1)}, f32[3,4,16,128]{3,2,1,0:T(8,128)S(1)}, u32[]{:S(2)}, u32[]{:S(2)}) collective-permute-start(f32[3,4,16,128]{3,2,1,0:T(8,128)S(1)} %get-tuple-element.93), channel_id=1, source_target_pairs={{0,1},{1,0},{2,3},{3,2},{4,5},{5,4},{6,7},{7,6},{8,9},{9,8},{10,11... | collective-permute-start | bytes 294920 | tf_op jit(solution)/shard_map/ppermute | solution.py:338
  84.6 7.0 %collective-permute-start.43 = (f32[3,4,16,128]{3,2,1,0:T(8,128)S(1)}, f32[3,4,16,128]{3,2,1,0:T(8,128)S(1)}, u32[]{:S(2)}, u32[]{:S(2)}) collective-permute-start(f32[3,4,16,128]{3,2,1,0:T(8,128)S(1)} %get-tuple-element.94), channel_id=1, source_target_pairs={{0,1},{1,0},{2,3},{3,2},{4,5},{5,4},{6,7},{7,6},{8,9},{9,8},{10,11... | collective-permute-start | bytes 294920 | tf_op jit(solution)/shard_map/ppermute | solution.py:338
  84.6 8.0 %collective-permute-start.44 = (f32[3,4,16,128]{3,2,1,0:T(8,128)S(1)}, f32[3,4,16,128]{3,2,1,0:T(8,128)S(1)}, u32[]{:S(2)}, u32[]{:S(2)}) collective-permute-start(f32[3,4,16,128]{3,2,1,0:T(8,128)S(1)} %get-tuple-element.95), channel_id=1, source_target_pairs={{0,1},{1,0},{2,3},{3,2},{4,5},{5,4},{6,7},{7,6},{8,9},{9,8},{10,11... | collective-permute-start | bytes 294920 | tf_op jit(solution)/shard_map/ppermute | solution.py:338
  84.6 8.2 %collective-permute-start.45 = (f32[3,4,16,128]{3,2,1,0:T(8,128)S(1)}, f32[3,4,16,128]{3,2,1,0:T(8,128)S(1)}, u32[]{:S(2)}, u32[]{:S(2)}) collective-permute-start(f32[3,4,16,128]{3,2,1,0:T(8,128)S(1)} %get-tuple-element.96), channel_id=1, source_target_pairs={{0,1},{1,0},{2,3},{3,2},{4,5},{5,4},{6,7},{7,6},{8,9},{9,8},{10,11... | collective-permute-start | bytes 294920 | tf_op jit(solution)/shard_map/ppermute | solution.py:338
  (32 other events, 185.4 us)

commit v3 on v2

v3 whole, which is shorter than its diff:
```python
import functools

import jax
import jax.numpy as jnp
from jax import lax
from jax.experimental import pallas as pl
from jax.experimental.pallas import tpu as pltpu
from jax.sharding import PartitionSpec as P


time_step = 0.019
FINE, MIDDLE, COARSE = time_step, 2.0 * time_step, 8.0 * time_step
DEPTH = 4
AXES = ("tm", "space")


def slab(low, own, high, base=0):
    def get(c, z):
        if z < 0:
            return low[base + c, z + DEPTH]
        if z >= DEPTH:
            return high[base + c, z - DEPTH]
        return own[base + c, z]

    return get


def deep_slab(lower, low, own, high, higher, lowest=None, highest=None):
    near = slab(low, own, high)

    def get(c, z):
        if z < -2 * DEPTH:
            return lowest[c, 0]
        if z < -DEPTH:
            return lower[c, z + 2 * DEPTH]
        if z >= 3 * DEPTH:
            return highest[c, 0]
        if z >= 2 * DEPTH:
            return higher[c, z - 2 * DEPTH]
        return near(c, z)

    return get


def reader(ref, shift=DEPTH):
    return lambda c, z: ref[c, z + shift]


def writer(ref, shift=DEPTH):
    def put(c, z, value):
        ref[c, z + shift] = value

    return put


def advance(get, put, first, last, table, step_size):
    edge = (table.shape[1] - DEPTH) // 2
    for z in range(first, last) if isinstance(first, int) else [first + i for i in range(last)]:
        alpha = table[0, z + edge]
        keep = table[1, z + edge]
        center = [get(c, z) for c in range(3)]
        half = [value * (0.5 * step_size) for value in center]
        east, west = alpha - half[0], alpha + half[0]
        north, south = alpha - half[1], alpha + half[1]
        up, down = alpha - half[2], alpha + half[2]
        for c in range(3):
            value = center[c]
            along_x = east * pltpu.roll(value, 127, 1) + west * pltpu.roll(value, 1, 1)
            along_y = north * pltpu.roll(value, 15, 0) + south * pltpu.roll(value, 1, 0)
            along_z = up * get(c, z + 1) + down * get(c, z - 1)
            put(c, z, (keep * value + table[2 + c, z + edge]) + along_x + (along_y + along_z))


def advance_halves(get, put, first, last, table, step_size):
    count = (last - first) // 2

    def body(i, carry):
        advance(get, put, first + i * count, count, table, step_size)
        return carry

    lax.fori_loop(0, 2, body, 0)


def fill(get, table, step_size):
    edge = (table.shape[1] - DEPTH) // 2
    for z in range(-edge, DEPTH + edge):
        alpha = get(3, z) * step_size
        table[0, z + edge] = alpha
        table[1, z + edge] = 1.0 - 6.0 * alpha
        for c in range(3):
            table[2 + c, z + edge] = get(c, z) * step_size


def tables_kernel(low, own, high, fine, middle, coarse):
    get = slab(low, own, high)
    for table, step_size in ((fine, FINE), (middle, MIDDLE), (coarse, COARSE)):
        fill(get, table, step_size)


def wide_table_kernel(lower, low, own, high, higher, middle):
    fill(deep_slab(lower, low, own, high, higher), middle, MIDDLE)


def defects_kernel(low, own, high, fine, middle, out, one, two):
    def body(i, carry):
        start = slab(low, own, high, 3 * (i + 1))
        advance(start, writer(one), -3, 7, fine, FINE)
        advance(reader(one), writer(two), -2, 6, fine, FINE)
        advance(reader(two), writer(one), -1, 5, fine, FINE)

        def store(c, z, value):
            out[i, c, z] = value

        def subtract(c, z, value):
            out[i, c, z] = out[i, c, z] - value

        advance(reader(one), store, 0, 4, fine, FINE)
        advance(start, writer(two), -1, 5, middle, MIDDLE)
        advance(reader(two), subtract, 0, 4, middle, MIDDLE)
        return carry

    lax.fori_loop(0, out.shape[0], body, 0)


def opening_kernel(
    member_low, members, member_high, low, own, high, fine, middle, next_one, to_up, to_down,
    one, two, both, moved,
):
    near = slab(member_low, members, member_high)
    for get, base in ((near, 0), (slab(low, own, high), 3)):
        for c in range(3):
            for z in range(-DEPTH, 2 * DEPTH):
                both[base + c, z + DEPTH] = get(c, z)

    def body(i, carry):
        def store(c, z, value):
            moved[3 * i + c, z] = value

        advance(lambda c, z: both[3 * i + c, z + DEPTH], writer(one), -3, 7, fine, FINE)
        advance(reader(one), writer(two), -2, 6, fine, FINE)
        advance(reader(two), writer(one), -1, 5, fine, FINE)
        advance(reader(one), store, 0, 4, fine, FINE)
        return carry

    lax.fori_loop(0, 2, body, 0)

    def subtract(c, z, value):
        next_one[0, c, z] = moved[c, z] - value

    advance(near, writer(one), -1, 5, middle, MIDDLE)
    advance(reader(one), subtract, 0, 4, middle, MIDDLE)
    for c in range(3):
        for z in range(DEPTH):
            to_up[c, z] = moved[3 + c, z]
            to_down[c, z] = moved[3 + c, z]
        for z in range(2):
            to_up[c, 4 + z] = next_one[0, c, 2 + z]
            to_down[c, 4 + z] = next_one[0, c, z]


def remainder_kernel(
    low, own, high, middle, coarse, next_one, others, first, initial, fields,
    defect, rest, late, deep_up, deep_down, kept, one,
):
    start = slab(low, own, high)
    advance(start, writer(one), -1, 5, middle, MIDDLE)

    def subtract(c, z, value):
        value = first[c, z] - value
        defect[c, z] = value
        late[3 + c, z] = value
        if z > 0:
            deep_up[4 + c, z - 1] = value
        if z < 3:
            deep_down[4 + c, z] = value

    advance(reader(one), subtract, 0, 4, middle, MIDDLE)
    advance(start, writer(one), -1, 5, coarse, COARSE)

    def subtract_rest(c, z, value):
        rest[c, z] = others[1, c, z] - value

    advance(reader(one), subtract_rest, 0, 4, coarse, COARSE)
    for c in range(3):
        for z in range(DEPTH):
            late[c, z] = initial[c, z]
            late[6 + c, z] = next_one[0, c, z]
            late[9 + c, z] = others[0, c, z]
            kept[c, z] = initial[c, z]
        deep_up[4 + c, 3] = next_one[0, c, 3]
        deep_down[4 + c, 3] = next_one[0, c, 0]
    for c in range(4):
        for z in range(DEPTH):
            deep_up[c, z] = fields[c, z]
            deep_down[c, z] = fields[c, z]


def second_kernel(low, own, high, middle, defects, others, rest, to_up, to_down, one, two):
    def added(c, z, value):
        if z < 0:
            term = low[c, 4 + 2 + z]
        elif z >= DEPTH:
            term = high[c, 4 + z - DEPTH]
        else:
            term = defects[0, c, z]
        two[c, z + DEPTH] = value + term

    def third(c, z, value):
        value = value + others[0, c, z]
        to_up[c, z] = value
        to_down[c, z] = value

    advance(slab(low, own, high), writer(one), -3, 7, middle, MIDDLE)
    advance(reader(one), added, -2, 6, middle, MIDDLE)
    advance(reader(two), writer(one), -1, 5, middle, MIDDLE)
    advance(reader(one), third, 0, 4, middle, MIDDLE)
    for c in range(3):
        for z in range(2):
            to_up[c, 4 + z] = rest[c, 2 + z]
            to_down[c, 4 + z] = rest[c, z]


def coarse_defect_kernel(low, own, high, middle, rest, out, middle_out, one):
    def added(c, z, value):
        if z < 0:
            term = low[c, 4 + 2 + z]
        elif z >= DEPTH:
            term = high[c, 4 + z - DEPTH]
        else:
            term = rest[c, z]
        out[c, z + 2] = value + term
        if 0 <= z < DEPTH:
            middle_out[c, z] = value + term

    advance(slab(low, own, high), writer(one), -3, 7, middle, MIDDLE)
    advance(reader(one), added, -2, 6, middle, MIDDLE)


def take(kept, arrived):
    shift = (arrived.shape[1] - DEPTH) // 2
    for c in range(3):
        for z in range(DEPTH):
            kept[c, z] = arrived[c, z + shift]


def march_kernel(
    done, low, own, high, coarse, term_one, term_two, term, kept_in,
    state, message_one, message_two, kept, one, two,
):
    def first(c, z, value):
        value = value + term_one[c, z + 2]
        two[c, z + DEPTH] = value
        if 0 <= z + edge < message_one.shape[1]:
            message_one[c, z + edge] = value

    def second(c, z, value):
        value = value + term_two[c, z]
        state[c, z] = value
        message_two[c, z] = value

    edge = (message_one.shape[1] - DEPTH) // 2
    column = lax.axis_index("tm")
    marching = column == lax.axis_size("tm") - 1

    @pl.when(marching)
    def _():
        advance(slab(low, own, high), writer(one), -3, 7, coarse, COARSE)
        advance(reader(one), first, -2, 6, coarse, COARSE)
        advance(reader(two), writer(one), -1, 5, coarse, COARSE)
        advance(reader(one), second, 0, 4, coarse, COARSE)

    @pl.when(jnp.logical_not(marching))
    def _():
        for c in range(3):
            for z in range(message_one.shape[1]):
                message_one[c, z] = term[c, z + 2 - edge]
            for z in range(DEPTH):
                message_two[c, z] = term[c, z + 2]
                state[c, z] = own[c, z]

    if done[0] is not None:
        pl.when(column == done[0])(functools.partial(take, kept, term_one))
    if done[1] is not None:
        pl.when(column == done[1])(functools.partial(take, kept, term_two))


def last_march_kernel(done, low, own, high, coarse, term_one, kept, *rest):
    arrivals, (start, one) = rest[:-2], rest[-2:]
    column = lax.axis_index("tm")
    marching = column == lax.axis_size("tm") - 1

    def first(c, z, value):
        start[c, z] = value + term_one[c, z + 2]

    @pl.when(marching)
    def _():
        advance(slab(low, own, high), writer(one), -1, 5, coarse, COARSE)
        advance(reader(one), first, 0, 4, coarse, COARSE)

    pl.when(jnp.logical_not(marching))(functools.partial(take, start, kept))
    for t, arrived in zip(done, (term_one,) + arrivals):
        if t is not None:
            pl.when(column == t)(functools.partial(take, start, arrived))


SHIFT = 2 * DEPTH + 2
FINE_SHIFT = 3


def finish_kernel(
    lowest, lower, low, own, high, higher, highest, fine, middle, coarse, term,
    deep_low, late_low, late, late_high, deep_high, result, rows, one, station, anchors, two, sem,
):
    def copy(i):
        return pltpu.make_async_copy(rows.at[i], result.at[i], sem.at[i])

    start = deep_slab(lower, low, own, high, higher, lowest, highest)
    near = slab(late_low, late, late_high, 3)
    for c in range(3):
        for z in range(-FINE_SHIFT, DEPTH + FINE_SHIFT):
            anchors[c, z + FINE_SHIFT] = start(c, z)

    def end(c, z, value):
        rows[15, c, z] = value + term[c, z + 2]

    advance(start, writer(one, SHIFT), -1, 5, coarse, COARSE)
    advance(reader(one, SHIFT), end, 0, 4, coarse, COARSE)
    copy(15).start()

    for number in range(3):
        reach = 7 - 2 * number

        def store(c, z, value):
            if z < -DEPTH:
                value = value + (deep_low[4 + c, 3] if number else deep_low[4 + c, z + 7])
            elif z >= 2 * DEPTH:
                value = value + (deep_high[4 + c, 3] if number else deep_high[4 + c, z - 8])
            else:
                value = value + near(3 * number + c, z)
            if number < 2:
                station[c, z + SHIFT] = value
            if -FINE_SHIFT <= z < DEPTH + FINE_SHIFT:
                anchors[3 * number + 3 + c, z + FINE_SHIFT] = value
            if 0 <= z < DEPTH:
                rows[4 * number + 3, c, z] = value

        whole = advance_halves if number else advance
        whole(start, writer(one, SHIFT), -reach - 1, reach + 5, middle, MIDDLE)
        advance(reader(one, SHIFT), store, -reach, reach + 4, middle, MIDDLE)
        start = reader(station, SHIFT)
        copy(4 * number + 3).start()

    def rest(i, carry):
        def first(c, z, value):
            one[c, z + SHIFT] = value
            if 0 <= z < DEPTH:
                rows[4 * i, c, z] = value

        def second(c, z, value):
            two[c, z + DEPTH] = value
            if 0 <= z < DEPTH:
                rows[4 * i + 1, c, z] = value

        def third(c, z, value):
            rows[4 * i + 2, c, z] = value

        advance(lambda c, z: anchors[3 * i + c, z + FINE_SHIFT], first, -2, 6, fine, FINE)
        advance(reader(one, SHIFT), second, -1, 5, fine, FINE)
        advance(reader(two), third, 0, 4, fine, FINE)
        for j in range(3):
            copy(4 * i + j).start()
        return carry

    lax.fori_loop(0, 4, rest, 0)
    for i in range(16):
        copy(i).wait()


def permute(x, moves):
    spaces = lax.axis_size("space")
    times = lax.axis_size("tm")
    pairs = []
    for t in range(times):
        if t in moves:
            target, by = moves[t]
            pairs += [(t * spaces + s, target * spaces + (s + by) % spaces) for s in range(spaces)]
        else:
            pairs += [(t * spaces + s, t * spaces + (s ^ 1)) for s in range(spaces)]
    return lax.ppermute(x, AXES, pairs)


def halos(to_up, to_down, columns, by=1):
    return (
        permute(to_up, {t: (t, by) for t in columns}),
        permute(to_down, {t: (t, -by) for t in columns}),
    )


def cycle(x, *columns):
    return permute(x, {t: (after, 0) for t, after in zip(columns, columns[1:] + columns[:1])})


PLANE = (16, 128)
WORK = pltpu.VMEM((3, 3 * DEPTH) + PLANE, jnp.float32)
VMEM_SPEC = pl.BlockSpec(memory_space=pltpu.VMEM)


def call(kernel, shapes, inputs, works, units, aliases=None, more=()):
    outs = [jax.ShapeDtypeStruct(tuple(shape) + PLANE, jnp.float32) for shape in shapes]
    result = pl.pallas_call(
        kernel,
        out_shape=outs,
        in_specs=[VMEM_SPEC] * len(inputs),
        out_specs=[VMEM_SPEC] * len(outs),
        scratch_shapes=[WORK] * works + [pltpu.VMEM(tuple(m) + PLANE, jnp.float32) for m in more],
        input_output_aliases=aliases or {},
        compiler_params=pltpu.CompilerParams(vmem_limit_bytes=8 << 20),
        cost_estimate=pl.CostEstimate(flops=units * 120000, bytes_accessed=units * 60000, transcendentals=0),
    )(*inputs)
    return result[0] if len(outs) == 1 else result


def finish(inputs):
    def work(*shape):
        return pltpu.VMEM(shape + PLANE, jnp.float32)

    wide = work(3, 2 * SHIFT + DEPTH)
    scratch = [work(16, 3, DEPTH), wide, wide, work(12, 2 * FINE_SHIFT + DEPTH), WORK]
    return pl.pallas_call(
        finish_kernel,
        name="finish",
        out_shape=jax.ShapeDtypeStruct((16, 3, DEPTH) + PLANE, jnp.float32),
        in_specs=[VMEM_SPEC] * len(inputs),
        out_specs=pl.BlockSpec(memory_space=pl.ANY),
        scratch_shapes=scratch + [pltpu.SemaphoreType.DMA((16,))],
        compiler_params=pltpu.CompilerParams(vmem_limit_bytes=8 << 20),
        cost_estimate=pl.CostEstimate(flops=20000000, bytes_accessed=4000000, transcendentals=0),
    )(*inputs)


def cycle_pass(initial, guesses, viscosity, forcing):
    times = lax.axis_size("tm")
    column = lax.axis_index("tm")
    every = range(times)
    marcher = times - 1
    alone = (marcher,)

    last, guesses = lax.optimization_barrier((guesses[3], guesses))
    members = guesses[:3].reshape((9,) + guesses.shape[2:])
    incoming = permute(last, {t: ((t + 1) % times, 0) for t in every})
    member_low, member_high = halos(members, members, every)
    fields = jnp.concatenate([forcing, viscosity[None]], axis=0)
    field_low, field_high = halos(fields, fields, every)
    opening = jnp.where(column == 0, initial, incoming)
    open_low, open_high = halos(opening, opening, every)

    table = (5, 3 * DEPTH)
    fine, middle, coarse = call(tables_kernel, [table] * 3, [field_low, fields, field_high], 0, 10)
    inputs = [member_low, members, member_high, fine, middle]
    defects, to_up, to_down = call(
        opening_kernel,
        [(1, 3, DEPTH), (3, 6), (3, 6)],
        inputs[:3] + [open_low, opening, open_high, fine, middle],
        2,
        66,
        more=[(6, 3 * DEPTH), (6, DEPTH)],
    )
    low, high = halos(to_up, to_down, every)
    others = call(defects_kernel, [(2, 3, DEPTH)], inputs, 2, 76)
    _, rest, late, deep_up, deep_down, kept = call(
        remainder_kernel,
        [(3, DEPTH)] * 2 + [(12, DEPTH)] + [(7, DEPTH)] * 2 + [(3, DEPTH)],
        [open_low, opening, open_high, middle, coarse, defects, others, to_up, initial, fields],
        1,
        20,
    )
    second_up, second_down = call(
        second_kernel, [(3, 6)] * 2, [low, to_up, high, middle, defects, others, rest], 2, 28
    )
    rest_low, rest_high = halos(second_up, second_down, every)
    term, term_middle = call(
        coarse_defect_kernel,
        [(3, 8), (3, DEPTH)],
        [rest_low, second_up, rest_high, middle, rest],
        1,
        18,
    )

    terms = {marcher: term}
    ahead = (term, term_middle)
    for t in range(min(6, marcher)):
        if t == 4:
            ahead = lax.optimization_barrier((term, term_middle, terms[0], terms[1]))
            ahead, (terms[0], terms[1]) = ahead[:2], ahead[2:]
        terms[t] = cycle(ahead[t % 2], t, marcher)
    late_low, late_high = halos(late, late, every)
    deep_low, deep_high = halos(deep_up, deep_down, every, 2)
    state, low, high = late, late_low, late_high
    brought, extra = {}, {}
    messages = None
    for period in range(times // 2):
        if period:
            low, high = halos(state, state, alone)
            for i in range(2):
                t = 2 * period + 6 + i
                done = 2 * period - 1 + i
                if period == 1 and t < marcher:
                    terms[t] = cycle(messages[i], t, marcher)
                    t -= 2
                if t < marcher:
                    terms[t] = cycle(messages[i], t, marcher, done)
                    brought[t] = done
                else:
                    extra[done] = cycle(messages[i], marcher, done)
        if 2 * period + 2 < times:
            pair = (2 * period, 2 * period + 1)
            wide = 8 if 2 * period + 8 < marcher else DEPTH
            state, *messages, kept = call(
                functools.partial(march_kernel, [brought.get(t) for t in pair]),
                [(3, DEPTH), (3, wide), (3, DEPTH), (3, DEPTH)],
                [low, state, high, coarse, terms[pair[0]], terms[pair[1]], term, kept],
                2,
                28,
                {7: 3},
            )
        else:
            start = call(
                functools.partial(last_march_kernel, [brought.get(2 * period)] + list(extra)),
                [(3, DEPTH)],
                [low, state, high, coarse, terms[2 * period], kept] + list(extra.values()),
                1,
                10,
            )

    wide = call(
        wide_table_kernel,
        [(5, 5 * DEPTH)],
        [deep_low, field_low, fields, field_high, deep_high],
        0,
        5,
    )
    lowest, highest = halos(start[:, DEPTH - 1 :], start[:, :1], every, 3)
    lower, higher = halos(start, start, every, 2)
    low, high = halos(start, start, every)
    return finish(
        [lowest, lower, low, start, high, higher, highest, fine, wide, coarse, term]
        + [deep_low, late_low, late, late_high, deep_high]
    )


def solution(mesh):
    return jax.shard_map(
        cycle_pass,
        mesh=mesh,
        in_specs=(
            P(None, "space", None, None),
            P("tm", None, "space", None, None),
            P("space", None, None),
            P(None, "space", None, None),
        ),
        out_specs=P("tm", None, "space", None, None),
        check_vma=False,
    )
```

time: 119 us -> 123 us (1.034)
  the two profiles are of different devices: /device:TPU:30 before, /device:TPU:31 now
where the time goes in v3:
time: 123 us
  starting transfers between devices  75.5 us (61%)
  waiting for transfers between devices  31 us (25%)
  Pallas kernels  12.9 us (10%)
  local copies, waits for them, and re-layouts  1.89 us (2%)
    ppermute x57, starting transfers between devices, permute(): return lax.ppermute(x, AXES, pairs)  75.5 us
    ppermute x57, waiting for transfers between devices, permute(): return lax.ppermute(x, AXES, pairs)  31 us
    pallas_call x15, Pallas kernels, call(): pl.pallas_call(kernel, out_shape=outs, in_specs=[VMEM_SPEC] * len(inputs)...  8.62 us
    pallas_call x1, Pallas kernels, finish(): pl.pallas_call(finish_kernel, name='finish', out_shape=jax.ShapeDtypeStru...  4.27 us
  transfers between devices with their start and end apart: 57, of which 18 were waited for; matrix products, arithmetic and copies ran while one was open for 2% of the time, Pallas kernels for 6%

profile of v3, /device:TPU:31, one launch (start us, length us, event | category | flops | bytes accessed | tf_op | source)
XLA Modules:
  0.0 122.7 jit_solution(9478097421307336241)
XLA Ops:
  1.8 2.5 %collective-permute-start.4 = (f32[4,4,16,128]{3,2,1,0:T(8,128)S(1)}, f32[4,4,16,128]{3,2,1,0:T(8,128)S(1)}, u32[]{:S(2)}, u32[]{:S(2)}) collective-permute-start(f32[4,4,16,128]{3,2,1,0:T(8,128)S(1)} %pad_maximum_fusion.own.fields), channel_id=1, source_target_pairs={{0,15},{1,0},{2,1},{3,2},{4,3},{5,4},{6,5},{7,6},{8,7},{9,8},{10,9... | collective-permute-start | bytes 393224 | tf_op jit(solution)/shard_map/ppermute | solution.py:389
  5.3 3.5 %collective-permute-start.6 = (f32[9,4,16,128]{3,2,1,0:T(8,128)S(1)}, f32[9,4,16,128]{3,2,1,0:T(8,128)S(1)}, u32[]{:S(2)}, u32[]{:S(2)}) collective-permute-start(f32[9,4,16,128]{3,2,1,0:T(8,128)S(1)} %bitcast.4), channel_id=1, source_target_pairs={{0,15},{1,0},{2,1},{3,2},{4,3},{5,4},{6,5},{7,6},{8,7},{9,8},{10,9... | collective-permute-start | bytes 884744 | tf_op jit(solution)/shard_map/ppermute | solution.py:389
  8.9 3.0 %collective-permute-start.2 = (f32[3,4,16,128]{3,2,1,0:T(8,128)S(1)}, f32[3,4,16,128]{3,2,1,0:T(8,128)S(1)}, u32[]{:S(2)}, u32[]{:S(2)}) collective-permute-start(f32[3,4,16,128]{3,2,1,0:T(8,128)S(1)} %broadcast_select_fusion.own), channel_id=1, source_target_pairs={{0,15},{1,0},{2,1},{3,2},{4,3},{5,4},{6,5},{7,6},{8,7},{9,8},{10,9... | collective-permute-start | bytes 294920 | tf_op jit(solution)/shard_map/ppermute | solution.py:389
  13.0 2.5 %collective-permute-done.1.low = f32[3,4,16,128]{3,2,1,0:T(8,128)S(1)} collective-permute-done((f32[3,4,16,128]{3,2,1,0:T(8,128)S(1)}, f32[3,4,16,128]{3,2,1,0:T(8,128)S(1)}, u32[]{:S(2)}, u32[]{:S(2)}) %collective-permute-start.1) | collective-permute-done | bytes 98336 | tf_op jit(solution)/shard_map/ppermute | solution.py:389
  16.9 4.6 %collective-permute-start.10 = (f32[3,6,16,128]{3,2,1,0:T(8,128)S(1)}, f32[3,6,16,128]{3,2,1,0:T(8,128)S(1)}, u32[]{:S(2)}, u32[]{:S(2)}) collective-permute-start(f32[3,6,16,128]{3,2,1,0:T(8,128)S(1)} %get-tuple-element.62), channel_id=1, source_target_pairs={{0,15},{1,0},{2,1},{3,2},{4,3},{5,4},{6,5},{7,6},{8,7},{9,8},{10,9... | collective-permute-start | bytes 442376 | tf_op jit(solution)/shard_map/ppermute | solution.py:389
  26.2 1.7 %collective-permute-start.12 = (f32[3,6,16,128]{3,2,1,0:T(8,128)S(1)}, f32[3,6,16,128]{3,2,1,0:T(8,128)S(1)}, u32[]{:S(2)}, u32[]{:S(2)}) collective-permute-start(f32[3,6,16,128]{3,2,1,0:T(8,128)S(1)} %get-tuple-element.65), channel_id=1, source_target_pairs={{0,15},{1,0},{2,1},{3,2},{4,3},{5,4},{6,5},{7,6},{8,7},{9,8},{10,9... | collective-permute-start | bytes 442376 | tf_op jit(solution)/shard_map/ppermute | solution.py:389
  27.9 5.0 %collective-permute-done.12.high = f32[3,6,16,128]{3,2,1,0:T(8,128)S(1)} collective-permute-done((f32[3,6,16,128]{3,2,1,0:T(8,128)S(1)}, f32[3,6,16,128]{3,2,1,0:T(8,128)S(1)}, u32[]{:S(2)}, u32[]{:S(2)}) %collective-permute-start.12) | collective-permute-done | bytes 147488 | tf_op jit(solution)/shard_map/ppermute | solution.py:389
  33.3 2.0 %collective-permute-start.13 = (f32[3,8,16,128]{3,2,1,0:T(8,128)S(1)}, f32[3,8,16,128]{3,2,1,0:T(8,128)S(1)}, u32[]{:S(2)}, u32[]{:S(2)}) collective-permute-start(f32[3,8,16,128]{3,2,1,0:T(8,128)S(1)} %get-tuple-element.74.term), channel_id=1, source_target_pairs={{0,240},{1,241},{2,242},{3,243},{4,244},{5,245},{6,246},{7,247},{8... | collective-permute-start | bytes 589832 | tf_op jit(solution)/shard_map/ppermute | solution.py:389
  35.3 4.2 %collective-permute-start.14 = (f32[3,4,16,128]{3,2,1,0:T(8,128)S(1)}, f32[3,4,16,128]{3,2,1,0:T(8,128)S(1)}, u32[]{:S(2)}, u32[]{:S(2)}) collective-permute-start(f32[3,4,16,128]{3,2,1,0:T(8,128)S(1)} %get-tuple-element.75), channel_id=1, source_target_pairs={{0,1},{1,0},{2,3},{3,2},{4,5},{5,4},{6,7},{7,6},{8,9},{9,8},{10,11... | collective-permute-start | bytes 294920 | tf_op jit(solution)/shard_map/ppermute | solution.py:389
  39.5 2.9 %collective-permute-done.14.term_two = f32[3,4,16,128]{3,2,1,0:T(8,128)S(1)} collective-permute-done((f32[3,4,16,128]{3,2,1,0:T(8,128)S(1)}, f32[3,4,16,128]{3,2,1,0:T(8,128)S(1)}, u32[]{:S(2)}, u32[]{:S(2)}) %collective-permute-start.14) | collective-permute-done | bytes 98336 | tf_op jit(solution)/shard_map/ppermute | solution.py:389
  42.9 5.4 %collective-permute-start.16 = (f32[3,4,16,128]{3,2,1,0:T(8,128)S(1)}, f32[3,4,16,128]{3,2,1,0:T(8,128)S(1)}, u32[]{:S(2)}, u32[]{:S(2)}) collective-permute-start(f32[3,4,16,128]{3,2,1,0:T(8,128)S(1)} %get-tuple-element.71.own), channel_id=1, source_target_pairs={{0,1},{1,0},{2,3},{3,2},{4,5},{5,4},{6,7},{7,6},{8,9},{9,8},{10,11... | collective-permute-start | bytes 294920 | tf_op jit(solution)/shard_map/ppermute | solution.py:389
  48.4 5.6 %collective-permute-start.25 = (f32[3,8,16,128]{3,2,1,0:T(8,128)S(1)}, f32[3,8,16,128]{3,2,1,0:T(8,128)S(1)}, u32[]{:S(2)}, u32[]{:S(2)}) collective-permute-start(f32[3,8,16,128]{3,2,1,0:T(8,128)S(1)} %get-tuple-element.78), channel_id=1, source_target_pairs={{0,1},{1,0},{2,3},{3,2},{4,5},{5,4},{6,7},{7,6},{8,9},{9,8},{10,11... | collective-permute-start | bytes 589832 | tf_op jit(solution)/shard_map/ppermute | solution.py:389
  56.8 1.8 %collective-permute-done.20.high = f32[3,4,16,128]{3,2,1,0:T(8,128)S(1)} collective-permute-done((f32[3,4,16,128]{3,2,1,0:T(8,128)S(1)}, f32[3,4,16,128]{3,2,1,0:T(8,128)S(1)}, u32[]{:S(2)}, u32[]{:S(2)}) %collective-permute-start.20) | collective-permute-done | bytes 98336 | tf_op jit(solution)/shard_map/ppermute | solution.py:389
  59.2 3.5 %collective-permute-start.24 = (f32[3,4,16,128]{3,2,1,0:T(8,128)S(1)}, f32[3,4,16,128]{3,2,1,0:T(8,128)S(1)}, u32[]{:S(2)}, u32[]{:S(2)}) collective-permute-start(f32[3,4,16,128]{3,2,1,0:T(8,128)S(1)} %get-tuple-element.77.own), channel_id=1, source_target_pairs={{0,1},{1,0},{2,3},{3,2},{4,5},{5,4},{6,7},{7,6},{8,9},{9,8},{10,11... | collective-permute-start | bytes 294920 | tf_op jit(solution)/shard_map/ppermute | solution.py:389
  64.9 4.0 %collective-permute-start.28 = (f32[3,4,16,128]{3,2,1,0:T(8,128)S(1)}, f32[3,4,16,128]{3,2,1,0:T(8,128)S(1)}, u32[]{:S(2)}, u32[]{:S(2)}) collective-permute-start(f32[3,4,16,128]{3,2,1,0:T(8,128)S(1)} %get-tuple-element.81.own), channel_id=1, source_target_pairs={{0,1},{1,0},{2,3},{3,2},{4,5},{5,4},{6,7},{7,6},{8,9},{9,8},{10,11... | collective-permute-start | bytes 294920 | tf_op jit(solution)/shard_map/ppermute | solution.py:389
  71.0 4.9 %collective-permute-start.32 = (f32[3,4,16,128]{3,2,1,0:T(8,128)S(1)}, f32[3,4,16,128]{3,2,1,0:T(8,128)S(1)}, u32[]{:S(2)}, u32[]{:S(2)}) collective-permute-start(f32[3,4,16,128]{3,2,1,0:T(8,128)S(1)} %get-tuple-element.83.own), channel_id=1, source_target_pairs={{0,1},{1,0},{2,3},{3,2},{4,5},{5,4},{6,7},{7,6},{8,9},{9,8},{10,11... | collective-permute-start | bytes 294920 | tf_op jit(solution)/shard_map/ppermute | solution.py:389
  78.1 3.8 %collective-permute-start.36 = (f32[3,4,16,128]{3,2,1,0:T(8,128)S(1)}, f32[3,4,16,128]{3,2,1,0:T(8,128)S(1)}, u32[]{:S(2)}, u32[]{:S(2)}) collective-permute-start(f32[3,4,16,128]{3,2,1,0:T(8,128)S(1)} %get-tuple-element.87.own), channel_id=1, source_target_pairs={{0,1},{1,0},{2,3},{3,2},{4,5},{5,4},{6,7},{7,6},{8,9},{9,8},{10,11... | collective-permute-start | bytes 294920 | tf_op jit(solution)/shard_map/ppermute | solution.py:389
  85.0 3.8 %collective-permute-done.35.low = f32[3,4,16,128]{3,2,1,0:T(8,128)S(1)} collective-permute-done((f32[3,4,16,128]{3,2,1,0:T(8,128)S(1)}, f32[3,4,16,128]{3,2,1,0:T(8,128)S(1)}, u32[]{:S(2)}, u32[]{:S(2)}) %collective-permute-start.35) | collective-permute-done | bytes 98336 | tf_op jit(solution)/shard_map/ppermute | solution.py:389
  90.8 6.6 %collective-permute-start.40 = (f32[3,4,16,128]{3,2,1,0:T(8,128)S(1)}, f32[3,4,16,128]{3,2,1,0:T(8,128)S(1)}, u32[]{:S(2)}, u32[]{:S(2)}) collective-permute-start(f32[3,4,16,128]{3,2,1,0:T(8,128)S(1)} %get-tuple-element.91.own), channel_id=1, source_target_pairs={{0,1},{1,0},{2,3},{3,2},{4,5},{5,4},{6,7},{7,6},{8,9},{9,8},{10,11... | collective-permute-start | bytes 294920 | tf_op jit(solution)/shard_map/ppermute | solution.py:389
  97.4 4.8 %collective-permute-start.56 = (f32[7,4,16,128]{3,2,1,0:T(8,128)S(1)}, f32[7,4,16,128]{3,2,1,0:T(8,128)S(1)}, u32[]{:S(2)}, u32[]{:S(2)}) collective-permute-start(f32[7,4,16,128]{3,2,1,0:T(8,128)S(1)} %get-tuple-element.102), channel_id=1, source_target_pairs={{0,14},{1,15},{2,0},{3,1},{4,2},{5,3},{6,4},{7,5},{8,6},{9,7},{10,... | collective-permute-start | bytes 688136 | tf_op jit(solution)/shard_map/ppermute | solution.py:389
  102.4 1.7 %collective-permute-start.53 = (f32[3,4,16,128]{3,2,1,0:T(8,128)S(1)}, f32[3,4,16,128]{3,2,1,0:T(8,128)S(1)}, u32[]{:S(2)}, u32[]{:S(2)}) collective-permute-start(f32[3,4,16,128]{3,2,1,0:T(8,128)S(1)} %shard_map.59.own), channel_id=1, source_target_pairs={{0,14},{1,15},{2,0},{3,1},{4,2},{5,3},{6,4},{7,5},{8,6},{9,7},{10,... | collective-permute-start | bytes 294920 | tf_op jit(solution)/shard_map/ppermute | solution.py:389
  107.1 5.2 %collective-permute-start.54 = (f32[3,1,16,128]{3,2,1,0:T(8,128)S(1)}, f32[3,1,16,128]{3,2,1,0:T(8,128)S(1)}, u32[]{:S(2)}, u32[]{:S(2)}) collective-permute-start(f32[3,1,16,128]{3,2,1,0:T(8,128)S(1)} %get-tuple-element.103), channel_id=1, source_target_pairs={{0,13},{1,14},{2,15},{3,0},{4,1},{5,2},{6,3},{7,4},{8,5},{9,6},{10... | collective-permute-start | bytes 73736 | tf_op jit(solution)/shard_map/ppermute | solution.py:389
  113.3 4.9 %collective-permute-done.49.lowest = f32[3,1,16,128]{3,2,1,0:T(8,128)S(1)} collective-permute-done((f32[3,1,16,128]{3,2,1,0:T(8,128)S(1)}, f32[3,1,16,128]{3,2,1,0:T(8,128)S(1)}, u32[]{:S(2)}, u32[]{:S(2)}) %collective-permute-start.49) | collective-permute-done | bytes 24608 | tf_op jit(solution)/shard_map/ppermute | solution.py:389
  118.3 4.3 %finish.1 = f32[16,3,4,16,128]{4,3,2,1,0:T(8,128)} custom-call(f32[3,1,16,128]{3,2,1,0:T(8,128)S(1)} %collective-permute-done.49.lowest, f32[3,4,16,128]{3,2,1,0:T(8,128)S(1)} %collective-permute-done.50.lower, f32[3,4,16,128]{3,2,1,0:T(8,128)S(1)} %collective-permute-done.51.low, f32[3,4,16,128]{3,2,1,0:T(8,128)S(1)} %shard_map.59.own, ...), custom_call_target="tpu_custom_call" | custom-call | flops 20000000 | bytes 4000000 | tf_op jit(solution)/shard_map/finish/pallas_call | solution.py:429
  (113 shorter events, 30.1 us)
Async XLA Ops:
  1.8 10.0 %collective-permute-start.4 = (f32[4,4,16,128]{3,2,1,0:T(8,128)S(1)}, f32[4,4,16,128]{3,2,1,0:T(8,128)S(1)}, u32[]{:S(2)}, u32[]{:S(2)}) collective-permute-start(f32[4,4,16,128]{3,2,1,0:T(8,128)S(1)} %pad_maximum_fusion.own.fields), channel_id=1, source_target_pairs={{0,15},{1,0},{2,1},{3,2},{4,3},{5,4},{6,5},{7,6},{8,7},{9,8},{10,9... | collective-permute-start | bytes 393224 | tf_op jit(solution)/shard_map/ppermute | solution.py:389
  5.3 10.2 %collective-permute-start.6 = (f32[9,4,16,128]{3,2,1,0:T(8,128)S(1)}, f32[9,4,16,128]{3,2,1,0:T(8,128)S(1)}, u32[]{:S(2)}, u32[]{:S(2)}) collective-permute-start(f32[9,4,16,128]{3,2,1,0:T(8,128)S(1)} %bitcast.4), channel_id=1, source_target_pairs={{0,15},{1,0},{2,1},{3,2},{4,3},{5,4},{6,5},{7,6},{8,7},{9,8},{10,9... | collective-permute-start | bytes 884744 | tf_op jit(solution)/shard_map/ppermute | solution.py:389
  16.9 8.7 %collective-permute-start.10 = (f32[3,6,16,128]{3,2,1,0:T(8,128)S(1)}, f32[3,6,16,128]{3,2,1,0:T(8,128)S(1)}, u32[]{:S(2)}, u32[]{:S(2)}) collective-permute-start(f32[3,6,16,128]{3,2,1,0:T(8,128)S(1)} %get-tuple-element.62), channel_id=1, source_target_pairs={{0,15},{1,0},{2,1},{3,2},{4,3},{5,4},{6,5},{7,6},{8,7},{9,8},{10,9... | collective-permute-start | bytes 442376 | tf_op jit(solution)/shard_map/ppermute | solution.py:389
  23.9 18.5 %collective-permute-start.8 = (f32[12,4,16,128]{3,2,1,0:T(8,128)S(1)}, f32[12,4,16,128]{3,2,1,0:T(8,128)S(1)}, u32[]{:S(2)}, u32[]{:S(2)}) collective-permute-start(f32[12,4,16,128]{3,2,1,0:T(8,128)S(1)} %get-tuple-element.61.own.late), channel_id=1, source_target_pairs={{0,15},{1,0},{2,1},{3,2},{4,3},{5,4},{6,5},{7,6},{8,7},{9,8},{10,9... | collective-permute-start | bytes 1179656 | tf_op jit(solution)/shard_map/ppermute | solution.py:389
  24.4 18.0 %collective-permute-start.7 = (f32[12,4,16,128]{3,2,1,0:T(8,128)S(1)}, f32[12,4,16,128]{3,2,1,0:T(8,128)S(1)}, u32[]{:S(2)}, u32[]{:S(2)}) collective-permute-start(f32[12,4,16,128]{3,2,1,0:T(8,128)S(1)} %get-tuple-element.61.own.late), channel_id=1, source_target_pairs={{0,1},{1,2},{2,3},{3,4},{4,5},{5,6},{6,7},{7,8},{8,9},{9,10},{10,1... | collective-permute-start | bytes 1179656 | tf_op jit(solution)/shard_map/ppermute | solution.py:389
  33.3 9.0 %collective-permute-start.13 = (f32[3,8,16,128]{3,2,1,0:T(8,128)S(1)}, f32[3,8,16,128]{3,2,1,0:T(8,128)S(1)}, u32[]{:S(2)}, u32[]{:S(2)}) collective-permute-start(f32[3,8,16,128]{3,2,1,0:T(8,128)S(1)} %get-tuple-element.74.term), channel_id=1, source_target_pairs={{0,240},{1,241},{2,242},{3,243},{4,244},{5,245},{6,246},{7,247},{8... | collective-permute-start | bytes 589832 | tf_op jit(solution)/shard_map/ppermute | solution.py:389
  39.5 8.9 %collective-permute-start.17 = (f32[3,8,16,128]{3,2,1,0:T(8,128)S(1)}, f32[3,8,16,128]{3,2,1,0:T(8,128)S(1)}, u32[]{:S(2)}, u32[]{:S(2)}) collective-permute-start(f32[3,8,16,128]{3,2,1,0:T(8,128)S(1)} %get-tuple-element.74.term), channel_id=1, source_target_pairs={{0,1},{1,0},{2,3},{3,2},{4,5},{5,4},{6,7},{7,6},{8,9},{9,8},{10,11... | collective-permute-start | bytes 589832 | tf_op jit(solution)/shard_map/ppermute | solution.py:389
  42.4 14.4 %collective-permute-start.21 = (f32[3,8,16,128]{3,2,1,0:T(8,128)S(1)}, f32[3,8,16,128]{3,2,1,0:T(8,128)S(1)}, u32[]{:S(2)}, u32[]{:S(2)}) collective-permute-start(f32[3,8,16,128]{3,2,1,0:T(8,128)S(1)} %get-tuple-element.74.term), channel_id=1, source_target_pairs={{0,1},{1,0},{2,3},{3,2},{4,5},{5,4},{6,7},{7,6},{8,9},{9,8},{10,11... | collective-permute-start | bytes 589832 | tf_op jit(solution)/shard_map/ppermute | solution.py:389
  42.9 11.0 %collective-permute-start.16 = (f32[3,4,16,128]{3,2,1,0:T(8,128)S(1)}, f32[3,4,16,128]{3,2,1,0:T(8,128)S(1)}, u32[]{:S(2)}, u32[]{:S(2)}) collective-permute-start(f32[3,4,16,128]{3,2,1,0:T(8,128)S(1)} %get-tuple-element.71.own), channel_id=1, source_target_pairs={{0,1},{1,0},{2,3},{3,2},{4,5},{5,4},{6,7},{7,6},{8,9},{9,8},{10,11... | collective-permute-start | bytes 294920 | tf_op jit(solution)/shard_map/ppermute | solution.py:389
  48.4 8.4 %collective-permute-start.22 = (f32[3,4,16,128]{3,2,1,0:T(8,128)S(1)}, f32[3,4,16,128]{3,2,1,0:T(8,128)S(1)}, u32[]{:S(2)}, u32[]{:S(2)}) collective-permute-start(f32[3,4,16,128]{3,2,1,0:T(8,128)S(1)} %get-tuple-element.75), channel_id=1, source_target_pairs={{0,1},{1,0},{2,3},{3,2},{4,5},{5,4},{6,7},{7,6},{8,9},{9,8},{10,11... | collective-permute-start | bytes 294920 | tf_op jit(solution)/shard_map/ppermute | solution.py:389
  48.4 14.4 %collective-permute-start.25 = (f32[3,8,16,128]{3,2,1,0:T(8,128)S(1)}, f32[3,8,16,128]{3,2,1,0:T(8,128)S(1)}, u32[]{:S(2)}, u32[]{:S(2)}) collective-permute-start(f32[3,8,16,128]{3,2,1,0:T(8,128)S(1)} %get-tuple-element.78), channel_id=1, source_target_pairs={{0,1},{1,0},{2,3},{3,2},{4,5},{5,4},{6,7},{7,6},{8,9},{9,8},{10,11... | collective-permute-start | bytes 589832 | tf_op jit(solution)/shard_map/ppermute | solution.py:389
  56.8 13.2 %collective-permute-start.29 = (f32[3,8,16,128]{3,2,1,0:T(8,128)S(1)}, f32[3,8,16,128]{3,2,1,0:T(8,128)S(1)}, u32[]{:S(2)}, u32[]{:S(2)}) collective-permute-start(f32[3,8,16,128]{3,2,1,0:T(8,128)S(1)} %get-tuple-element.78), channel_id=1, source_target_pairs={{0,1},{1,0},{2,3},{3,2},{4,5},{5,4},{6,7},{7,6},{8,9},{9,8},{10,11... | collective-permute-start | bytes 589832 | tf_op jit(solution)/shard_map/ppermute | solution.py:389
  62.7 13.2 %collective-permute-start.33 = (f32[3,8,16,128]{3,2,1,0:T(8,128)S(1)}, f32[3,8,16,128]{3,2,1,0:T(8,128)S(1)}, u32[]{:S(2)}, u32[]{:S(2)}) collective-permute-start(f32[3,8,16,128]{3,2,1,0:T(8,128)S(1)} %get-tuple-element.84), channel_id=1, source_target_pairs={{0,1},{1,0},{2,3},{3,2},{4,5},{5,4},{6,7},{7,6},{8,9},{9,8},{10,11... | collective-permute-start | bytes 589832 | tf_op jit(solution)/shard_map/ppermute | solution.py:389
  70.0 14.4 %collective-permute-start.37 = (f32[3,8,16,128]{3,2,1,0:T(8,128)S(1)}, f32[3,8,16,128]{3,2,1,0:T(8,128)S(1)}, u32[]{:S(2)}, u32[]{:S(2)}) collective-permute-start(f32[3,8,16,128]{3,2,1,0:T(8,128)S(1)} %get-tuple-element.88), channel_id=1, source_target_pairs={{0,1},{1,0},{2,3},{3,2},{4,5},{5,4},{6,7},{7,6},{8,9},{9,8},{10,11... | collective-permute-start | bytes 589832 | tf_op jit(solution)/shard_map/ppermute | solution.py:389
  76.0 8.9 %collective-permute-start.41 = (f32[3,8,16,128]{3,2,1,0:T(8,128)S(1)}, f32[3,8,16,128]{3,2,1,0:T(8,128)S(1)}, u32[]{:S(2)}, u32[]{:S(2)}) collective-permute-start(f32[3,8,16,128]{3,2,1,0:T(8,128)S(1)} %get-tuple-element.92), channel_id=1, source_target_pairs={{0,1},{1,0},{2,3},{3,2},{4,5},{5,4},{6,7},{7,6},{8,9},{9,8},{10,11... | collective-permute-start | bytes 589832 | tf_op jit(solution)/shard_map/ppermute | solution.py:389
  84.4 22.4 %collective-permute-start.55 = (f32[7,4,16,128]{3,2,1,0:T(8,128)S(1)}, f32[7,4,16,128]{3,2,1,0:T(8,128)S(1)}, u32[]{:S(2)}, u32[]{:S(2)}) collective-permute-start(f32[7,4,16,128]{3,2,1,0:T(8,128)S(1)} %get-tuple-element.101), channel_id=1, source_target_pairs={{0,2},{1,3},{2,4},{3,5},{4,6},{5,7},{6,8},{7,9},{8,10},{9,11},{10,... | collective-permute-start | bytes 688136 | tf_op jit(solution)/shard_map/ppermute | solution.py:389
  88.8 8.6 %collective-permute-start.46 = (f32[3,4,16,128]{3,2,1,0:T(8,128)S(1)}, f32[3,4,16,128]{3,2,1,0:T(8,128)S(1)}, u32[]{:S(2)}, u32[]{:S(2)}) collective-permute-start(f32[3,4,16,128]{3,2,1,0:T(8,128)S(1)} %get-tuple-element.98), channel_id=1, source_target_pairs={{0,1},{1,0},{2,3},{3,2},{4,5},{5,4},{6,7},{7,6},{8,9},{9,8},{10,11... | collective-permute-start | bytes 294920 | tf_op jit(solution)/shard_map/ppermute | solution.py:389
  90.8 11.3 %collective-permute-start.48 = (f32[3,4,16,128]{3,2,1,0:T(8,128)S(1)}, f32[3,4,16,128]{3,2,1,0:T(8,128)S(1)}, u32[]{:S(2)}, u32[]{:S(2)}) collective-permute-start(f32[3,4,16,128]{3,2,1,0:T(8,128)S(1)} %get-tuple-element.100), channel_id=1, source_target_pairs={{0,1},{1,0},{2,3},{3,2},{4,5},{5,4},{6,7},{7,6},{8,9},{9,8},{10,11... | collective-permute-start | bytes 294920 | tf_op jit(solution)/shard_map/ppermute | solution.py:389
  90.8 11.3 %collective-permute-start.40 = (f32[3,4,16,128]{3,2,1,0:T(8,128)S(1)}, f32[3,4,16,128]{3,2,1,0:T(8,128)S(1)}, u32[]{:S(2)}, u32[]{:S(2)}) collective-permute-start(f32[3,4,16,128]{3,2,1,0:T(8,128)S(1)} %get-tuple-element.91.own), channel_id=1, source_target_pairs={{0,1},{1,0},{2,3},{3,2},{4,5},{5,4},{6,7},{7,6},{8,9},{9,8},{10,11... | collective-permute-start | bytes 294920 | tf_op jit(solution)/shard_map/ppermute | solution.py:389
  97.4 9.8 %collective-permute-start.56 = (f32[7,4,16,128]{3,2,1,0:T(8,128)S(1)}, f32[7,4,16,128]{3,2,1,0:T(8,128)S(1)}, u32[]{:S(2)}, u32[]{:S(2)}) collective-permute-start(f32[7,4,16,128]{3,2,1,0:T(8,128)S(1)} %get-tuple-element.102), channel_id=1, source_target_pairs={{0,14},{1,15},{2,0},{3,1},{4,2},{5,3},{6,4},{7,5},{8,6},{9,7},{10,... | collective-permute-start | bytes 688136 | tf_op jit(solution)/shard_map/ppermute | solution.py:389
  102.4 15.9 %collective-permute-start.53 = (f32[3,4,16,128]{3,2,1,0:T(8,128)S(1)}, f32[3,4,16,128]{3,2,1,0:T(8,128)S(1)}, u32[]{:S(2)}, u32[]{:S(2)}) collective-permute-start(f32[3,4,16,128]{3,2,1,0:T(8,128)S(1)} %shard_map.59.own), channel_id=1, source_target_pairs={{0,14},{1,15},{2,0},{3,1},{4,2},{5,3},{6,4},{7,5},{8,6},{9,7},{10,... | collective-permute-start | bytes 294920 | tf_op jit(solution)/shard_map/ppermute | solution.py:389
  104.1 14.2 %collective-permute-start.52 = (f32[3,4,16,128]{3,2,1,0:T(8,128)S(1)}, f32[3,4,16,128]{3,2,1,0:T(8,128)S(1)}, u32[]{:S(2)}, u32[]{:S(2)}) collective-permute-start(f32[3,4,16,128]{3,2,1,0:T(8,128)S(1)} %shard_map.59.own), channel_id=1, source_target_pairs={{0,15},{1,0},{2,1},{3,2},{4,3},{5,4},{6,5},{7,6},{8,7},{9,8},{10,9... | collective-permute-start | bytes 294920 | tf_op jit(solution)/shard_map/ppermute | solution.py:389
  105.2 13.1 %collective-permute-start.51 = (f32[3,4,16,128]{3,2,1,0:T(8,128)S(1)}, f32[3,4,16,128]{3,2,1,0:T(8,128)S(1)}, u32[]{:S(2)}, u32[]{:S(2)}) collective-permute-start(f32[3,4,16,128]{3,2,1,0:T(8,128)S(1)} %shard_map.59.own), channel_id=1, source_target_pairs={{0,1},{1,2},{2,3},{3,4},{4,5},{5,6},{6,7},{7,8},{8,9},{9,10},{10,1... | collective-permute-start | bytes 294920 | tf_op jit(solution)/shard_map/ppermute | solution.py:389
  106.8 11.5 %collective-permute-start.50 = (f32[3,4,16,128]{3,2,1,0:T(8,128)S(1)}, f32[3,4,16,128]{3,2,1,0:T(8,128)S(1)}, u32[]{:S(2)}, u32[]{:S(2)}) collective-permute-start(f32[3,4,16,128]{3,2,1,0:T(8,128)S(1)} %shard_map.59.own), channel_id=1, source_target_pairs={{0,2},{1,3},{2,4},{3,5},{4,6},{5,7},{6,8},{7,9},{8,10},{9,11},{10,... | collective-permute-start | bytes 294920 | tf_op jit(solution)/shard_map/ppermute | solution.py:389
  (34 other events, 185.9 us)

commit v4 on v3

--- a/solution.py
+++ b/solution.py
@@ -12,6 +12,9 @@
 FINE, MIDDLE, COARSE = time_step, 2.0 * time_step, 8.0 * time_step
 DEPTH = 4
 AXES = ("tm", "space")
+
+
+INITIAL = 4
 
 
 def slab(low, own, high, base=0):
@@ -159,7 +162,7 @@
 
 
 def remainder_kernel(
-    low, own, high, middle, coarse, next_one, others, first, initial, fields,
+    low, own, high, middle, coarse, next_one, others, first, fields,
     defect, rest, late, deep_up, deep_down, kept, one,
 ):
     start = slab(low, own, high)
@@ -168,7 +171,7 @@
     def subtract(c, z, value):
         value = first[c, z] - value
         defect[c, z] = value
-        late[3 + c, z] = value
+        late[c, z] = value
         if z > 0:
             deep_up[4 + c, z - 1] = value
         if z < 3:
@@ -183,10 +186,9 @@
     advance(reader(one), subtract_rest, 0, 4, coarse, COARSE)
     for c in range(3):
         for z in range(DEPTH):
-            late[c, z] = initial[c, z]
-            late[6 + c, z] = next_one[0, c, z]
-            late[9 + c, z] = others[0, c, z]
-            kept[c, z] = initial[c, z]
+            late[3 + c, z] = next_one[0, c, z]
+            late[6 + c, z] = others[0, c, z]
+            kept[c, z] = fields[INITIAL + c, z]
         deep_up[4 + c, 3] = next_one[0, c, 3]
         deep_down[4 + c, 3] = next_one[0, c, 0]
     for c in range(4):
@@ -244,7 +246,7 @@
 
 
 def march_kernel(
-    done, low, own, high, coarse, term_one, term_two, term, kept_in,
+    base, done, low, own, high, coarse, term_one, term_two, term, kept_in,
     state, message_one, message_two, kept, one, two,
 ):
     def first(c, z, value):
@@ -264,7 +266,7 @@
 
     @pl.when(marching)
     def _():
-        advance(slab(low, own, high), writer(one), -3, 7, coarse, COARSE)
+        advance(slab(low, own, high, base), writer(one), -3, 7, coarse, COARSE)
         advance(reader(one), first, -2, 6, coarse, COARSE)
         advance(reader(two), writer(one), -1, 5, coarse, COARSE)
         advance(reader(one), second, 0, 4, coarse, COARSE)
@@ -276,7 +278,8 @@
                 message_one[c, z] = term[c, z + 2 - edge]
             for z in range(DEPTH):
                 message_two[c, z] = term[c, z + 2]
-                state[c, z] = own[c, z]
+                state[c, z] = own[base + c, z]
+                kept[c, z] = kept_in[c, z]
 
     if done[0] is not None:
         pl.when(column == done[0])(functools.partial(take, kept, term_one))
@@ -315,7 +318,7 @@
         return pltpu.make_async_copy(rows.at[i], result.at[i], sem.at[i])
 
     start = deep_slab(lower, low, own, high, higher, lowest, highest)
-    near = slab(late_low, late, late_high, 3)
+    near = slab(late_low, late, late_high)
     for c in range(3):
         for z in range(-FINE_SHIFT, DEPTH + FINE_SHIFT):
             anchors[c, z + FINE_SHIFT] = start(c, z)
@@ -405,7 +408,7 @@
 VMEM_SPEC = pl.BlockSpec(memory_space=pltpu.VMEM)
 
 
-def call(kernel, shapes, inputs, works, units, aliases=None, more=()):
+def call(kernel, shapes, inputs, works, units, more=()):
     outs = [jax.ShapeDtypeStruct(tuple(shape) + PLANE, jnp.float32) for shape in shapes]
     result = pl.pallas_call(
         kernel,
@@ -413,7 +416,6 @@
         in_specs=[VMEM_SPEC] * len(inputs),
         out_specs=[VMEM_SPEC] * len(outs),
         scratch_shapes=[WORK] * works + [pltpu.VMEM(tuple(m) + PLANE, jnp.float32) for m in more],
-        input_output_aliases=aliases or {},
         compiler_params=pltpu.CompilerParams(vmem_limit_bytes=8 << 20),
         cost_estimate=pl.CostEstimate(flops=units * 120000, bytes_accessed=units * 60000, transcendentals=0),
     )(*inputs)
@@ -449,7 +451,7 @@
     members = guesses[:3].reshape((9,) + guesses.shape[2:])
     incoming = permute(last, {t: ((t + 1) % times, 0) for t in every})
     member_low, member_high = halos(members, members, every)
-    fields = jnp.concatenate([forcing, viscosity[None]], axis=0)
+    fields = jnp.concatenate([forcing, viscosity[None], initial], axis=0)
     field_low, field_high = halos(fields, fields, every)
     opening = jnp.where(column == 0, initial, incoming)
     open_low, open_high = halos(opening, opening, every)
@@ -469,8 +471,8 @@
     others = call(defects_kernel, [(2, 3, DEPTH)], inputs, 2, 76)
     _, rest, late, deep_up, deep_down, kept = call(
         remainder_kernel,
-        [(3, DEPTH)] * 2 + [(12, DEPTH)] + [(7, DEPTH)] * 2 + [(3, DEPTH)],
-        [open_low, opening, open_high, middle, coarse, defects, others, to_up, initial, fields],
+        [(3, DEPTH)] * 2 + [(9, DEPTH)] + [(7, DEPTH)] * 2 + [(3, DEPTH)],
+        [open_low, opening, open_high, middle, coarse, defects, others, to_up, fields],
         1,
         20,
     )
@@ -495,7 +497,7 @@
         terms[t] = cycle(ahead[t % 2], t, marcher)
     late_low, late_high = halos(late, late, every)
     deep_low, deep_high = halos(deep_up, deep_down, every, 2)
-    state, low, high = late, late_low, late_high
+    state, low, high = fields, field_low, field_high
     brought, extra = {}, {}
     messages = None
     for period in range(times // 2):
@@ -516,12 +518,11 @@
             pair = (2 * period, 2 * period + 1)
             wide = 8 if 2 * period + 8 < marcher else DEPTH
             state, *messages, kept = call(
-                functools.partial(march_kernel, [brought.get(t) for t in pair]),
+                functools.partial(march_kernel, 0 if period else INITIAL, [brought.get(t) for t in pair]),
                 [(3, DEPTH), (3, wide), (3, DEPTH), (3, DEPTH)],
                 [low, state, high, coarse, terms[pair[0]], terms[pair[1]], term, kept],
                 2,
                 28,
-                {7: 3},
             )
         else:
             start = call(

time: 123 us -> 121 us (0.984)
  the two profiles are of different devices: /device:TPU:31 before, /device:TPU:30 now
where the time goes in v4:
time: 121 us; the launch traced here: 120 us
  waiting for transfers between devices  71.5 us (59%)
  starting transfers between devices  32.8 us (27%)
  Pallas kernels  12.8 us (11%)
  local copies, waits for them, and re-layouts  1.88 us (2%)
    ppermute x57, waiting for transfers between devices, permute(): return lax.ppermute(x, AXES, pairs)  71.5 us
    ppermute x57, starting transfers between devices, permute(): return lax.ppermute(x, AXES, pairs)  32.8 us
    pallas_call x15, Pallas kernels, call(): pl.pallas_call(kernel, out_shape=outs, in_specs=[VMEM_SPEC] * len(inputs)...  8.59 us
    pallas_call x1, Pallas kernels, finish(): pl.pallas_call(finish_kernel, name='finish', out_shape=jax.ShapeDtypeStru...  4.26 us
  transfers between devices with their start and end apart: 57, of which 25 were waited for; matrix products, arithmetic and copies ran while one was open for 2% of the time, Pallas kernels for 5%

profile of v4, /device:TPU:30, one launch (start us, length us, event | category | flops | bytes accessed | tf_op | source)
XLA Modules:
  0.0 120.5 jit_solution(13262454652367977017)
XLA Ops:
  3.7 3.5 %collective-permute-start.1 = (f32[7,4,16,128]{3,2,1,0:T(8,128)S(1)}, f32[7,4,16,128]{3,2,1,0:T(8,128)S(1)}, u32[]{:S(2)}, u32[]{:S(2)}) collective-permute-start(f32[7,4,16,128]{3,2,1,0:T(8,128)S(1)} %pad_maximum_fusion.own.fields), channel_id=1, source_target_pairs={{0,15},{1,0},{2,1},{3,2},{4,3},{5,4},{6,5},{7,6},{8,7},{9,8},{10,9... | collective-permute-start | bytes 688136 | tf_op jit(solution)/shard_map/ppermute | solution.py:392
  8.2 3.0 %collective-permute-start.3 = (f32[9,4,16,128]{3,2,1,0:T(8,128)S(1)}, f32[9,4,16,128]{3,2,1,0:T(8,128)S(1)}, u32[]{:S(2)}, u32[]{:S(2)}) collective-permute-start(f32[9,4,16,128]{3,2,1,0:T(8,128)S(1)} %bitcast.4), channel_id=1, source_target_pairs={{0,15},{1,0},{2,1},{3,2},{4,3},{5,4},{6,5},{7,6},{8,7},{9,8},{10,9... | collective-permute-start | bytes 884744 | tf_op jit(solution)/shard_map/ppermute | solution.py:392
  11.2 3.0 %collective-permute-start.6 = (f32[3,4,16,128]{3,2,1,0:T(8,128)S(1)}, f32[3,4,16,128]{3,2,1,0:T(8,128)S(1)}, u32[]{:S(2)}, u32[]{:S(2)}) collective-permute-start(f32[3,4,16,128]{3,2,1,0:T(8,128)S(1)} %broadcast_select_fusion.own), channel_id=1, source_target_pairs={{0,15},{1,0},{2,1},{3,2},{4,3},{5,4},{6,5},{7,6},{8,7},{9,8},{10,9... | collective-permute-start | bytes 294920 | tf_op jit(solution)/shard_map/ppermute | solution.py:392
  14.3 2.2 %collective-permute-done.6.high = f32[3,4,16,128]{3,2,1,0:T(8,128)S(1)} collective-permute-done((f32[3,4,16,128]{3,2,1,0:T(8,128)S(1)}, f32[3,4,16,128]{3,2,1,0:T(8,128)S(1)}, u32[]{:S(2)}, u32[]{:S(2)}) %collective-permute-start.6) | collective-permute-done | bytes 98336 | tf_op jit(solution)/shard_map/ppermute | solution.py:392
  16.5 3.1 %collective-permute-done.5.low = f32[3,4,16,128]{3,2,1,0:T(8,128)S(1)} collective-permute-done((f32[3,4,16,128]{3,2,1,0:T(8,128)S(1)}, f32[3,4,16,128]{3,2,1,0:T(8,128)S(1)}, u32[]{:S(2)}, u32[]{:S(2)}) %collective-permute-start.5) | collective-permute-done | bytes 98336 | tf_op jit(solution)/shard_map/ppermute | solution.py:392
  23.8 2.9 %collective-permute-done.7.low = f32[3,6,16,128]{3,2,1,0:T(8,128)S(1)} collective-permute-done((f32[3,6,16,128]{3,2,1,0:T(8,128)S(1)}, f32[3,6,16,128]{3,2,1,0:T(8,128)S(1)}, u32[]{:S(2)}, u32[]{:S(2)}) %collective-permute-start.7) | collective-permute-done | bytes 147488 | tf_op jit(solution)/shard_map/ppermute | solution.py:392
  27.7 2.2 %collective-permute-done.10.high = f32[3,6,16,128]{3,2,1,0:T(8,128)S(1)} collective-permute-done((f32[3,6,16,128]{3,2,1,0:T(8,128)S(1)}, f32[3,6,16,128]{3,2,1,0:T(8,128)S(1)}, u32[]{:S(2)}, u32[]{:S(2)}) %collective-permute-start.10) | collective-permute-done | bytes 147488 | tf_op jit(solution)/shard_map/ppermute | solution.py:392
  29.9 3.1 %collective-permute-done.9.low = f32[3,6,16,128]{3,2,1,0:T(8,128)S(1)} collective-permute-done((f32[3,6,16,128]{3,2,1,0:T(8,128)S(1)}, f32[3,6,16,128]{3,2,1,0:T(8,128)S(1)}, u32[]{:S(2)}, u32[]{:S(2)}) %collective-permute-start.9) | collective-permute-done | bytes 147488 | tf_op jit(solution)/shard_map/ppermute | solution.py:392
  33.4 2.2 %collective-permute-start.11 = (f32[3,8,16,128]{3,2,1,0:T(8,128)S(1)}, f32[3,8,16,128]{3,2,1,0:T(8,128)S(1)}, u32[]{:S(2)}, u32[]{:S(2)}) collective-permute-start(f32[3,8,16,128]{3,2,1,0:T(8,128)S(1)} %get-tuple-element.73.term), channel_id=1, source_target_pairs={{0,240},{1,241},{2,242},{3,243},{4,244},{5,245},{6,246},{7,247},{8... | collective-permute-start | bytes 589832 | tf_op jit(solution)/shard_map/ppermute | solution.py:392
  36.4 8.8 %collective-permute-done.12.term_two = f32[3,4,16,128]{3,2,1,0:T(8,128)S(1)} collective-permute-done((f32[3,4,16,128]{3,2,1,0:T(8,128)S(1)}, f32[3,4,16,128]{3,2,1,0:T(8,128)S(1)}, u32[]{:S(2)}, u32[]{:S(2)}) %collective-permute-start.12) | collective-permute-done | bytes 98336 | tf_op jit(solution)/shard_map/ppermute | solution.py:392
  46.4 6.1 %collective-permute-start.23 = (f32[3,8,16,128]{3,2,1,0:T(8,128)S(1)}, f32[3,8,16,128]{3,2,1,0:T(8,128)S(1)}, u32[]{:S(2)}, u32[]{:S(2)}) collective-permute-start(f32[3,8,16,128]{3,2,1,0:T(8,128)S(1)} %get-tuple-element.77), channel_id=1, source_target_pairs={{0,1},{1,0},{2,3},{3,2},{4,5},{5,4},{6,7},{7,6},{8,9},{9,8},{10,11... | collective-permute-start | bytes 589832 | tf_op jit(solution)/shard_map/ppermute | solution.py:392
  53.6 4.0 %collective-permute-done.20.term_two = f32[3,4,16,128]{3,2,1,0:T(8,128)S(1)} collective-permute-done((f32[3,4,16,128]{3,2,1,0:T(8,128)S(1)}, f32[3,4,16,128]{3,2,1,0:T(8,128)S(1)}, u32[]{:S(2)}, u32[]{:S(2)}) %collective-permute-start.20) | collective-permute-done | bytes 98336 | tf_op jit(solution)/shard_map/ppermute | solution.py:392
  60.0 3.7 %collective-permute-done.24.term_two = f32[3,4,16,128]{3,2,1,0:T(8,128)S(1)} collective-permute-done((f32[3,4,16,128]{3,2,1,0:T(8,128)S(1)}, f32[3,4,16,128]{3,2,1,0:T(8,128)S(1)}, u32[]{:S(2)}, u32[]{:S(2)}) %collective-permute-start.24) | collective-permute-done | bytes 98336 | tf_op jit(solution)/shard_map/ppermute | solution.py:392
  66.4 4.4 %collective-permute-done.28.term_two = f32[3,4,16,128]{3,2,1,0:T(8,128)S(1)} collective-permute-done((f32[3,4,16,128]{3,2,1,0:T(8,128)S(1)}, f32[3,4,16,128]{3,2,1,0:T(8,128)S(1)}, u32[]{:S(2)}, u32[]{:S(2)}) %collective-permute-start.28) | collective-permute-done | bytes 98336 | tf_op jit(solution)/shard_map/ppermute | solution.py:392
  71.9 3.4 %collective-permute-done.32.term_two = f32[3,4,16,128]{3,2,1,0:T(8,128)S(1)} collective-permute-done((f32[3,4,16,128]{3,2,1,0:T(8,128)S(1)}, f32[3,4,16,128]{3,2,1,0:T(8,128)S(1)}, u32[]{:S(2)}, u32[]{:S(2)}) %collective-permute-start.32) | collective-permute-done | bytes 98336 | tf_op jit(solution)/shard_map/ppermute | solution.py:392
  75.5 5.1 %collective-permute-done.29.low = f32[3,4,16,128]{3,2,1,0:T(8,128)S(1)} collective-permute-done((f32[3,4,16,128]{3,2,1,0:T(8,128)S(1)}, f32[3,4,16,128]{3,2,1,0:T(8,128)S(1)}, u32[]{:S(2)}, u32[]{:S(2)}) %collective-permute-start.29) | collective-permute-done | bytes 98336 | tf_op jit(solution)/shard_map/ppermute | solution.py:392
  84.2 3.6 %collective-permute-done.33.low = f32[3,4,16,128]{3,2,1,0:T(8,128)S(1)} collective-permute-done((f32[3,4,16,128]{3,2,1,0:T(8,128)S(1)}, f32[3,4,16,128]{3,2,1,0:T(8,128)S(1)}, u32[]{:S(2)}, u32[]{:S(2)}) %collective-permute-start.33) | collective-permute-done | bytes 98336 | tf_op jit(solution)/shard_map/ppermute | solution.py:392
  90.0 2.8 %collective-permute-start.54 = (f32[7,4,16,128]{3,2,1,0:T(8,128)S(1)}, f32[7,4,16,128]{3,2,1,0:T(8,128)S(1)}, u32[]{:S(2)}, u32[]{:S(2)}) collective-permute-start(f32[7,4,16,128]{3,2,1,0:T(8,128)S(1)} %get-tuple-element.101), channel_id=1, source_target_pairs={{0,14},{1,15},{2,0},{3,1},{4,2},{5,3},{6,4},{7,5},{8,6},{9,7},{10,... | collective-permute-start | bytes 688136 | tf_op jit(solution)/shard_map/ppermute | solution.py:392
  92.9 2.9 %collective-permute-done.45.rest_5_ = f32[3,4,16,128]{3,2,1,0:T(8,128)S(1)} collective-permute-done((f32[3,4,16,128]{3,2,1,0:T(8,128)S(1)}, f32[3,4,16,128]{3,2,1,0:T(8,128)S(1)}, u32[]{:S(2)}, u32[]{:S(2)}) %collective-permute-start.45) | collective-permute-done | bytes 98336 | tf_op jit(solution)/shard_map/ppermute | solution.py:392
  97.7 2.2 %collective-permute-done.38.high = f32[3,4,16,128]{3,2,1,0:T(8,128)S(1)} collective-permute-done((f32[3,4,16,128]{3,2,1,0:T(8,128)S(1)}, f32[3,4,16,128]{3,2,1,0:T(8,128)S(1)}, u32[]{:S(2)}, u32[]{:S(2)}) %collective-permute-start.38) | collective-permute-done | bytes 98336 | tf_op jit(solution)/shard_map/ppermute | solution.py:392
  100.0 3.0 %collective-permute-done.37.low = f32[3,4,16,128]{3,2,1,0:T(8,128)S(1)} collective-permute-done((f32[3,4,16,128]{3,2,1,0:T(8,128)S(1)}, f32[3,4,16,128]{3,2,1,0:T(8,128)S(1)}, u32[]{:S(2)}, u32[]{:S(2)}) %collective-permute-start.37) | collective-permute-done | bytes 98336 | tf_op jit(solution)/shard_map/ppermute | solution.py:392
  108.0 2.7 %collective-permute-done.52.highest = f32[3,1,16,128]{3,2,1,0:T(8,128)S(1)} collective-permute-done((f32[3,1,16,128]{3,2,1,0:T(8,128)S(1)}, f32[3,1,16,128]{3,2,1,0:T(8,128)S(1)}, u32[]{:S(2)}, u32[]{:S(2)}) %collective-permute-start.52) | collective-permute-done | bytes 24608 | tf_op jit(solution)/shard_map/ppermute | solution.py:392
  110.7 5.3 %collective-permute-done.47.lowest = f32[3,1,16,128]{3,2,1,0:T(8,128)S(1)} collective-permute-done((f32[3,1,16,128]{3,2,1,0:T(8,128)S(1)}, f32[3,1,16,128]{3,2,1,0:T(8,128)S(1)}, u32[]{:S(2)}, u32[]{:S(2)}) %collective-permute-start.47) | collective-permute-done | bytes 24608 | tf_op jit(solution)/shard_map/ppermute | solution.py:392
  116.0 4.3 %finish.1 = f32[16,3,4,16,128]{4,3,2,1,0:T(8,128)} custom-call(f32[3,1,16,128]{3,2,1,0:T(8,128)S(1)} %collective-permute-done.47.lowest, f32[3,4,16,128]{3,2,1,0:T(8,128)S(1)} %collective-permute-done.48.lower, f32[3,4,16,128]{3,2,1,0:T(8,128)S(1)} %collective-permute-done.49.low, f32[3,4,16,128]{3,2,1,0:T(8,128)S(1)} %shard_map.59.own, ...), custom_call_target="tpu_custom_call" | custom-call | flops 20000000 | bytes 4000000 | tf_op jit(solution)/shard_map/finish/pallas_call | solution.py:431
  (111 shorter events, 32.6 us)
Async XLA Ops:
  0.9 10.3 %collective-permute-start.4 = (f32[3,4,16,128]{3,2,1,0:T(8,128)S(1)}, f32[3,4,16,128]{3,2,1,0:T(8,128)S(1)}, u32[]{:S(2)}, u32[]{:S(2)}) collective-permute-start(f32[3,4,16,128]{3,2,1,0:T(8,128)S(1)} %slice_bitcast_fusion), channel_id=1, source_target_pairs={{0,16},{1,17},{2,18},{3,19},{4,20},{5,21},{6,22},{7,23},{8,24},{9,... | collective-permute-start | bytes 294920 | tf_op jit(solution)/shard_map/ppermute | solution.py:392
  3.7 10.4 %collective-permute-start.1 = (f32[7,4,16,128]{3,2,1,0:T(8,128)S(1)}, f32[7,4,16,128]{3,2,1,0:T(8,128)S(1)}, u32[]{:S(2)}, u32[]{:S(2)}) collective-permute-start(f32[7,4,16,128]{3,2,1,0:T(8,128)S(1)} %pad_maximum_fusion.own.fields), channel_id=1, source_target_pairs={{0,15},{1,0},{2,1},{3,2},{4,3},{5,4},{6,5},{7,6},{8,7},{9,8},{10,9... | collective-permute-start | bytes 688136 | tf_op jit(solution)/shard_map/ppermute | solution.py:392
  8.2 11.4 %collective-permute-start.3 = (f32[9,4,16,128]{3,2,1,0:T(8,128)S(1)}, f32[9,4,16,128]{3,2,1,0:T(8,128)S(1)}, u32[]{:S(2)}, u32[]{:S(2)}) collective-permute-start(f32[9,4,16,128]{3,2,1,0:T(8,128)S(1)} %bitcast.4), channel_id=1, source_target_pairs={{0,15},{1,0},{2,1},{3,2},{4,3},{5,4},{6,5},{7,6},{8,7},{9,8},{10,9... | collective-permute-start | bytes 884744 | tf_op jit(solution)/shard_map/ppermute | solution.py:392
  11.2 8.4 %collective-permute-start.2 = (f32[9,4,16,128]{3,2,1,0:T(8,128)S(1)}, f32[9,4,16,128]{3,2,1,0:T(8,128)S(1)}, u32[]{:S(2)}, u32[]{:S(2)}) collective-permute-start(f32[9,4,16,128]{3,2,1,0:T(8,128)S(1)} %bitcast.5), channel_id=1, source_target_pairs={{0,1},{1,2},{2,3},{3,4},{4,5},{5,6},{6,7},{7,8},{8,9},{9,10},{10,1... | collective-permute-start | bytes 884744 | tf_op jit(solution)/shard_map/ppermute | solution.py:392
  33.4 11.8 %collective-permute-start.11 = (f32[3,8,16,128]{3,2,1,0:T(8,128)S(1)}, f32[3,8,16,128]{3,2,1,0:T(8,128)S(1)}, u32[]{:S(2)}, u32[]{:S(2)}) collective-permute-start(f32[3,8,16,128]{3,2,1,0:T(8,128)S(1)} %get-tuple-element.73.term), channel_id=1, source_target_pairs={{0,240},{1,241},{2,242},{3,243},{4,244},{5,245},{6,246},{7,247},{8... | collective-permute-start | bytes 589832 | tf_op jit(solution)/shard_map/ppermute | solution.py:392
  35.6 10.7 %collective-permute-start.15 = (f32[3,8,16,128]{3,2,1,0:T(8,128)S(1)}, f32[3,8,16,128]{3,2,1,0:T(8,128)S(1)}, u32[]{:S(2)}, u32[]{:S(2)}) collective-permute-start(f32[3,8,16,128]{3,2,1,0:T(8,128)S(1)} %get-tuple-element.73.term), channel_id=1, source_target_pairs={{0,1},{1,0},{2,3},{3,2},{4,5},{5,4},{6,7},{7,6},{8,9},{9,8},{10,11... | collective-permute-start | bytes 589832 | tf_op jit(solution)/shard_map/ppermute | solution.py:392
  35.6 9.6 %collective-permute-start.12 = (f32[3,4,16,128]{3,2,1,0:T(8,128)S(1)}, f32[3,4,16,128]{3,2,1,0:T(8,128)S(1)}, u32[]{:S(2)}, u32[]{:S(2)}) collective-permute-start(f32[3,4,16,128]{3,2,1,0:T(8,128)S(1)} %get-tuple-element.74), channel_id=1, source_target_pairs={{0,1},{1,0},{2,3},{3,2},{4,5},{5,4},{6,7},{7,6},{8,9},{9,8},{10,11... | collective-permute-start | bytes 294920 | tf_op jit(solution)/shard_map/ppermute | solution.py:392
  36.4 9.9 %collective-permute-start.16 = (f32[3,4,16,128]{3,2,1,0:T(8,128)S(1)}, f32[3,4,16,128]{3,2,1,0:T(8,128)S(1)}, u32[]{:S(2)}, u32[]{:S(2)}) collective-permute-start(f32[3,4,16,128]{3,2,1,0:T(8,128)S(1)} %get-tuple-element.74), channel_id=1, source_target_pairs={{0,1},{1,0},{2,3},{3,2},{4,5},{5,4},{6,7},{7,6},{8,9},{9,8},{10,11... | collective-permute-start | bytes 294920 | tf_op jit(solution)/shard_map/ppermute | solution.py:392
  46.3 12.5 %collective-permute-start.19 = (f32[3,8,16,128]{3,2,1,0:T(8,128)S(1)}, f32[3,8,16,128]{3,2,1,0:T(8,128)S(1)}, u32[]{:S(2)}, u32[]{:S(2)}) collective-permute-start(f32[3,8,16,128]{3,2,1,0:T(8,128)S(1)} %get-tuple-element.73.term), channel_id=1, source_target_pairs={{0,1},{1,0},{2,3},{3,2},{4,5},{5,4},{6,7},{7,6},{8,9},{9,8},{10,11... | collective-permute-start | bytes 589832 | tf_op jit(solution)/shard_map/ppermute | solution.py:392
  46.4 11.2 %collective-permute-start.20 = (f32[3,4,16,128]{3,2,1,0:T(8,128)S(1)}, f32[3,4,16,128]{3,2,1,0:T(8,128)S(1)}, u32[]{:S(2)}, u32[]{:S(2)}) collective-permute-start(f32[3,4,16,128]{3,2,1,0:T(8,128)S(1)} %get-tuple-element.74), channel_id=1, source_target_pairs={{0,1},{1,0},{2,3},{3,2},{4,5},{5,4},{6,7},{7,6},{8,9},{9,8},{10,11... | collective-permute-start | bytes 294920 | tf_op jit(solution)/shard_map/ppermute | solution.py:392
  46.4 17.3 %collective-permute-start.23 = (f32[3,8,16,128]{3,2,1,0:T(8,128)S(1)}, f32[3,8,16,128]{3,2,1,0:T(8,128)S(1)}, u32[]{:S(2)}, u32[]{:S(2)}) collective-permute-start(f32[3,8,16,128]{3,2,1,0:T(8,128)S(1)} %get-tuple-element.77), channel_id=1, source_target_pairs={{0,1},{1,0},{2,3},{3,2},{4,5},{5,4},{6,7},{7,6},{8,9},{9,8},{10,11... | collective-permute-start | bytes 589832 | tf_op jit(solution)/shard_map/ppermute | solution.py:392
  57.6 13.1 %collective-permute-start.27 = (f32[3,8,16,128]{3,2,1,0:T(8,128)S(1)}, f32[3,8,16,128]{3,2,1,0:T(8,128)S(1)}, u32[]{:S(2)}, u32[]{:S(2)}) collective-permute-start(f32[3,8,16,128]{3,2,1,0:T(8,128)S(1)} %get-tuple-element.77), channel_id=1, source_target_pairs={{0,1},{1,0},{2,3},{3,2},{4,5},{5,4},{6,7},{7,6},{8,9},{9,8},{10,11... | collective-permute-start | bytes 589832 | tf_op jit(solution)/shard_map/ppermute | solution.py:392
  63.7 11.6 %collective-permute-start.31 = (f32[3,8,16,128]{3,2,1,0:T(8,128)S(1)}, f32[3,8,16,128]{3,2,1,0:T(8,128)S(1)}, u32[]{:S(2)}, u32[]{:S(2)}) collective-permute-start(f32[3,8,16,128]{3,2,1,0:T(8,128)S(1)} %get-tuple-element.83), channel_id=1, source_target_pairs={{0,1},{1,0},{2,3},{3,2},{4,5},{5,4},{6,7},{7,6},{8,9},{9,8},{10,11... | collective-permute-start | bytes 589832 | tf_op jit(solution)/shard_map/ppermute | solution.py:392
  70.7 11.9 %collective-permute-start.35 = (f32[3,8,16,128]{3,2,1,0:T(8,128)S(1)}, f32[3,8,16,128]{3,2,1,0:T(8,128)S(1)}, u32[]{:S(2)}, u32[]{:S(2)}) collective-permute-start(f32[3,8,16,128]{3,2,1,0:T(8,128)S(1)} %get-tuple-element.87), channel_id=1, source_target_pairs={{0,1},{1,0},{2,3},{3,2},{4,5},{5,4},{6,7},{7,6},{8,9},{9,8},{10,11... | collective-permute-start | bytes 589832 | tf_op jit(solution)/shard_map/ppermute | solution.py:392
  71.8 12.3 %collective-permute-start.39 = (f32[3,8,16,128]{3,2,1,0:T(8,128)S(1)}, f32[3,8,16,128]{3,2,1,0:T(8,128)S(1)}, u32[]{:S(2)}, u32[]{:S(2)}) collective-permute-start(f32[3,8,16,128]{3,2,1,0:T(8,128)S(1)} %get-tuple-element.91), channel_id=1, source_target_pairs={{0,1},{1,0},{2,3},{3,2},{4,5},{5,4},{6,7},{7,6},{8,9},{9,8},{10,11... | collective-permute-start | bytes 589832 | tf_op jit(solution)/shard_map/ppermute | solution.py:392
  75.4 8.7 %collective-permute-start.40 = (f32[3,4,16,128]{3,2,1,0:T(8,128)S(1)}, f32[3,4,16,128]{3,2,1,0:T(8,128)S(1)}, u32[]{:S(2)}, u32[]{:S(2)}) collective-permute-start(f32[3,4,16,128]{3,2,1,0:T(8,128)S(1)} %get-tuple-element.93), channel_id=1, source_target_pairs={{0,1},{1,0},{2,3},{3,2},{4,5},{5,4},{6,7},{7,6},{8,9},{9,8},{10,11... | collective-permute-start | bytes 294920 | tf_op jit(solution)/shard_map/ppermute | solution.py:392
  84.1 8.7 %collective-permute-start.44 = (f32[3,4,16,128]{3,2,1,0:T(8,128)S(1)}, f32[3,4,16,128]{3,2,1,0:T(8,128)S(1)}, u32[]{:S(2)}, u32[]{:S(2)}) collective-permute-start(f32[3,4,16,128]{3,2,1,0:T(8,128)S(1)} %get-tuple-element.97), channel_id=1, source_target_pairs={{0,1},{1,0},{2,3},{3,2},{4,5},{5,4},{6,7},{7,6},{8,9},{9,8},{10,11... | collective-permute-start | bytes 294920 | tf_op jit(solution)/shard_map/ppermute | solution.py:392
  87.8 16.4 %collective-permute-start.56 = (f32[9,4,16,128]{3,2,1,0:T(8,128)S(1)}, f32[9,4,16,128]{3,2,1,0:T(8,128)S(1)}, u32[]{:S(2)}, u32[]{:S(2)}) collective-permute-start(f32[9,4,16,128]{3,2,1,0:T(8,128)S(1)} %get-tuple-element.102.late), channel_id=1, source_target_pairs={{0,15},{1,0},{2,1},{3,2},{4,3},{5,4},{6,5},{7,6},{8,7},{9,8},{10,9... | collective-permute-start | bytes 884744 | tf_op jit(solution)/shard_map/ppermute | solution.py:392
  89.6 14.1 %collective-permute-start.53 = (f32[7,4,16,128]{3,2,1,0:T(8,128)S(1)}, f32[7,4,16,128]{3,2,1,0:T(8,128)S(1)}, u32[]{:S(2)}, u32[]{:S(2)}) collective-permute-start(f32[7,4,16,128]{3,2,1,0:T(8,128)S(1)} %get-tuple-element.100), channel_id=1, source_target_pairs={{0,2},{1,3},{2,4},{3,5},{4,6},{5,7},{6,8},{7,9},{8,10},{9,11},{10,... | collective-permute-start | bytes 688136 | tf_op jit(solution)/shard_map/ppermute | solution.py:392
  90.0 13.7 %collective-permute-start.54 = (f32[7,4,16,128]{3,2,1,0:T(8,128)S(1)}, f32[7,4,16,128]{3,2,1,0:T(8,128)S(1)}, u32[]{:S(2)}, u32[]{:S(2)}) collective-permute-start(f32[7,4,16,128]{3,2,1,0:T(8,128)S(1)} %get-tuple-element.101), channel_id=1, source_target_pairs={{0,14},{1,15},{2,0},{3,1},{4,2},{5,3},{6,4},{7,5},{8,6},{9,7},{10,... | collective-permute-start | bytes 688136 | tf_op jit(solution)/shard_map/ppermute | solution.py:392
  103.3 12.8 %collective-permute-start.51 = (f32[3,4,16,128]{3,2,1,0:T(8,128)S(1)}, f32[3,4,16,128]{3,2,1,0:T(8,128)S(1)}, u32[]{:S(2)}, u32[]{:S(2)}) collective-permute-start(f32[3,4,16,128]{3,2,1,0:T(8,128)S(1)} %shard_map.59.own), channel_id=1, source_target_pairs={{0,14},{1,15},{2,0},{3,1},{4,2},{5,3},{6,4},{7,5},{8,6},{9,7},{10,... | collective-permute-start | bytes 294920 | tf_op jit(solution)/shard_map/ppermute | solution.py:392
  103.7 12.3 %collective-permute-start.50 = (f32[3,4,16,128]{3,2,1,0:T(8,128)S(1)}, f32[3,4,16,128]{3,2,1,0:T(8,128)S(1)}, u32[]{:S(2)}, u32[]{:S(2)}) collective-permute-start(f32[3,4,16,128]{3,2,1,0:T(8,128)S(1)} %shard_map.59.own), channel_id=1, source_target_pairs={{0,15},{1,0},{2,1},{3,2},{4,3},{5,4},{6,5},{7,6},{8,7},{9,8},{10,9... | collective-permute-start | bytes 294920 | tf_op jit(solution)/shard_map/ppermute | solution.py:392
  103.7 12.3 %collective-permute-start.49 = (f32[3,4,16,128]{3,2,1,0:T(8,128)S(1)}, f32[3,4,16,128]{3,2,1,0:T(8,128)S(1)}, u32[]{:S(2)}, u32[]{:S(2)}) collective-permute-start(f32[3,4,16,128]{3,2,1,0:T(8,128)S(1)} %shard_map.59.own), channel_id=1, source_target_pairs={{0,1},{1,2},{2,3},{3,4},{4,5},{5,6},{6,7},{7,8},{8,9},{9,10},{10,1... | collective-permute-start | bytes 294920 | tf_op jit(solution)/shard_map/ppermute | solution.py:392
  104.3 11.8 %collective-permute-start.48 = (f32[3,4,16,128]{3,2,1,0:T(8,128)S(1)}, f32[3,4,16,128]{3,2,1,0:T(8,128)S(1)}, u32[]{:S(2)}, u32[]{:S(2)}) collective-permute-start(f32[3,4,16,128]{3,2,1,0:T(8,128)S(1)} %shard_map.59.own), channel_id=1, source_target_pairs={{0,2},{1,3},{2,4},{3,5},{4,6},{5,7},{6,8},{7,9},{8,10},{9,11},{10,... | collective-permute-start | bytes 294920 | tf_op jit(solution)/shard_map/ppermute | solution.py:392
  (33 other events, 175.0 us)
